TPU v7x, 128 devices: a whole 4x4x4 slice. The times are simulated.
128 devices in a mesh: row: 8 (over x, core), col: 16 (over y, z).
Axes of the slice: x: 4, y: 4, z: 4, core: 2. Of those that a mesh axis runs over, the one named last changes fastest.
Arguments:
- density_factor: bfloat16 [524288, 256], P(('row', 'col'))
- onsite: float32 [524288], P(('row', 'col')), may hold values from -4 to 4
- neighbour_ids: int32 [1024, 8], P(('row', 'col')), may hold values from 0 to 1023, as said below
- neighbour_count: int32 [1024], P(('row', 'col')), may hold values from 1 to 8, as said below
- coupling_type: int32 [1024, 8], P(('row', 'col')), may hold values from 0 to 3
- coupling_blocks: bfloat16 [4, 512, 512], replicated, may hold values from -0.25 to 0.25
- bath_pattern: int32 [1024], P(('row', 'col')), may hold values from 0 to 3
- bath_blocks: bfloat16 [4, 512, 512], replicated, may hold values from -0.25 to 0.25
Outputs:
- new_factor: bfloat16 [524288, 256], P(('row', 'col'))
Inputs may be any that keep to these rules, and one draw needn't show every extreme that they name: `neighbour_ids`: every neighbour of block b lies among the 128 blocks that share b's index of row, at most half of 128 blocks from b when that group is taken as a loop, and is never b itself; some block has a neighbour exactly half of 128 blocks away. Only the first neighbour_count[b] slots of block b's lists are used; some block uses all 8.
All inputs are finite; a program needn't handle non-finite values.
Results may differ from a plain program's by a relative error of at most 0.0056.
Values may be sent and summed in bfloat16 or wider, within the bound.
A program may use at most 192 MiB of HBM per device.

v0:
```python
import jax
import jax.numpy as jnp
from jax import lax
from jax.sharding import PartitionSpec as P

SWEEPS = 2


time_step = 0.25


def orthonormal_steps(gram, rank_cols):
    basis = jnp.eye(2 * rank_cols, rank_cols, dtype=jnp.float32)
    for sweep in range(SWEEPS):
        image = jnp.dot(gram, basis, precision=lax.Precision.HIGHEST)
        inner = jnp.dot(image.T, image, precision=lax.Precision.HIGHEST)
        factor = jnp.linalg.cholesky(inner)
        basis = lax.linalg.triangular_solve(
            factor, image, left_side=False, lower=True, transpose_a=True
        )
    return basis


def shards(
    density_factor,
    onsite,
    neighbour_ids,
    neighbour_count,
    coupling_type,
    coupling_blocks,
    bath_pattern,
    bath_blocks,
):
    blocks, slots = neighbour_ids.shape
    kinds = coupling_blocks.shape[0]
    block_rows = coupling_blocks.shape[1]
    rank_cols = density_factor.shape[1]
    col_count = lax.axis_size("col")
    group_blocks = col_count * blocks
    row_place = lax.axis_index("row")
    in_group = neighbour_ids - row_place * group_blocks
    slot_live = jnp.arange(slots, dtype=jnp.int32)[None, :] < neighbour_count[:, None]
    kind_match = (
        coupling_type[:, :, None] == jnp.arange(kinds, dtype=jnp.int32)[None, None, :]
    ) & slot_live[:, :, None]
    kind_float = kind_match.astype(jnp.float32)
    gathered = lax.all_gather(density_factor, "col", axis=0, tiled=True)
    hits = (
        in_group[:, :, None] == jnp.arange(group_blocks, dtype=jnp.int32)[None, None, :]
    ).astype(jnp.float32)
    mixing = jnp.einsum("bkt,bkn->btn", kind_float, hits).astype(jnp.bfloat16)
    flat_blocks = gathered.reshape(group_blocks, block_rows * rank_cols)
    summed = jnp.einsum("btn,nm->btm", mixing, flat_blocks, preferred_element_type=jnp.float32)
    summed = summed.reshape(blocks, kinds, block_rows, rank_cols).astype(jnp.bfloat16)
    coupled = jnp.einsum(
        "tij,btjr->bir", coupling_blocks, summed, preferred_element_type=jnp.float32
    )
    own_rows = density_factor.reshape(blocks, block_rows, rank_cols)
    bath_pick = bath_blocks[bath_pattern]
    bathed = jnp.einsum(
        "bij,bjr->bir", bath_pick, own_rows, preferred_element_type=jnp.float32
    ).astype(jnp.bfloat16)
    factor_wide = own_rows.astype(jnp.float32)
    energy = onsite.reshape(blocks, block_rows, 1)
    moved = (factor_wide - time_step * (energy * factor_wide + coupled)).astype(jnp.bfloat16)
    stacked = jnp.concatenate([moved, bathed], axis=2).reshape(blocks * block_rows, 2 * rank_cols)
    local_gram = lax.dot_general(
        stacked, stacked, (((0,), (0,)), ((), ())), preferred_element_type=jnp.float32
    )
    gram_sum = lax.psum(local_gram, ("row", "col"))
    rotation = orthonormal_steps(gram_sum, rank_cols).astype(jnp.bfloat16)
    return jnp.dot(stacked, rotation, preferred_element_type=jnp.float32).astype(jnp.bfloat16)


def solution(mesh):
    placed = (
        P(("row", "col"), None),
        P(("row", "col")),
        P(("row", "col"), None),
        P(("row", "col")),
        P(("row", "col"), None),
        P(),
        P(("row", "col")),
        P(),
    )
    return jax.shard_map(
        shards, mesh=mesh, in_specs=placed, out_specs=P(("row", "col"), None), check_vma=False
    )
```

profile of v0, /device:TPU:1, one launch (start us, length us, event | category | flops | bytes accessed | tf_op | source)
XLA Modules:
  0.0 618.0 jit_solution(14788270948122039171)
XLA Ops:
  6.5 0.7 all-gather.2.cloned.1.call-update
  7.3 0.7 mul.19
  8.0 3.9 copy.12
  12.0 2.9 gather_fusion
  14.9 4.2 convolution_convert_fusion.1
  19.1 190.8 %all-gather.2.cloned.1.call-done = bf16[65536,256]{1,0:T(8,128)(2,1)} async-done(((bf16[4096,256]{1,0:T(8,128)(2,1)}), bf16[65536,256]{1,0:T(8,128)(2,1)}) %all-gather.2.cloned.1.call-update) | async-done | bytes 33554448 | tf_op jit(solution)/shard_map/all_gather | solution.py:47
  210.0 33.2 %reshape.54 = bf16[128,131072]{1,0:T(8,128)(2,1)} reshape(bf16[65536,256]{1,0:T(8,128)(2,1)} %all-gather.2.cloned.1.call-done) | data formatting | bytes 67108864 | tf_op jit(solution)/shard_map/reshape | solution.py:52
  243.2 23.1 %copy.24 = bf16[16,8,512,256]{3,2,1,0:T(8,128)(2,1)} copy(bf16[16,8,512,256]{3,1,2,0:T(8,128)(2,1)} %bitcast.98) | data formatting | bytes 67108864
  266.2 36.0 %fusion = bf16[8,4,512,256]{3,1,2,0:T(4,128)(2,1)} fusion(bf16[512,256,128,1]{1,0,2,3:T(8,128)(2,1)} %bitcast.99, s32[8,8]{1,0:T(8,128)S(1)} %broadcast_subtract_fusion, s32[8,8]{1,0:T(8,128)S(1)} %copy-done.5, pred[8,8]{1,0:T(8,128)(4,1)S(1)} %iota_compare_fusion.9), kind=kOutput, calls=%fused_computation.5 | convolution fusion | flops 1073820160 | bytes 41943616 | tf_op jit(solution)/shard_map/btn,nm->btm/dot_general | solution.py:53
  302.3 13.8 %copy.20 = bf16[8,4,512,256]{2,3,1,0:T(8,128)(2,1)} copy(bf16[8,4,512,256]{3,1,2,0:T(4,128)(2,1)} %fusion) | data formatting | bytes 16777216 | tf_op jit(solution)/shard_map/btn,nm->btm/dot_general | solution.py:53
  316.1 9.6 %fusion.6 = bf16[8,512,256]{1,2,0:T(8,128)(2,1)S(1)} fusion(bf16[8,512,256]{1,2,0:T(8,128)(2,1)} %copy.12, bf16[8,4,512,256]{2,3,1,0:T(8,128)(2,1)} %copy.20, bf16[4,512,512]{2,1,0:T(8,128)(2,1)} %param.16, f32[8,512]{1,0:T(8,128)S(1)} %mul.19), kind=kOutput, calls=%fused_computation.14 | convolution fusion | flops 4301258752 | bytes 14696448 | tf_op jit(solution)/shard_map/tij,btjr->bir/dot_general | solution.py:55
  325.7 1.3 copy-done.3
  327.0 3.3 convolution_bitcast_fusion
  330.3 3.8 pad_maximum_fusion
  334.2 6.5 %copy.14 = bf16[8,512,512]{2,1,0:T(8,128)(2,1)} copy(bf16[8,512,512]{1,2,0:T(8,128)(2,1)} %pad_maximum_fusion) | data formatting | bytes 8388608 | tf_op jit(solution)/shard_map/concatenate | solution.py:66
  340.6 136.9 %all-reduce.3.cloned.1.call-done = f32[512,512]{1,0:T(8,128)} async-done(((f32[512,512]{1,0:T(8,128)}), f32[512,512]{1,0:T(8,128)}) %all-reduce.3.cloned.1.call-update) | async-done | bytes 1048592 | tf_op jit(solution)/shard_map/psum | solution.py:70
  477.5 1.9 fusion.15
  479.4 1.0 fusion.49
  480.7 11.7 %cholesky.130 = f32[128,128]{1,0:T(8,128)S(1)} custom-call(f32[128,128]{1,0:T(8,128)S(1)} %cholesky.194), custom_call_target="Cholesky" | custom-call | tf_op jit(solution)/shard_map/jit(cholesky)/cholesky | solution.py:17
  492.4 9.8 %custom-call.13 = f32[1,128,128]{1,2,0:T(8,128)S(1)} custom-call(f32[1,128,128]{2,1,0:T(8,128)S(1)} %get-tuple-element.50), custom_call_target="InvertDiagBlocksLowerTriangular" | custom-call | tf_op jit(solution)/shard_map/jit(cholesky)/cholesky | solution.py:17
  502.7 11.7 %cholesky.147 = f32[128,128]{1,0:T(8,128)S(1)} custom-call(f32[128,128]{1,0:T(8,128)S(1)} %convolution_subtract_fusion.3), custom_call_target="Cholesky" | custom-call | tf_op jit(solution)/shard_map/jit(cholesky)/cholesky | solution.py:17
  514.5 0.7 compare_reduce_fusion.2
  516.6 4.0 while.4
  516.6 0.6 fusion.71
  517.2 1.4 bitcast_dynamic-update-slice_fusion.4
  518.6 0.6 fusion.71
  519.2 1.4 bitcast_dynamic-update-slice_fusion.4
  520.6 20.1 %custom-call.14 = f32[2,128,128]{1,2,0:T(8,128)S(1)} custom-call(f32[2,128,128]{2,1,0:T(8,128)S(1)} %get-tuple-element.21), custom_call_target="InvertDiagBlocksLowerTriangular" | custom-call | tf_op jit(solution)/shard_map/triangular_solve/custom-call.0 | solution.py:18
  540.6 0.4 fusion.18
  541.1 0.6 convolution_subtract_fusion.1
  541.7 0.4 fusion.26
  542.1 1.0 fusion.11
  543.1 1.0 fusion.50
  544.3 11.7 %cholesky.164 = f32[128,128]{1,0:T(8,128)S(1)} custom-call(f32[128,128]{1,0:T(8,128)S(1)} %cholesky.197), custom_call_target="Cholesky" | custom-call | tf_op jit(solution)/shard_map/jit(cholesky)/cholesky | solution.py:17
  556.1 0.6 compare_reduce_fusion.1
  556.7 9.8 %custom-call.15 = f32[1,128,128]{1,2,0:T(8,128)S(1)} custom-call(f32[1,128,128]{2,1,0:T(8,128)S(1)} %get-tuple-element.46), custom_call_target="InvertDiagBlocksLowerTriangular" | custom-call | tf_op jit(solution)/shard_map/jit(cholesky)/cholesky | solution.py:17
  567.1 11.9 %cholesky.181 = f32[128,128]{1,0:T(8,128)S(1)} custom-call(f32[128,128]{1,0:T(8,128)S(1)} %convolution_subtract_fusion.2), custom_call_target="Cholesky" | custom-call | tf_op jit(solution)/shard_map/jit(cholesky)/cholesky | solution.py:17
  579.0 0.6 compare_reduce_fusion
  580.9 3.9 while.5
  581.0 0.6 fusion.72
  581.5 1.4 bitcast_dynamic-update-slice_fusion.5
  582.9 0.6 fusion.72
  583.5 1.4 bitcast_dynamic-update-slice_fusion.5
  584.9 19.7 %custom-call.16 = f32[2,128,128]{1,2,0:T(8,128)S(1)} custom-call(f32[2,128,128]{2,1,0:T(8,128)S(1)} %get-tuple-element.22), custom_call_target="InvertDiagBlocksLowerTriangular" | custom-call | tf_op jit(solution)/shard_map/triangular_solve/custom-call.0 | solution.py:18
  604.6 0.4 fusion.16
  605.0 0.6 convolution_subtract_fusion
  605.6 0.4 fusion.22
  606.0 4.9 convolution_convert_fusion
  (48 shorter events, 1.8 us)
Async XLA Ops:
  6.5 5.4 copy-start
  6.5 5.4 copy-start.6
  6.5 203.4 %all-gather.2.cloned.1.call-start = ((), (), s32[]{:S(2)}) async-start(), calls=%async_computation | async-start | bytes 35651584 | tf_op jit(solution)/shard_map/all_gather | solution.py:47
  7.3 470.3 %all-reduce.3.cloned.1.call-start = ((), (), s32[]{:S(2)}) async-start(), calls=%async_computation.1 | async-start | bytes 2097152 | tf_op jit(solution)/shard_map/psum | solution.py:70
  12.0 2.9 copy-start.7
  12.0 3.0 copy-start.4
  243.2 23.1 %copy-start.5 = (s32[8,8]{1,0:T(8,128)S(1)}, s32[8,8]{1,0:T(8,128)}, u32[]{:S(2)}) copy-start(s32[8,8]{1,0:T(8,128)} %param.15) | copy-start | bytes 772
  325.6 1.3 copy-start.3
  477.5 64.6 %copy-start.2 = (f32[512,512]{1,0:T(8,128)S(1)}, f32[512,512]{1,0:T(8,128)}, u32[]{:S(2)}) copy-start(f32[512,512]{1,0:T(8,128)} %all-reduce.3.cloned.1.call-done) | copy-start | bytes 3145732
  606.0 5.0 copy-start.1
Sparse Core Ops, SparseCore 0:
  9.5 200.4 all-gather.1
  330.4 147.0 all-reduce.2
where the time goes:
time: 623 us; the launch traced here: 618 us
  waiting for transfers between devices  328 us (53%)
  other arithmetic  113 us (18%)
  local copies, waits for them, and re-layouts  93.6 us (15%)
  matrix products  66.8 us (11%)
  between operations  16.5 us (3%)
    all_gather x1, waiting for transfers between devices, shards(): gathered = lax.all_gather(density_factor, 'col', axis=0, tiled=True)  191 us
    psum x1, waiting for transfers between devices, shards(): gram_sum = lax.psum(local_gram, ('row', 'col'))  137 us
    another operation x13, other arithmetic, orthonormal_steps(): factor = jnp.linalg.cholesky(inner)  68.8 us
    another operation x5, other arithmetic, orthonormal_steps(): lax.linalg.triangular_solve(factor, image, left_side=False, lower=True, t...  39.8 us
    dot_general x1, matrix products, shards(): jnp.einsum('btn,nm->btm', mixing, flat_blocks, preferred_element_type=jnp...  36 us
    reshape x1, local copies, waits for them, and re-layouts, shards(): flat_blocks = gathered.reshape(group_blocks, block_rows * rank_cols)  33.2 us
    unnamed x17, local copies, waits for them, and re-layouts  24.4 us
    dot_general x1, local copies, waits for them, and re-layouts, shards(): jnp.einsum('btn,nm->btm', mixing, flat_blocks, preferred_element_type=jnp...  13.8 us
  transfers between devices with their start and end apart: 2, of which 2 were waited for; matrix products, arithmetic and copies ran while one was open for 4% of the time, Pallas kernels for 0%

commit v1 on v0

v1 whole, which is shorter than its diff:
```python
import functools

import jax
import jax.numpy as jnp
from jax import lax
from jax.experimental import pallas as pl
from jax.experimental.pallas import tpu as pltpu
from jax.sharding import PartitionSpec as P

SWEEPS = 2


time_step = 0.25


def orthonormal_steps(gram, rank_cols):
    basis = jnp.eye(2 * rank_cols, rank_cols, dtype=jnp.float32)
    for sweep in range(SWEEPS):
        image = jnp.dot(gram, basis, precision=lax.Precision.HIGHEST)
        inner = jnp.dot(image.T, image, precision=lax.Precision.HIGHEST)
        factor = jnp.linalg.cholesky(inner)
        basis = lax.linalg.triangular_solve(
            factor, image, left_side=False, lower=True, transpose_a=True
        )
    return basis


def step_kernel(slots, ids_ref, cnt_ref, kind_ref, bath_ref,
                nbr_ref, own_ref, ons_ref, cpl_ref, bth_ref, out_ref, acc):
    b = pl.program_id(0)
    k = pl.program_id(1)
    rank_cols = own_ref.shape[2]

    @pl.when(k == 0)
    def _():
        acc[...] = jnp.zeros_like(acc)

    @pl.when(k < cnt_ref[b])
    def _():
        t = kind_ref[b * slots + k]
        acc[t] += nbr_ref[0].astype(jnp.float32)

    @pl.when(k == slots - 1)
    def _():
        coupled = jnp.dot(cpl_ref[0], acc[0].astype(jnp.bfloat16), preferred_element_type=jnp.float32)
        for t in range(1, cpl_ref.shape[0]):
            coupled += jnp.dot(cpl_ref[t], acc[t].astype(jnp.bfloat16), preferred_element_type=jnp.float32)
        own = own_ref[0]
        wide = own.astype(jnp.float32)
        moved = wide - time_step * (ons_ref[0] * wide + coupled)
        out_ref[0, :, :rank_cols] = moved.astype(out_ref.dtype)
        bathed = jnp.dot(bth_ref[0], own, preferred_element_type=jnp.float32)
        out_ref[0, :, rank_cols:] = bathed.astype(out_ref.dtype)


def stacked_blocks(group_rows, own_rows, energy, ids, counts, kinds, bath_pattern, coupling_blocks, bath_blocks):
    blocks, block_rows, rank_cols = own_rows.shape
    slots = ids.shape[0] // blocks
    kinds_n = coupling_blocks.shape[0]

    def nbr_map(b, k, ids_ref, cnt_ref, kind_ref, bath_ref):
        live = jnp.minimum(k, cnt_ref[b] - 1)
        return (ids_ref[b * slots + live], 0, 0)

    grid_spec = pltpu.PrefetchScalarGridSpec(
        num_scalar_prefetch=4,
        grid=(blocks, slots),
        in_specs=[
            pl.BlockSpec((1, block_rows, rank_cols), nbr_map),
            pl.BlockSpec((1, block_rows, rank_cols), lambda b, k, *_: (b, 0, 0)),
            pl.BlockSpec((1, block_rows, 1), lambda b, k, *_: (b, 0, 0)),
            pl.BlockSpec((kinds_n, block_rows, block_rows), lambda b, k, *_: (0, 0, 0)),
            pl.BlockSpec((1, block_rows, block_rows), lambda b, k, i, c, t, bp: (bp[b], 0, 0)),
        ],
        out_specs=pl.BlockSpec((1, block_rows, 2 * rank_cols), lambda b, k, *_: (b, 0, 0)),
        scratch_shapes=[pltpu.VMEM((kinds_n, block_rows, rank_cols), jnp.float32)],
    )
    return pl.pallas_call(
        functools.partial(step_kernel, slots),
        grid_spec=grid_spec,
        out_shape=jax.ShapeDtypeStruct((blocks, block_rows, 2 * rank_cols), jnp.bfloat16),
    )(ids, counts, kinds, bath_pattern, group_rows, own_rows, energy, coupling_blocks, bath_blocks)


def halving_sum(local, axes, count):
    me = lax.axis_index(axes)
    buf = local.reshape(-1)
    stages = []
    order = [s for s in range(count.bit_length() - 1)]
    for s in order:
        bit = (me >> s) & 1
        half = buf.shape[0] // 2
        low, high = buf[:half], buf[half:]
        send = jnp.where(bit == 1, low, high)
        keep = jnp.where(bit == 1, high, low)
        pairs = [(i, i ^ (1 << s)) for i in range(count)]
        buf = keep + lax.ppermute(send, axes, pairs)
        stages.append((s, bit))
    for s, bit in reversed(stages):
        pairs = [(i, i ^ (1 << s)) for i in range(count)]
        other = lax.ppermute(buf, axes, pairs)
        buf = jnp.where(bit == 1, jnp.concatenate([other, buf]), jnp.concatenate([buf, other]))
    return buf.reshape(local.shape)


def shards(
    density_factor,
    onsite,
    neighbour_ids,
    neighbour_count,
    coupling_type,
    coupling_blocks,
    bath_pattern,
    bath_blocks,
):
    blocks, slots = neighbour_ids.shape
    block_rows = coupling_blocks.shape[1]
    rank_cols = density_factor.shape[1]
    col_count = lax.axis_size("col")
    group_blocks = col_count * blocks
    row_place = lax.axis_index("row")
    in_group = jnp.clip(neighbour_ids - row_place * group_blocks, 0, group_blocks - 1)
    counts = jnp.clip(neighbour_count, 1, slots)
    kinds = jnp.clip(coupling_type, 0, coupling_blocks.shape[0] - 1)
    bath_kind = jnp.clip(bath_pattern, 0, bath_blocks.shape[0] - 1)
    gathered = lax.all_gather(density_factor, "col", axis=0, tiled=True)
    group_rows = gathered.reshape(group_blocks, block_rows, rank_cols)
    own_rows = density_factor.reshape(blocks, block_rows, rank_cols)
    energy = onsite.reshape(blocks, block_rows, 1)
    stacked = stacked_blocks(
        group_rows, own_rows, energy, in_group.reshape(-1), counts, kinds.reshape(-1), bath_kind,
        coupling_blocks, bath_blocks,
    ).reshape(blocks * block_rows, 2 * rank_cols)
    local_gram = lax.dot_general(
        stacked, stacked, (((0,), (0,)), ((), ())), preferred_element_type=jnp.float32
    )
    devices = lax.axis_size("row") * col_count
    gram_sum = halving_sum(local_gram, ("row", "col"), devices)
    rotation = orthonormal_steps(gram_sum, rank_cols).astype(jnp.bfloat16)
    return jnp.dot(stacked, rotation, preferred_element_type=jnp.float32).astype(jnp.bfloat16)


def solution(mesh):
    placed = (
        P(("row", "col"), None),
        P(("row", "col")),
        P(("row", "col"), None),
        P(("row", "col")),
        P(("row", "col"), None),
        P(),
        P(("row", "col")),
        P(),
    )
    return jax.shard_map(
        shards, mesh=mesh, in_specs=placed, out_specs=P(("row", "col"), None), check_vma=False
    )
```

time: 623 us -> 485 us (0.78)
  the two profiles are of different devices: /device:TPU:1 before, /device:TPU:10 now
where the time goes in v1:
time: 485 us; the launch traced here: 478 us
  waiting for transfers between devices  279 us (58%)
  other arithmetic  112 us (23%)
  Pallas kernels  36.8 us (8%)
  matrix products  18.1 us (4%)
  between operations  16.6 us (3%)
  local copies, waits for them, and re-layouts  13.8 us (3%)
    all_gather x1, waiting for transfers between devices, shards(): gathered = lax.all_gather(density_factor, 'col', axis=0, tiled=True)  194 us
    another operation x14, other arithmetic, orthonormal_steps(): factor = jnp.linalg.cholesky(inner)  69.6 us
    ppermute x7, waiting for transfers between devices, halving_sum(): buf = keep + lax.ppermute(send, axes, pairs)  45.4 us
    another operation x5, other arithmetic, orthonormal_steps(): lax.linalg.triangular_solve(factor, image, left_side=False, lower=True, t...  39.4 us
    ppermute x7, waiting for transfers between devices, halving_sum(): other = lax.ppermute(buf, axes, pairs)  38.9 us
    pallas_call x1, Pallas kernels, stacked_blocks(): pl.pallas_call(functools.partial(step_kernel, slots), grid_spec=grid_spec...  36.8 us
  transfers between devices with their start and end apart: 15, of which 15 were waited for; matrix products, arithmetic and copies ran while one was open for 2% of the time, Pallas kernels for 0%

profile of v1, /device:TPU:10, one launch (start us, length us, event | category | flops | bytes accessed | tf_op | source)
XLA Modules:
  0.0 478.1 jit_solution(12249396276539511136)
XLA Ops:
  6.5 0.7 all-gather.2.cloned.1.call-update
  7.3 0.7 subtract_clamp_fusion
  8.0 0.7 reshape.59.ids_ref
  8.6 0.7 broadcast_clamp_fusion
  9.3 0.6 reshape.60.kind_ref
  10.0 4.0 reshape.94.ons_ref
  14.0 0.6 broadcast_clamp_fusion.1
  14.5 194.5 %all-gather.2.cloned.1.call-done = bf16[65536,256]{1,0:T(8,128)(2,1)} async-done(((bf16[4096,256]{1,0:T(8,128)(2,1)}), bf16[65536,256]{1,0:T(8,128)(2,1)}) %all-gather.2.cloned.1.call-update) | async-done | bytes 33554448 | tf_op jit(solution)/shard_map/all_gather | solution.py:126
  209.0 36.8 %shard_map.82 = bf16[8,512,512]{2,1,0:T(8,128)(2,1)} custom-call(s32[64]{0:T(128)} %reshape.59.ids_ref, s32[8]{0:T(128)} %get-tuple-element.58.cnt_ref, s32[64]{0:T(128)} %reshape.60.kind_ref, s32[8]{0:T(128)} %get-tuple-element.57.bath_ref, bf16[128,512,256]{2,1,0:T(8,128)(2,1)} %bitcast.83, bf16[8,512,256]{2,1,0:T(8,128)(2,1)} %bitcast.84, ...), custom_call_target="tpu_custom_call" | custom-call | tf_op jit(solution)/shard_map/pallas_call | solution.py:78
  245.8 5.8 %convolution_bitcast_fusion = f32[512,512]{1,0:T(8,128)S(1)} fusion(bf16[8,512,512]{2,1,0:T(8,128)(2,1)} %shard_map.82), kind=kOutput, calls=%fused_computation.5 | convolution fusion | flops 2147483648 | bytes 5242880 | tf_op jit(solution)/shard_map/dot_general | solution.py:134
  252.1 13.5 %collective-permute-done = f32[131072]{0:T(1024)S(1)} collective-permute-done((f32[131072]{0:T(1024)S(1)}, f32[131072]{0:T(1024)S(1)}, u32[]{:S(2)}, u32[]{:S(2)}) %collective-permute-start) | collective-permute-done | bytes 524320 | tf_op jit(solution)/shard_map/ppermute | solution.py:97
  265.8 10.6 %collective-permute-done.1 = f32[65536]{0:T(1024)S(1)} collective-permute-done((f32[65536]{0:T(1024)S(1)}, f32[65536]{0:T(1024)S(1)}, u32[]{:S(2)}, u32[]{:S(2)}) %collective-permute-start.1) | collective-permute-done | bytes 262176 | tf_op jit(solution)/shard_map/ppermute | solution.py:97
  276.6 5.5 %collective-permute-done.2 = f32[32768]{0:T(1024)S(1)} collective-permute-done((f32[32768]{0:T(1024)S(1)}, f32[32768]{0:T(1024)S(1)}, u32[]{:S(2)}, u32[]{:S(2)}) %collective-permute-start.2) | collective-permute-done | bytes 131104 | tf_op jit(solution)/shard_map/ppermute | solution.py:97
  282.2 5.8 %collective-permute-done.3 = f32[16384]{0:T(1024)S(1)} collective-permute-done((f32[16384]{0:T(1024)S(1)}, f32[16384]{0:T(1024)S(1)}, u32[]{:S(2)}, u32[]{:S(2)}) %collective-permute-start.3) | collective-permute-done | bytes 65568 | tf_op jit(solution)/shard_map/ppermute | solution.py:97
  288.1 1.2 collective-permute-done.4
  289.4 3.7 collective-permute-done.5
  293.2 5.1 %collective-permute-done.6 = f32[2048]{0:T(1024)S(1)} collective-permute-done((f32[2048]{0:T(1024)S(1)}, f32[2048]{0:T(1024)S(1)}, u32[]{:S(2)}, u32[]{:S(2)}) %collective-permute-start.6) | collective-permute-done | bytes 8224 | tf_op jit(solution)/shard_map/ppermute | solution.py:97
  298.4 5.1 %collective-permute-done.7 = f32[2048]{0:T(1024)S(1)} collective-permute-done((f32[2048]{0:T(1024)S(1)}, f32[2048]{0:T(1024)S(1)}, u32[]{:S(2)}, u32[]{:S(2)}) %collective-permute-start.7) | collective-permute-done | bytes 8224 | tf_op jit(solution)/shard_map/ppermute | solution.py:101
  303.5 3.7 collective-permute-done.8
  307.3 1.2 collective-permute-done.9
  308.6 5.8 %collective-permute-done.10 = f32[16384]{0:T(1024)S(1)} collective-permute-done((f32[16384]{0:T(1024)S(1)}, f32[16384]{0:T(1024)S(1)}, u32[]{:S(2)}, u32[]{:S(2)}) %collective-permute-start.10) | collective-permute-done | bytes 65568 | tf_op jit(solution)/shard_map/ppermute | solution.py:101
  314.7 4.7 collective-permute-done.11
  319.5 9.4 %collective-permute-done.12 = f32[65536]{0:T(1024)S(1)} collective-permute-done((f32[65536]{0:T(1024)S(1)}, f32[65536]{0:T(1024)S(1)}, u32[]{:S(2)}, u32[]{:S(2)}) %collective-permute-start.12) | collective-permute-done | bytes 262176 | tf_op jit(solution)/shard_map/ppermute | solution.py:101
  329.8 8.9 %collective-permute-done.13 = f32[131072]{0:T(1024)S(1)} collective-permute-done((f32[131072]{0:T(1024)S(1)}, f32[131072]{0:T(1024)S(1)}, u32[]{:S(2)}, u32[]{:S(2)}) %collective-permute-start.13) | collective-permute-done | bytes 524320 | tf_op jit(solution)/shard_map/ppermute | solution.py:101
  338.8 0.6 fusion.1
  339.5 1.0 fusion.32
  340.7 11.7 %cholesky.130 = f32[128,128]{1,0:T(8,128)S(1)} custom-call(f32[128,128]{1,0:T(8,128)S(1)} %cholesky.194), custom_call_target="Cholesky" | custom-call | tf_op jit(solution)/shard_map/jit(cholesky)/cholesky | solution.py:21
  352.5 9.8 %custom-call.13 = f32[1,128,128]{1,2,0:T(8,128)S(1)} custom-call(f32[1,128,128]{2,1,0:T(8,128)S(1)} %get-tuple-element.52), custom_call_target="InvertDiagBlocksLowerTriangular" | custom-call | tf_op jit(solution)/shard_map/jit(cholesky)/cholesky | solution.py:21
  362.8 11.9 %cholesky.147 = f32[128,128]{1,0:T(8,128)S(1)} custom-call(f32[128,128]{1,0:T(8,128)S(1)} %convolution_subtract_fusion.3), custom_call_target="Cholesky" | custom-call | tf_op jit(solution)/shard_map/jit(cholesky)/cholesky | solution.py:21
  374.7 0.6 compare_reduce_fusion.3
  375.3 0.7 compare_reduce_fusion.2
  377.4 3.9 while.4
  378.0 1.3 bitcast_dynamic-update-slice_fusion.4
  380.0 1.3 bitcast_dynamic-update-slice_fusion.4
  381.3 19.7 %custom-call.14 = f32[2,128,128]{1,2,0:T(8,128)S(1)} custom-call(f32[2,128,128]{2,1,0:T(8,128)S(1)} %get-tuple-element.21), custom_call_target="InvertDiagBlocksLowerTriangular" | custom-call | tf_op jit(solution)/shard_map/triangular_solve/custom-call.0 | solution.py:22
  402.4 1.0 fusion
  403.5 1.0 fusion.33
  404.7 11.7 %cholesky.164 = f32[128,128]{1,0:T(8,128)S(1)} custom-call(f32[128,128]{1,0:T(8,128)S(1)} %cholesky.197), custom_call_target="Cholesky" | custom-call | tf_op jit(solution)/shard_map/jit(cholesky)/cholesky | solution.py:21
  416.5 9.8 %custom-call.15 = f32[1,128,128]{1,2,0:T(8,128)S(1)} custom-call(f32[1,128,128]{2,1,0:T(8,128)S(1)} %get-tuple-element.48), custom_call_target="InvertDiagBlocksLowerTriangular" | custom-call | tf_op jit(solution)/shard_map/jit(cholesky)/cholesky | solution.py:21
  426.8 11.9 %cholesky.181 = f32[128,128]{1,0:T(8,128)S(1)} custom-call(f32[128,128]{1,0:T(8,128)S(1)} %convolution_subtract_fusion.2), custom_call_target="Cholesky" | custom-call | tf_op jit(solution)/shard_map/jit(cholesky)/cholesky | solution.py:21
  438.7 0.6 compare_reduce_fusion.1
  439.3 0.6 compare_reduce_fusion
  441.2 3.8 while.5
  441.8 1.3 bitcast_dynamic-update-slice_fusion.5
  443.8 1.3 bitcast_dynamic-update-slice_fusion.5
  445.1 19.7 %custom-call.16 = f32[2,128,128]{1,2,0:T(8,128)S(1)} custom-call(f32[2,128,128]{2,1,0:T(8,128)S(1)} %get-tuple-element.22), custom_call_target="InvertDiagBlocksLowerTriangular" | custom-call | tf_op jit(solution)/shard_map/triangular_solve/custom-call.0 | solution.py:22
  465.2 0.6 convolution_subtract_fusion
  466.2 4.8 %convolution_convert_fusion = bf16[4096,256]{1,0:T(8,128)(2,1)} fusion(bf16[4096,512]{1,0:T(8,128)(2,1)} %bitcast.82, bf16[512,128]{0,1:T(8,128)(2,1)S(1)} %fusion.13, f32[512,128]{0,1:T(8,128)S(1)} %bitcast.87), kind=kOutput, calls=%fused_computation.4 | convolution fusion | flops 1075314688 | bytes 6684672 | tf_op jit(solution)/shard_map/dot_general | solution.py:140
  (84 shorter events, 8.9 us)
Async XLA Ops:
  6.5 7.4 %copy-start = (s32[8]{0:T(128)S(1)}, s32[8]{0:T(128)}, u32[]{:S(2)}) copy-start(s32[8]{0:T(128)} %param.17) | copy-start | bytes 100
  6.5 7.4 %copy-start.1 = (s32[8]{0:T(128)S(1)}, s32[8]{0:T(128)}, u32[]{:S(2)}) copy-start(s32[8]{0:T(128)} %param.14) | copy-start | bytes 100
  6.5 202.5 %all-gather.2.cloned.1.call-start = ((), (), s32[]{:S(2)}) async-start(), calls=%async_computation | async-start | bytes 35651584 | tf_op jit(solution)/shard_map/all_gather | solution.py:126
  251.9 13.8 %collective-permute-start = (f32[131072]{0:T(1024)S(1)}, f32[131072]{0:T(1024)S(1)}, u32[]{:S(2)}, u32[]{:S(2)}) collective-permute-start(f32[131072]{0:T(1024)S(1)} %bitcast.88), channel_id=1, source_target_pairs={{0,1},{1,0},{2,3},{3,2},{4,5},{5,4},{6,7},{7,6},{8,9},{9,8},{10,11... | collective-permute-start | bytes 1572872 | tf_op jit(solution)/shard_map/ppermute | solution.py:97
  265.7 10.7 %collective-permute-start.1 = (f32[65536]{0:T(1024)S(1)}, f32[65536]{0:T(1024)S(1)}, u32[]{:S(2)}, u32[]{:S(2)}) collective-permute-start(f32[65536]{0:T(1024)S(1)} %slice_select_fusion), channel_id=1, source_target_pairs={{0,2},{1,3},{2,0},{3,1},{4,6},{5,7},{6,4},{7,5},{8,10},{9,11},{10,... | collective-permute-start | bytes 786440 | tf_op jit(solution)/shard_map/ppermute | solution.py:97
  276.5 5.6 %collective-permute-start.2 = (f32[32768]{0:T(1024)S(1)}, f32[32768]{0:T(1024)S(1)}, u32[]{:S(2)}, u32[]{:S(2)}) collective-permute-start(f32[32768]{0:T(1024)S(1)} %slice_select_fusion.1), channel_id=1, source_target_pairs={{0,4},{1,5},{2,6},{3,7},{4,0},{5,1},{6,2},{7,3},{8,12},{9,13},{10,... | collective-permute-start | bytes 393224 | tf_op jit(solution)/shard_map/ppermute | solution.py:97
  282.1 5.8 %collective-permute-start.3 = (f32[16384]{0:T(1024)S(1)}, f32[16384]{0:T(1024)S(1)}, u32[]{:S(2)}, u32[]{:S(2)}) collective-permute-start(f32[16384]{0:T(1024)S(1)} %slice_select_fusion.2), channel_id=1, source_target_pairs={{0,8},{1,9},{2,10},{3,11},{4,12},{5,13},{6,14},{7,15},{8,0},{9,1},... | collective-permute-start | bytes 196616 | tf_op jit(solution)/shard_map/ppermute | solution.py:97
  288.0 1.3 collective-permute-start.4
  289.3 3.8 collective-permute-start.5
  293.1 5.2 %collective-permute-start.6 = (f32[2048]{0:T(1024)S(1)}, f32[2048]{0:T(1024)S(1)}, u32[]{:S(2)}, u32[]{:S(2)}) collective-permute-start(f32[2048]{0:T(1024)S(1)} %slice_select_fusion.5), channel_id=1, source_target_pairs={{0,64},{1,65},{2,66},{3,67},{4,68},{5,69},{6,70},{7,71},{8,72},{9,... | collective-permute-start | bytes 24584 | tf_op jit(solution)/shard_map/ppermute | solution.py:97
  298.4 5.2 %collective-permute-start.7 = (f32[2048]{0:T(1024)S(1)}, f32[2048]{0:T(1024)S(1)}, u32[]{:S(2)}, u32[]{:S(2)}) collective-permute-start(f32[2048]{0:T(1024)S(1)} %select_add_fusion.5), channel_id=1, source_target_pairs={{0,64},{1,65},{2,66},{3,67},{4,68},{5,69},{6,70},{7,71},{8,72},{9,... | collective-permute-start | bytes 24584 | tf_op jit(solution)/shard_map/ppermute | solution.py:101
  303.5 3.7 collective-permute-start.8
  307.3 1.2 collective-permute-start.9
  308.5 5.8 %collective-permute-start.10 = (f32[16384]{0:T(1024)S(1)}, f32[16384]{0:T(1024)S(1)}, u32[]{:S(2)}, u32[]{:S(2)}) collective-permute-start(f32[16384]{0:T(1024)S(1)} %maximum_select_fusion.9), channel_id=1, source_target_pairs={{0,8},{1,9},{2,10},{3,11},{4,12},{5,13},{6,14},{7,15},{8,0},{9,1},... | collective-permute-start | bytes 196616 | tf_op jit(solution)/shard_map/ppermute | solution.py:101
  314.4 5.0 %collective-permute-start.11 = (f32[32768]{0:T(1024)S(1)}, f32[32768]{0:T(1024)S(1)}, u32[]{:S(2)}, u32[]{:S(2)}) collective-permute-start(f32[32768]{0:T(1024)S(1)} %maximum_select_fusion.7), channel_id=1, source_target_pairs={{0,4},{1,5},{2,6},{3,7},{4,0},{5,1},{6,2},{7,3},{8,12},{9,13},{10,... | collective-permute-start | bytes 393224 | tf_op jit(solution)/shard_map/ppermute | solution.py:101
  319.5 9.5 %collective-permute-start.12 = (f32[65536]{0:T(1024)S(1)}, f32[65536]{0:T(1024)S(1)}, u32[]{:S(2)}, u32[]{:S(2)}) collective-permute-start(f32[65536]{0:T(1024)S(1)} %maximum_select_fusion.5), channel_id=1, source_target_pairs={{0,2},{1,3},{2,0},{3,1},{4,6},{5,7},{6,4},{7,5},{8,10},{9,11},{10,... | collective-permute-start | bytes 786440 | tf_op jit(solution)/shard_map/ppermute | solution.py:101
  329.0 9.7 %collective-permute-start.13 = (f32[131072]{0:T(1024)S(1)}, f32[131072]{0:T(1024)S(1)}, u32[]{:S(2)}, u32[]{:S(2)}) collective-permute-start(f32[131072]{0:T(1024)S(1)} %maximum_select_fusion.3), channel_id=1, source_target_pairs={{0,1},{1,0},{2,3},{3,2},{4,5},{5,4},{6,7},{7,6},{8,9},{9,8},{10,11... | collective-permute-start | bytes 1572872 | tf_op jit(solution)/shard_map/ppermute | solution.py:101
Sparse Core Ops, SparseCore 0:
  9.5 199.4 all-gather.1

commit v2 on v1

--- a/solution.py
+++ b/solution.py
@@ -26,67 +26,104 @@
 
 
 def step_kernel(slots, ids_ref, cnt_ref, kind_ref, bath_ref,
-                nbr_ref, own_ref, ons_ref, cpl_ref, bth_ref, out_ref, acc):
+                group_hbm, own_ref, ons_ref, cpl_ref, bth_ref, out_ref, buf, sems, acc):
     b = pl.program_id(0)
-    k = pl.program_id(1)
+    last = pl.num_programs(0) - 1
     rank_cols = own_ref.shape[2]
 
-    @pl.when(k == 0)
+    def fetch(blk, slot):
+        for k in range(slots):
+            @pl.when(k < cnt_ref[blk])
+            def _():
+                pltpu.make_async_copy(
+                    group_hbm.at[ids_ref[blk * slots + k]], buf.at[slot, k], sems.at[slot, k]
+                ).start()
+
+    @pl.when(b == 0)
     def _():
-        acc[...] = jnp.zeros_like(acc)
+        fetch(0, 0)
 
-    @pl.when(k < cnt_ref[b])
+    @pl.when(b < last)
     def _():
-        t = kind_ref[b * slots + k]
-        acc[t] += nbr_ref[0].astype(jnp.float32)
+        fetch(b + 1, (b + 1) % 2)
 
-    @pl.when(k == slots - 1)
-    def _():
-        coupled = jnp.dot(cpl_ref[0], acc[0].astype(jnp.bfloat16), preferred_element_type=jnp.float32)
-        for t in range(1, cpl_ref.shape[0]):
-            coupled += jnp.dot(cpl_ref[t], acc[t].astype(jnp.bfloat16), preferred_element_type=jnp.float32)
-        own = own_ref[0]
-        wide = own.astype(jnp.float32)
-        moved = wide - time_step * (ons_ref[0] * wide + coupled)
-        out_ref[0, :, :rank_cols] = moved.astype(out_ref.dtype)
-        bathed = jnp.dot(bth_ref[0], own, preferred_element_type=jnp.float32)
-        out_ref[0, :, rank_cols:] = bathed.astype(out_ref.dtype)
+    slot = b % 2
+    acc[...] = jnp.zeros_like(acc)
+    for k in range(slots):
+        @pl.when(k < cnt_ref[b])
+        def _():
+            pltpu.make_async_copy(group_hbm.at[0], buf.at[slot, k], sems.at[slot, k]).wait()
+            t = kind_ref[b * slots + k]
+            acc[t] += buf[slot, k].astype(jnp.float32)
+
+    coupled = jnp.dot(cpl_ref[0], acc[0].astype(jnp.bfloat16), preferred_element_type=jnp.float32)
+    for t in range(1, cpl_ref.shape[0]):
+        coupled += jnp.dot(cpl_ref[t], acc[t].astype(jnp.bfloat16), preferred_element_type=jnp.float32)
+    own = own_ref[0]
+    wide = own.astype(jnp.float32)
+    moved = wide - time_step * (ons_ref[0] * wide + coupled)
+    out_ref[0, :, :rank_cols] = moved.astype(out_ref.dtype)
+    bathed = jnp.dot(bth_ref[0], own, preferred_element_type=jnp.float32)
+    out_ref[0, :, rank_cols:] = bathed.astype(out_ref.dtype)
 
 
 def stacked_blocks(group_rows, own_rows, energy, ids, counts, kinds, bath_pattern, coupling_blocks, bath_blocks):
     blocks, block_rows, rank_cols = own_rows.shape
     slots = ids.shape[0] // blocks
     kinds_n = coupling_blocks.shape[0]
-
-    def nbr_map(b, k, ids_ref, cnt_ref, kind_ref, bath_ref):
-        live = jnp.minimum(k, cnt_ref[b] - 1)
-        return (ids_ref[b * slots + live], 0, 0)
-
     grid_spec = pltpu.PrefetchScalarGridSpec(
         num_scalar_prefetch=4,
-        grid=(blocks, slots),
+        grid=(blocks,),
         in_specs=[
-            pl.BlockSpec((1, block_rows, rank_cols), nbr_map),
-            pl.BlockSpec((1, block_rows, rank_cols), lambda b, k, *_: (b, 0, 0)),
-            pl.BlockSpec((1, block_rows, 1), lambda b, k, *_: (b, 0, 0)),
-            pl.BlockSpec((kinds_n, block_rows, block_rows), lambda b, k, *_: (0, 0, 0)),
-            pl.BlockSpec((1, block_rows, block_rows), lambda b, k, i, c, t, bp: (bp[b], 0, 0)),
+            pl.BlockSpec(memory_space=pl.ANY),
+            pl.BlockSpec((1, block_rows, rank_cols), lambda b, *_: (b, 0, 0)),
+            pl.BlockSpec((1, block_rows, 1), lambda b, *_: (b, 0, 0)),
+            pl.BlockSpec((kinds_n, block_rows, block_rows), lambda b, *_: (0, 0, 0)),
+            pl.BlockSpec((1, block_rows, block_rows), lambda b, i, c, t, bp: (bp[b], 0, 0)),
         ],
-        out_specs=pl.BlockSpec((1, block_rows, 2 * rank_cols), lambda b, k, *_: (b, 0, 0)),
-        scratch_shapes=[pltpu.VMEM((kinds_n, block_rows, rank_cols), jnp.float32)],
+        out_specs=pl.BlockSpec((1, block_rows, 2 * rank_cols), lambda b, *_: (b, 0, 0)),
+        scratch_shapes=[
+            pltpu.VMEM((2, slots, block_rows, rank_cols), group_rows.dtype),
+            pltpu.SemaphoreType.DMA((2, slots)),
+            pltpu.VMEM((kinds_n, block_rows, rank_cols), jnp.float32),
+        ],
     )
     return pl.pallas_call(
         functools.partial(step_kernel, slots),
         grid_spec=grid_spec,
         out_shape=jax.ShapeDtypeStruct((blocks, block_rows, 2 * rank_cols), jnp.bfloat16),
+        compiler_params=pltpu.CompilerParams(dimension_semantics=("arbitrary",)),
     )(ids, counts, kinds, bath_pattern, group_rows, own_rows, energy, coupling_blocks, bath_blocks)
 
 
-def halving_sum(local, axes, count):
+def pack_symmetric(gram, half):
+    upper = gram[:half, half:]
+    rows = lax.broadcasted_iota(jnp.int32, (half, half), 0)
+    cols = lax.broadcasted_iota(jnp.int32, (half, half), 1)
+    corner = gram[half:, half:]
+    mixed = jnp.where(rows <= cols, gram[:half, :half], corner)
+    return jnp.concatenate([upper.reshape(-1), mixed.reshape(-1), jnp.diagonal(corner)])
+
+
+def unpack_symmetric(packed, half):
+    area = half * half
+    upper = packed[:area].reshape(half, half)
+    mixed = packed[area:2 * area].reshape(half, half)
+    diag = packed[2 * area:]
+    rows = lax.broadcasted_iota(jnp.int32, (half, half), 0)
+    cols = lax.broadcasted_iota(jnp.int32, (half, half), 1)
+    first = jnp.where(rows <= cols, mixed, mixed.T)
+    corner = jnp.where(rows > cols, mixed, mixed.T)
+    corner = jnp.where(rows == cols, diag[None, :], corner)
+    return jnp.concatenate(
+        [jnp.concatenate([first, upper], axis=1), jnp.concatenate([upper.T, corner], axis=1)], axis=0
+    )
+
+
+def halving_sum(local, axes, count, order):
     me = lax.axis_index(axes)
-    buf = local.reshape(-1)
+    buf = local
     stages = []
-    order = [s for s in range(count.bit_length() - 1)]
     for s in order:
         bit = (me >> s) & 1
         half = buf.shape[0] // 2
@@ -100,7 +137,7 @@
         pairs = [(i, i ^ (1 << s)) for i in range(count)]
         other = lax.ppermute(buf, axes, pairs)
         buf = jnp.where(bit == 1, jnp.concatenate([other, buf]), jnp.concatenate([buf, other]))
-    return buf.reshape(local.shape)
+    return buf
 
 
 def shards(
@@ -135,7 +172,10 @@
         stacked, stacked, (((0,), (0,)), ((), ())), preferred_element_type=jnp.float32
     )
     devices = lax.axis_size("row") * col_count
-    gram_sum = halving_sum(local_gram, ("row", "col"), devices)
+    stage_bits = devices.bit_length() - 1
+    order = [4, 0, 2, 5, 1, 3, 6] if stage_bits == 7 else list(range(stage_bits))
+    packed = halving_sum(pack_symmetric(local_gram, rank_cols), ("row", "col"), devices, order)
+    gram_sum = unpack_symmetric(packed, rank_cols)
     rotation = orthonormal_steps(gram_sum, rank_cols).astype(jnp.bfloat16)
     return jnp.dot(stacked, rotation, preferred_element_type=jnp.float32).astype(jnp.bfloat16)
 

time: 485 us -> 447 us (0.922)
  the two profiles are of different devices: /device:TPU:10 before, /device:TPU:1 now
where the time goes in v2:
time: 447 us; the launch traced here: 439 us
  waiting for transfers between devices  222 us (50%)
  other arithmetic  112 us (25%)
  starting transfers between devices  38.4 us (9%)
  matrix products  18.1 us (4%)
  between operations  16.8 us (4%)
  local copies, waits for them, and re-layouts  16.7 us (4%)
  Pallas kernels  15.4 us (3%)
    all_gather x1, waiting for transfers between devices, shards(): gathered = lax.all_gather(density_factor, 'col', axis=0, tiled=True)  196 us
    another operation x14, other arithmetic, orthonormal_steps(): factor = jnp.linalg.cholesky(inner)  69.7 us
    another operation x5, other arithmetic, orthonormal_steps(): lax.linalg.triangular_solve(factor, image, left_side=False, lower=True, t...  39.4 us
    ppermute x7, starting transfers between devices, halving_sum(): other = lax.ppermute(buf, axes, pairs)  25.4 us
    pallas_call x1, Pallas kernels, stacked_blocks(): pl.pallas_call(functools.partial(step_kernel, slots), grid_spec=grid_spec...  15.4 us
    ppermute x7, starting transfers between devices, halving_sum(): buf = keep + lax.ppermute(send, axes, pairs)  13 us
    ppermute x7, waiting for transfers between devices, halving_sum(): buf = keep + lax.ppermute(send, axes, pairs)  12.7 us
    ppermute x7, waiting for transfers between devices, halving_sum(): other = lax.ppermute(buf, axes, pairs)  12.1 us
  transfers between devices with their start and end apart: 15, of which 15 were waited for; matrix products, arithmetic and copies ran while one was open for 2% of the time, Pallas kernels for 0%

profile of v2, /device:TPU:1, one launch (start us, length us, event | category | flops | bytes accessed | tf_op | source)
XLA Modules:
  0.0 439.4 jit_solution(1850478725053020581)
XLA Ops:
  8.6 4.0 reshape.97.ons_ref
  13.9 196.0 %all-gather.2.cloned.1.call-done = bf16[65536,256]{1,0:T(8,128)(2,1)} async-done(((bf16[4096,256]{1,0:T(8,128)(2,1)}), bf16[65536,256]{1,0:T(8,128)(2,1)}) %all-gather.2.cloned.1.call-update) | async-done | bytes 33554448 | tf_op jit(solution)/shard_map/all_gather | solution.py:163
  210.0 15.4 %shard_map.82 = bf16[8,512,512]{2,1,0:T(8,128)(2,1)} custom-call(s32[64]{0:T(128)} %reshape.54.ids_ref, s32[8]{0:T(128)} %get-tuple-element.63.cnt_ref, s32[64]{0:T(128)} %reshape.55.kind_ref, s32[8]{0:T(128)} %get-tuple-element.62.bath_ref, bf16[128,512,256]{2,1,0:T(8,128)(2,1)} %bitcast.90, bf16[8,512,256]{2,1,0:T(8,128)(2,1)} %bitcast.92, ...), custom_call_target="tpu_custom_call" | custom-call | tf_op jit(solution)/shard_map/pallas_call | solution.py:91
  225.4 5.8 %convolution_bitcast_fusion = f32[512,512]{1,0:T(8,128)S(1)} fusion(bf16[8,512,512]{2,1,0:T(8,128)(2,1)} %shard_map.82), kind=kOutput, calls=%fused_computation.6 | convolution fusion | flops 2147483648 | bytes 5242880 | tf_op jit(solution)/shard_map/dot_general | solution.py:171
  231.6 2.3 gather_fusion
  234.0 1.3 collective-permute-start
  235.3 1.2 collective-permute-done
  236.6 1.3 collective-permute-start.1
  237.9 3.6 collective-permute-done.1
  241.7 1.2 collective-permute-start.2
  242.9 2.0 collective-permute-done.2
  245.1 1.2 collective-permute-start.3
  246.2 1.7 collective-permute-done.3
  248.1 2.5 collective-permute-start.4
  250.7 1.6 collective-permute-done.4
  252.4 2.5 collective-permute-start.5
  255.0 1.6 collective-permute-done.5
  256.7 3.0 collective-permute-start.6
  259.7 1.0 collective-permute-done.6
  260.8 3.0 collective-permute-start.7
  263.8 1.0 collective-permute-done.7
  264.9 2.5 collective-permute-start.8
  267.4 1.5 collective-permute-done.8
  269.0 2.5 collective-permute-start.9
  271.5 1.6 collective-permute-done.9
  273.3 1.1 collective-permute-start.10
  274.4 1.8 collective-permute-done.10
  276.2 1.2 collective-permute-start.11
  277.4 2.1 collective-permute-done.11
  279.6 1.3 collective-permute-start.12
  280.8 2.9 collective-permute-done.12
  283.9 13.8 %collective-permute-start.13 = (f32[65664]{0:T(1024)S(1)}, f32[65664]{0:T(1024)S(1)}, u32[]{:S(2)}, u32[]{:S(2)}) collective-permute-start(f32[65664]{0:T(1024)S(1)} %maximum_select_fusion.1), channel_id=1, source_target_pairs={{0,16},{1,17},{2,18},{3,19},{4,20},{5,21},{6,22},{7,23},{8,24},{9,... | collective-permute-start | bytes 787976 | tf_op jit(solution)/shard_map/ppermute | solution.py:138
  297.7 1.2 collective-permute-done.13
  301.3 11.7 %cholesky.130 = f32[128,128]{1,0:T(8,128)S(1)} custom-call(f32[128,128]{1,0:T(8,128)S(1)} %cholesky.194), custom_call_target="Cholesky" | custom-call | tf_op jit(solution)/shard_map/jit(cholesky)/cholesky | solution.py:21
  313.1 9.8 %custom-call.15 = f32[1,128,128]{1,2,0:T(8,128)S(1)} custom-call(f32[1,128,128]{2,1,0:T(8,128)S(1)} %get-tuple-element.57), custom_call_target="InvertDiagBlocksLowerTriangular" | custom-call | tf_op jit(solution)/shard_map/jit(cholesky)/cholesky | solution.py:21
  323.4 11.9 %cholesky.147 = f32[128,128]{1,0:T(8,128)S(1)} custom-call(f32[128,128]{1,0:T(8,128)S(1)} %convolution_subtract_fusion.3), custom_call_target="Cholesky" | custom-call | tf_op jit(solution)/shard_map/jit(cholesky)/cholesky | solution.py:21
  338.0 4.1 while.4
  338.7 1.3 bitcast_dynamic-update-slice_fusion.4
  340.7 1.3 bitcast_dynamic-update-slice_fusion.4
  342.1 19.7 %custom-call.16 = f32[2,128,128]{1,2,0:T(8,128)S(1)} custom-call(f32[2,128,128]{2,1,0:T(8,128)S(1)} %get-tuple-element.21), custom_call_target="InvertDiagBlocksLowerTriangular" | custom-call | tf_op jit(solution)/shard_map/triangular_solve/custom-call.0 | solution.py:22
  365.5 11.7 %cholesky.164 = f32[128,128]{1,0:T(8,128)S(1)} custom-call(f32[128,128]{1,0:T(8,128)S(1)} %cholesky.197), custom_call_target="Cholesky" | custom-call | tf_op jit(solution)/shard_map/jit(cholesky)/cholesky | solution.py:21
  377.2 9.8 %custom-call.17 = f32[1,128,128]{1,2,0:T(8,128)S(1)} custom-call(f32[1,128,128]{2,1,0:T(8,128)S(1)} %get-tuple-element.53), custom_call_target="InvertDiagBlocksLowerTriangular" | custom-call | tf_op jit(solution)/shard_map/jit(cholesky)/cholesky | solution.py:21
  387.5 11.9 %cholesky.181 = f32[128,128]{1,0:T(8,128)S(1)} custom-call(f32[128,128]{1,0:T(8,128)S(1)} %convolution_subtract_fusion.2), custom_call_target="Cholesky" | custom-call | tf_op jit(solution)/shard_map/jit(cholesky)/cholesky | solution.py:21
  402.2 4.0 while.5
  402.8 1.3 bitcast_dynamic-update-slice_fusion.5
  404.8 1.3 bitcast_dynamic-update-slice_fusion.5
  406.2 19.7 %custom-call.18 = f32[2,128,128]{1,2,0:T(8,128)S(1)} custom-call(f32[2,128,128]{2,1,0:T(8,128)S(1)} %get-tuple-element.22), custom_call_target="InvertDiagBlocksLowerTriangular" | custom-call | tf_op jit(solution)/shard_map/triangular_solve/custom-call.0 | solution.py:22
  427.3 4.8 %convolution_convert_fusion = bf16[4096,256]{1,0:T(8,128)(2,1)} fusion(bf16[4096,512]{1,0:T(8,128)(2,1)} %bitcast.89, bf16[512,128]{0,1:T(8,128)(2,1)S(1)} %fusion.14, f32[512,128]{0,1:T(8,128)S(1)} %bitcast.98), kind=kOutput, calls=%fused_computation.5 | convolution fusion | flops 1075314688 | bytes 6684672 | tf_op jit(solution)/shard_map/dot_general | solution.py:180
  (89 shorter events, 19.2 us)
Async XLA Ops:
  6.5 6.1 %copy-start = (s32[8,8]{1,0:T(8,128)S(1)}, s32[8,8]{1,0:T(8,128)}, u32[]{:S(2)}) copy-start(s32[8,8]{1,0:T(8,128)} %param.15) | copy-start | bytes 772
  6.5 6.8 %copy-start.2 = (s32[8]{0:T(128)S(1)}, s32[8]{0:T(128)}, u32[]{:S(2)}) copy-start(s32[8]{0:T(128)} %param.14) | copy-start | bytes 100
  6.5 6.8 %copy-start.1 = (s32[8]{0:T(128)S(1)}, s32[8]{0:T(128)}, u32[]{:S(2)}) copy-start(s32[8]{0:T(128)} %param.17) | copy-start | bytes 100
  6.5 203.4 %all-gather.2.cloned.1.call-start = ((), (), s32[]{:S(2)}) async-start(), calls=%async_computation | async-start | bytes 35651584 | tf_op jit(solution)/shard_map/all_gather | solution.py:163
  234.0 2.4 collective-permute-start
  236.6 4.9 %collective-permute-start.1 = (f32[32832]{0:T(1024)S(1)}, f32[32832]{0:T(1024)S(1)}, u32[]{:S(2)}, u32[]{:S(2)}) collective-permute-start(f32[32832]{0:T(1024)S(1)} %slice_select_fusion.1), channel_id=1, source_target_pairs={{0,1},{1,0},{2,3},{3,2},{4,5},{5,4},{6,7},{7,6},{8,9},{9,8},{10,11... | collective-permute-start | bytes 393992 | tf_op jit(solution)/shard_map/ppermute | solution.py:134
  241.7 3.2 collective-permute-start.2
  245.1 2.9 collective-permute-start.3
  248.1 4.2 collective-permute-start.4
  252.4 4.1 collective-permute-start.5
  256.7 4.0 collective-permute-start.6
  260.8 4.0 collective-permute-start.7
  264.9 4.1 collective-permute-start.8
  269.0 4.2 collective-permute-start.9
  273.3 2.8 collective-permute-start.10
  276.2 3.2 collective-permute-start.11
  279.6 4.2 collective-permute-start.12
  283.9 15.0 %collective-permute-start.13 = (f32[65664]{0:T(1024)S(1)}, f32[65664]{0:T(1024)S(1)}, u32[]{:S(2)}, u32[]{:S(2)}) collective-permute-start(f32[65664]{0:T(1024)S(1)} %maximum_select_fusion.1), channel_id=1, source_target_pairs={{0,16},{1,17},{2,18},{3,19},{4,20},{5,21},{6,22},{7,23},{8,24},{9,... | collective-permute-start | bytes 787976 | tf_op jit(solution)/shard_map/ppermute | solution.py:138
Sparse Core Ops, SparseCore 0:
  9.5 200.4 all-gather.1

commit v3 on v2

--- a/solution.py
+++ b/solution.py
@@ -14,15 +14,15 @@
 
 
 def orthonormal_steps(gram, rank_cols):
-    basis = jnp.eye(2 * rank_cols, rank_cols, dtype=jnp.float32)
-    for sweep in range(SWEEPS):
+    def sweep(_, basis):
         image = jnp.dot(gram, basis, precision=lax.Precision.HIGHEST)
         inner = jnp.dot(image.T, image, precision=lax.Precision.HIGHEST)
         factor = jnp.linalg.cholesky(inner)
-        basis = lax.linalg.triangular_solve(
+        return lax.linalg.triangular_solve(
             factor, image, left_side=False, lower=True, transpose_a=True
         )
-    return basis
+
+    return lax.fori_loop(0, SWEEPS, sweep, jnp.eye(2 * rank_cols, rank_cols, dtype=jnp.float32))
 
 
 def step_kernel(slots, ids_ref, cnt_ref, kind_ref, bath_ref,

time: 447 us -> 439 us (0.982); the launches traced: 439 us -> 439 us
  starting transfers between devices: 38.4 us -> 32 us
  waiting for transfers between devices: 222 us -> 228 us
    another operation x19 -> x20, other arithmetic: 109 us -> 108 us  [the longest x12 68.1 us: sweep(): factor = jnp.linalg.cholesky(inner)]
where the time goes in v3:
time: 439 us
  waiting for transfers between devices  228 us (52%)
  other arithmetic  111 us (25%)
  starting transfers between devices  32 us (7%)
  matrix products  18.6 us (4%)
  local copies, waits for them, and re-layouts  16.9 us (4%)
  Pallas kernels  15.4 us (4%)
  between operations  13.6 us (3%)
    all_gather x1, waiting for transfers between devices, shards(): gathered = lax.all_gather(density_factor, 'col', axis=0, tiled=True)  196 us
    another operation x12, other arithmetic, sweep(): factor = jnp.linalg.cholesky(inner)  68.1 us
    another operation x8, other arithmetic, sweep(): lax.linalg.triangular_solve(factor, image, left_side=False, lower=True, t...  39.5 us
    ppermute x7, starting transfers between devices, halving_sum(): other = lax.ppermute(buf, axes, pairs)  22.5 us
    ppermute x7, waiting for transfers between devices, halving_sum(): buf = keep + lax.ppermute(send, axes, pairs)  16.7 us
    pallas_call x1, Pallas kernels, stacked_blocks(): pl.pallas_call(functools.partial(step_kernel, slots), grid_spec=grid_spec...  15.4 us
    ppermute x7, waiting for transfers between devices, halving_sum(): other = lax.ppermute(buf, axes, pairs)  14.8 us
    ppermute x7, starting transfers between devices, halving_sum(): buf = keep + lax.ppermute(send, axes, pairs)  9.56 us
  transfers between devices with their start and end apart: 15, of which 15 were waited for; matrix products, arithmetic and copies ran while one was open for 2% of the time, Pallas kernels for 0%

profile of v3, /device:TPU:1, one launch (start us, length us, event | category | flops | bytes accessed | tf_op | source)
XLA Modules:
  0.0 438.7 jit_solution(2975770604354398241)
XLA Ops:
  8.6 4.0 reshape.88.ons_ref
  13.9 196.1 %all-gather.2.cloned.1.call-done = bf16[65536,256]{1,0:T(8,128)(2,1)} async-done(((bf16[4096,256]{1,0:T(8,128)(2,1)}), bf16[65536,256]{1,0:T(8,128)(2,1)}) %all-gather.2.cloned.1.call-update) | async-done | bytes 33554448 | tf_op jit(solution)/shard_map/all_gather | solution.py:163
  210.0 15.4 %shard_map.82 = bf16[8,512,512]{2,1,0:T(8,128)(2,1)} custom-call(s32[64]{0:T(128)} %reshape.54.ids_ref, s32[8]{0:T(128)} %get-tuple-element.63.cnt_ref, s32[64]{0:T(128)} %reshape.55.kind_ref, s32[8]{0:T(128)} %get-tuple-element.62.bath_ref, bf16[128,512,256]{2,1,0:T(8,128)(2,1)} %bitcast.81, bf16[8,512,256]{2,1,0:T(8,128)(2,1)} %bitcast.83, ...), custom_call_target="tpu_custom_call" | custom-call | tf_op jit(solution)/shard_map/pallas_call | solution.py:91
  225.4 5.9 %convolution_bitcast_fusion = f32[512,512]{1,0:T(8,128)S(1)} fusion(bf16[8,512,512]{2,1,0:T(8,128)(2,1)} %shard_map.82), kind=kOutput, calls=%fused_computation.30 | convolution fusion | flops 2147483648 | bytes 5242880 | tf_op jit(solution)/shard_map/dot_general | solution.py:171
  231.6 2.3 gather_fusion
  234.0 1.8 collective-permute-start
  235.8 1.2 collective-permute-done
  237.7 4.3 collective-permute-done.1
  242.3 3.1 collective-permute-done.2
  246.3 2.2 collective-permute-done.3
  248.7 2.3 collective-permute-start.4
  250.9 1.9 collective-permute-done.4
  253.0 2.0 collective-permute-start.5
  254.9 2.1 collective-permute-done.5
  257.2 2.2 collective-permute-start.6
  259.4 1.9 collective-permute-done.6
  261.3 2.2 collective-permute-start.7
  263.5 1.9 collective-permute-done.7
  265.4 2.2 collective-permute-start.8
  267.6 1.9 collective-permute-done.8
  269.6 2.2 collective-permute-start.9
  271.8 1.9 collective-permute-done.9
  274.4 2.3 collective-permute-done.10
  277.4 2.6 collective-permute-done.11
  280.1 0.8 collective-permute-start.12
  280.9 3.2 collective-permute-done.12
  284.2 13.9 %collective-permute-start.13 = (f32[65664]{0:T(1024)S(1)}, f32[65664]{0:T(1024)S(1)}, u32[]{:S(2)}, u32[]{:S(2)}) collective-permute-start(f32[65664]{0:T(1024)S(1)} %maximum_select_fusion.1), channel_id=1, source_target_pairs={{0,16},{1,17},{2,18},{3,19},{4,20},{5,21},{6,22},{7,23},{8,24},{9,... | collective-permute-start | bytes 787976 | tf_op jit(solution)/shard_map/ppermute | solution.py:138
  298.1 1.1 collective-permute-done.13
  300.0 127.0 %while.13 = (s32[]{:T(128)}, f32[512,256]{0,1:T(8,128)S(1)}, f32[512,512]{1,0:T(8,128)S(1)}, s32[]{:T(128)}, s32[]{:T(128)}, /*index=5*/f32[]{:T(128)}, s32[]{:T(128)}) while((s32[]{:T(128)}, f32[512,256]{0,1:T(8,128)S(1)}, f32[512,512]{1,0:T(8,128)S(1)}, s32[]{:T(128)}, s32[]{:T(128)}, /*index=5*/f32[]{:T(128)}, s32[]{:T(128)}) %tuple.56), condition=%wide.region_5.6_spmd, body=%wide.region_0.5_spmd.sunk | while | flops 1561018624 | bytes 9177364 | solution.py:25
  300.2 1.0 fusion.54
  301.2 1.0 fusion.55
  302.4 11.7 %cholesky.185 = f32[128,128]{1,0:T(8,128)S(1)} custom-call(f32[128,128]{1,0:T(8,128)S(1)} %cholesky.184), custom_call_target="Cholesky" | custom-call | tf_op jit(solution)/shard_map/while/body/eval_jaxpr/jit(cholesky)/cholesky | solution.py:20
  314.2 9.8 %custom-call.20 = f32[1,128,128]{1,2,0:T(8,128)S(1)} custom-call(f32[1,128,128]{2,1,0:T(8,128)S(1)} %get-tuple-element.123), custom_call_target="InvertDiagBlocksLowerTriangular" | custom-call | tf_op jit(solution)/shard_map/while/body/eval_jaxpr/jit(cholesky)/cholesky | solution.py:20
  324.5 11.7 %cholesky.187 = f32[128,128]{1,0:T(8,128)S(1)} custom-call(f32[128,128]{1,0:T(8,128)S(1)} %convolution_subtract_fusion.4), custom_call_target="Cholesky" | custom-call | tf_op jit(solution)/shard_map/while/body/eval_jaxpr/jit(cholesky)/cholesky | solution.py:20
  338.4 4.1 while.14
  339.0 1.3 bitcast_dynamic-update-slice_fusion.2
  341.1 1.3 bitcast_dynamic-update-slice_fusion.2
  342.4 19.7 %custom-call.22 = f32[2,128,128]{1,2,0:T(8,128)S(1)} custom-call(f32[2,128,128]{2,1,0:T(8,128)S(1)} %get-tuple-element.131), custom_call_target="InvertDiagBlocksLowerTriangular" | custom-call | tf_op jit(solution)/shard_map/while/body/eval_jaxpr/triangular_solve | solution.py:21
  363.6 1.0 fusion.54
  364.6 1.0 fusion.55
  365.9 11.7 %cholesky.185 = f32[128,128]{1,0:T(8,128)S(1)} custom-call(f32[128,128]{1,0:T(8,128)S(1)} %cholesky.184), custom_call_target="Cholesky" | custom-call | tf_op jit(solution)/shard_map/while/body/eval_jaxpr/jit(cholesky)/cholesky | solution.py:20
  377.6 9.8 %custom-call.20 = f32[1,128,128]{1,2,0:T(8,128)S(1)} custom-call(f32[1,128,128]{2,1,0:T(8,128)S(1)} %get-tuple-element.123), custom_call_target="InvertDiagBlocksLowerTriangular" | custom-call | tf_op jit(solution)/shard_map/while/body/eval_jaxpr/jit(cholesky)/cholesky | solution.py:20
  387.9 11.7 %cholesky.187 = f32[128,128]{1,0:T(8,128)S(1)} custom-call(f32[128,128]{1,0:T(8,128)S(1)} %convolution_subtract_fusion.4), custom_call_target="Cholesky" | custom-call | tf_op jit(solution)/shard_map/while/body/eval_jaxpr/jit(cholesky)/cholesky | solution.py:20
  401.8 4.1 while.14
  402.5 1.3 bitcast_dynamic-update-slice_fusion.2
  404.5 1.3 bitcast_dynamic-update-slice_fusion.2
  405.8 19.7 %custom-call.22 = f32[2,128,128]{1,2,0:T(8,128)S(1)} custom-call(f32[2,128,128]{2,1,0:T(8,128)S(1)} %get-tuple-element.131), custom_call_target="InvertDiagBlocksLowerTriangular" | custom-call | tf_op jit(solution)/shard_map/while/body/eval_jaxpr/triangular_solve | solution.py:21
  427.0 4.8 %convolution_convert_fusion = bf16[4096,256]{1,0:T(8,128)(2,1)} fusion(bf16[4096,512]{1,0:T(8,128)(2,1)} %bitcast.80, f32[512,256]{0,1:T(8,128)S(1)} %get-tuple-element.22), kind=kOutput, calls=%fused_computation.29 | convolution fusion | flops 1074921472 | bytes 6815744 | tf_op jit(solution)/shard_map/dot_general | solution.py:180
  (94 shorter events, 17.3 us)
Async XLA Ops:
  6.5 6.1 %copy-start = (s32[8,8]{1,0:T(8,128)S(1)}, s32[8,8]{1,0:T(8,128)}, u32[]{:S(2)}) copy-start(s32[8,8]{1,0:T(8,128)} %param.14) | copy-start | bytes 772
  6.5 6.8 %copy-start.2 = (s32[8]{0:T(128)S(1)}, s32[8]{0:T(128)}, u32[]{:S(2)}) copy-start(s32[8]{0:T(128)} %param.13) | copy-start | bytes 100
  6.5 6.8 %copy-start.1 = (s32[8]{0:T(128)S(1)}, s32[8]{0:T(128)}, u32[]{:S(2)}) copy-start(s32[8]{0:T(128)} %param.16) | copy-start | bytes 100
  6.5 203.4 %all-gather.2.cloned.1.call-start = ((), (), s32[]{:S(2)}) async-start(), calls=%async_computation | async-start | bytes 35651584 | tf_op jit(solution)/shard_map/all_gather | solution.py:163
  234.0 2.9 collective-permute-start
  237.1 4.9 %collective-permute-start.1 = (f32[32832]{0:T(1024)S(1)}, f32[32832]{0:T(1024)S(1)}, u32[]{:S(2)}, u32[]{:S(2)}) collective-permute-start(f32[32832]{0:T(1024)S(1)} %slice_select_fusion.1), channel_id=1, source_target_pairs={{0,1},{1,0},{2,3},{3,2},{4,5},{5,4},{6,7},{7,6},{8,9},{9,8},{10,11... | collective-permute-start | bytes 393992 | tf_op jit(solution)/shard_map/ppermute | solution.py:134
  242.2 3.2 collective-permute-start.2
  245.6 2.9 collective-permute-start.3
  248.7 4.2 collective-permute-start.4
  253.0 4.1 collective-permute-start.5
  257.2 4.0 collective-permute-start.6
  261.3 4.0 collective-permute-start.7
  265.4 4.1 collective-permute-start.8
  269.6 4.2 collective-permute-start.9
  273.8 2.8 collective-permute-start.10
  276.7 3.2 collective-permute-start.11
  280.1 4.0 collective-permute-start.12
  284.2 15.0 %collective-permute-start.13 = (f32[65664]{0:T(1024)S(1)}, f32[65664]{0:T(1024)S(1)}, u32[]{:S(2)}, u32[]{:S(2)}) collective-permute-start(f32[65664]{0:T(1024)S(1)} %maximum_select_fusion.1), channel_id=1, source_target_pairs={{0,16},{1,17},{2,18},{3,19},{4,20},{5,21},{6,22},{7,23},{8,24},{9,... | collective-permute-start | bytes 787976 | tf_op jit(solution)/shard_map/ppermute | solution.py:138
Sparse Core Ops, SparseCore 0:
  9.5 200.4 all-gather.1

commit v4 on v3

--- a/solution.py
+++ b/solution.py
@@ -96,48 +96,78 @@
     )(ids, counts, kinds, bath_pattern, group_rows, own_rows, energy, coupling_blocks, bath_blocks)
 
 
-def pack_symmetric(gram, half):
-    upper = gram[:half, half:]
-    rows = lax.broadcasted_iota(jnp.int32, (half, half), 0)
-    cols = lax.broadcasted_iota(jnp.int32, (half, half), 1)
-    corner = gram[half:, half:]
-    mixed = jnp.where(rows <= cols, gram[:half, :half], corner)
-    return jnp.concatenate([upper.reshape(-1), mixed.reshape(-1), jnp.diagonal(corner)])
-
-
-def unpack_symmetric(packed, half):
-    area = half * half
-    upper = packed[:area].reshape(half, half)
-    mixed = packed[area:2 * area].reshape(half, half)
-    diag = packed[2 * area:]
-    rows = lax.broadcasted_iota(jnp.int32, (half, half), 0)
-    cols = lax.broadcasted_iota(jnp.int32, (half, half), 1)
-    first = jnp.where(rows <= cols, mixed, mixed.T)
-    corner = jnp.where(rows > cols, mixed, mixed.T)
-    corner = jnp.where(rows == cols, diag[None, :], corner)
-    return jnp.concatenate(
-        [jnp.concatenate([first, upper], axis=1), jnp.concatenate([upper.T, corner], axis=1)], axis=0
-    )
-
-
-def halving_sum(local, axes, count, order):
-    me = lax.axis_index(axes)
-    buf = local
-    stages = []
+def allreduce_kernel(order, cols, x_ref, o_ref, *scratch):
+    stages = len(order)
+    recv_bufs = scratch[:stages]
+    send_sems, recv_sems, work = scratch[stages], scratch[stages + 1], scratch[stages + 2]
+    me = lax.axis_index("row") * cols + lax.axis_index("col")
+
+    def bit(s):
+        return (me // (1 << s)) % 2
+
+    def place(s):
+        other = me + (1 - 2 * bit(s)) * (1 << s)
+        return (other // cols, other % cols)
+
+    barrier = pltpu.get_barrier_semaphore()
     for s in order:
-        bit = (me >> s) & 1
-        half = buf.shape[0] // 2
-        low, high = buf[:half], buf[half:]
-        send = jnp.where(bit == 1, low, high)
-        keep = jnp.where(bit == 1, high, low)
-        pairs = [(i, i ^ (1 << s)) for i in range(count)]
-        buf = keep + lax.ppermute(send, axes, pairs)
-        stages.append((s, bit))
-    for s, bit in reversed(stages):
-        pairs = [(i, i ^ (1 << s)) for i in range(count)]
-        other = lax.ppermute(buf, axes, pairs)
-        buf = jnp.where(bit == 1, jnp.concatenate([other, buf]), jnp.concatenate([buf, other]))
-    return buf
+        pl.semaphore_signal(barrier, inc=1, device_id=place(s), device_id_type=pl.DeviceIdType.MESH)
+    pl.semaphore_wait(barrier, stages)
+
+    base = 0
+    size = x_ref.shape[0]
+    for j, s in enumerate(order):
+        half = size // 2
+        b = bit(s)
+        keep = pl.multiple_of(base + b * half, 8)
+        give = pl.multiple_of(base + (1 - b) * half, 8)
+        src = x_ref if j == 0 else work
+        copy = pltpu.make_async_remote_copy(
+            src_ref=src.at[pl.ds(give, half)],
+            dst_ref=recv_bufs[j],
+            send_sem=send_sems.at[j],
+            recv_sem=recv_sems.at[j],
+            device_id=place(s),
+            device_id_type=pl.DeviceIdType.MESH,
+        )
+        copy.start()
+        copy.wait()
+        work[pl.ds(keep, half)] = src[pl.ds(keep, half)] + recv_bufs[j][...]
+        base, size = keep, half
+    o_ref[pl.ds(base, size)] = work[pl.ds(base, size)]
+    for j in reversed(range(stages)):
+        s = order[j]
+        block = o_ref.at[pl.ds(base, size)]
+        copy = pltpu.make_async_remote_copy(
+            src_ref=block,
+            dst_ref=block,
+            send_sem=send_sems.at[stages + j],
+            recv_sem=recv_sems.at[stages + j],
+            device_id=place(s),
+            device_id_type=pl.DeviceIdType.MESH,
+        )
+        copy.start()
+        copy.wait()
+        base = pl.multiple_of(base - bit(s) * size, 8)
+        size = size * 2
+
+
+def kernel_sum(local, order, cols):
+    lanes = 128
+    flat = local.reshape(-1, lanes)
+    rows = flat.shape[0]
+    scratch = [pltpu.VMEM((rows >> (j + 1), lanes), jnp.float32) for j in range(len(order))]
+    scratch += [pltpu.SemaphoreType.DMA((2 * len(order),)), pltpu.SemaphoreType.DMA((2 * len(order),))]
+    scratch += [pltpu.VMEM(flat.shape, jnp.float32)]
+    total = pl.pallas_call(
+        functools.partial(allreduce_kernel, tuple(order), cols),
+        out_shape=jax.ShapeDtypeStruct(flat.shape, flat.dtype),
+        in_specs=[pl.BlockSpec(memory_space=pltpu.VMEM)],
+        out_specs=pl.BlockSpec(memory_space=pltpu.VMEM),
+        scratch_shapes=scratch,
+        compiler_params=pltpu.CompilerParams(collective_id=0, has_side_effects=True),
+    )(flat)
+    return total.reshape(local.shape)
 
 
 def shards(
@@ -174,8 +204,7 @@
     devices = lax.axis_size("row") * col_count
     stage_bits = devices.bit_length() - 1
     order = [4, 0, 2, 5, 1, 3, 6] if stage_bits == 7 else list(range(stage_bits))
-    packed = halving_sum(pack_symmetric(local_gram, rank_cols), ("row", "col"), devices, order)
-    gram_sum = unpack_symmetric(packed, rank_cols)
+    gram_sum = kernel_sum(local_gram, order, col_count)
     rotation = orthonormal_steps(gram_sum, rank_cols).astype(jnp.bfloat16)
     return jnp.dot(stacked, rotation, preferred_element_type=jnp.float32).astype(jnp.bfloat16)
 

time: 439 us -> 431 us (0.982)
  Pallas kernels: 15.4 us -> 73.9 us
  starting transfers between devices: 32 us -> 0.03 us
  waiting for transfers between devices: 228 us -> 197 us
    pallas_call x0 -> x1, Pallas kernels: none -> 58.8 us  [kernel_sum(): pl.pallas_call(functools.partial(allreduce_kernel, tuple(order), cols), o...]
    ppermute x14 -> x0, starting transfers between devices: 32 us -> none  [the longest x7 22.5 us: halving_sum(): other = lax.ppermute(buf, axes, pairs)]
    ppermute x14 -> x0, waiting for transfers between devices: 31.5 us -> none  [the longest x7 16.7 us: halving_sum(): buf = keep + lax.ppermute(send, axes, pairs)]
  transfers between devices with their start and end apart: 15 -> 1, of which waited for: 15 -> 1; matrix products, arithmetic and copies ran while one was open for 2% -> 1% of each run, Pallas kernels for 0% -> 0%
where the time goes in v4:
time: 431 us; the launch traced here: 430 us
  waiting for transfers between devices  197 us (46%)
  other arithmetic  108 us (25%)
  Pallas kernels  73.9 us (17%)
  matrix products  18.5 us (4%)
  local copies, waits for them, and re-layouts  16 us (4%)
  between operations  13.5 us (3%)
    all_gather x1, waiting for transfers between devices, shards(): gathered = lax.all_gather(density_factor, 'col', axis=0, tiled=True)  197 us
    another operation x12, other arithmetic, sweep(): factor = jnp.linalg.cholesky(inner)  68 us
    pallas_call x1, Pallas kernels, kernel_sum(): pl.pallas_call(functools.partial(allreduce_kernel, tuple(order), cols), o...  58.8 us
    another operation x8, other arithmetic, sweep(): lax.linalg.triangular_solve(factor, image, left_side=False, lower=True, t...  39.5 us
    pallas_call x1, Pallas kernels, stacked_blocks(): pl.pallas_call(functools.partial(step_kernel, slots), grid_spec=grid_spec...  15.1 us
  transfers between devices with their start and end apart: 1, of which 1 were waited for; matrix products, arithmetic and copies ran while one was open for 1% of the time, Pallas kernels for 0%

profile of v4, /device:TPU:1, one launch (start us, length us, event | category | flops | bytes accessed | tf_op | source)
XLA Modules:
  0.0 430.5 jit_solution(17850379504384612376)
XLA Ops:
  6.6 0.7 all-gather.2.cloned.1.call-update
  7.3 4.0 reshape.69.ons_ref
  11.3 0.7 reshape.41.ids_ref
  11.9 0.6 reshape.42.kind_ref
  12.7 0.6 broadcast_clamp_fusion.1
  13.2 196.7 %all-gather.2.cloned.1.call-done = bf16[65536,256]{1,0:T(8,128)(2,1)} async-done(((bf16[4096,256]{1,0:T(8,128)(2,1)}), bf16[65536,256]{1,0:T(8,128)(2,1)}) %all-gather.2.cloned.1.call-update) | async-done | bytes 33554448 | tf_op jit(solution)/shard_map/all_gather | solution.py:193
  210.0 15.1 %shard_map.82 = bf16[8,512,512]{2,1,0:T(8,128)(2,1)} custom-call(s32[64]{0:T(128)} %reshape.41.ids_ref, s32[8]{0:T(128)} %get-tuple-element.56.cnt_ref, s32[64]{0:T(128)} %reshape.42.kind_ref, s32[8]{0:T(128)} %get-tuple-element.55.bath_ref, bf16[128,512,256]{2,1,0:T(8,128)(2,1)} %bitcast.68, bf16[8,512,256]{2,1,0:T(8,128)(2,1)} %bitcast.69, ...), custom_call_target="tpu_custom_call" | custom-call | tf_op jit(solution)/shard_map/pallas_call | solution.py:91
  225.1 5.8 %convolution_bitcast_fusion = f32[512,512]{1,0:T(8,128)S(1)} fusion(bf16[8,512,512]{2,1,0:T(8,128)(2,1)} %shard_map.82), kind=kOutput, calls=%fused_computation.29 | convolution fusion | flops 2147483648 | bytes 5242880 | tf_op jit(solution)/shard_map/dot_general | solution.py:201
  230.9 1.0 reshape.47.x_ref
  231.9 58.8 %shard_map.83 = f32[2048,128]{1,0:T(8,128)} custom-call(f32[2048,128]{1,0:T(8,128)} %reshape.47.x_ref), custom_call_target="tpu_custom_call" | custom-call | tf_op jit(solution)/shard_map/pallas_call | solution.py:162
  290.8 1.4 reshape.48
  292.2 126.7 %while.13 = (s32[]{:T(128)}, f32[512,256]{0,1:T(8,128)S(1)}, f32[512,512]{1,0:T(8,128)S(1)}, s32[]{:T(128)}, s32[]{:T(128)}, /*index=5*/f32[]{:T(128)}, s32[]{:T(128)}) while((s32[]{:T(128)}, f32[512,256]{0,1:T(8,128)S(1)}, f32[512,512]{1,0:T(8,128)S(1)}, s32[]{:T(128)}, s32[]{:T(128)}, /*index=5*/f32[]{:T(128)}, s32[]{:T(128)}) %tuple.52), condition=%wide.region_5.6_spmd, body=%wide.region_0.5_spmd.sunk | while | flops 1561018624 | bytes 9177364 | solution.py:25
  292.4 1.0 fusion.50
  293.4 1.0 fusion.51
  294.4 0.1 copy.16
  294.6 11.7 %cholesky.185 = f32[128,128]{1,0:T(8,128)S(1)} custom-call(f32[128,128]{1,0:T(8,128)S(1)} %cholesky.184), custom_call_target="Cholesky" | custom-call | tf_op jit(solution)/shard_map/while/body/eval_jaxpr/jit(cholesky)/cholesky | solution.py:20
  306.4 9.8 %custom-call.18 = f32[1,128,128]{1,2,0:T(8,128)S(1)} custom-call(f32[1,128,128]{2,1,0:T(8,128)S(1)} %get-tuple-element.116), custom_call_target="InvertDiagBlocksLowerTriangular" | custom-call | tf_op jit(solution)/shard_map/while/body/eval_jaxpr/jit(cholesky)/cholesky | solution.py:20
  316.2 0.2 constant_dynamic-update-slice_fusion.3
  316.4 0.3 convolution_subtract_fusion.4
  316.7 11.7 %cholesky.187 = f32[128,128]{1,0:T(8,128)S(1)} custom-call(f32[128,128]{1,0:T(8,128)S(1)} %convolution_subtract_fusion.4), custom_call_target="Cholesky" | custom-call | tf_op jit(solution)/shard_map/while/body/eval_jaxpr/jit(cholesky)/cholesky | solution.py:20
  328.5 0.7 compare_reduce_fusion.3
  330.5 3.9 while.14
  330.5 0.6 fusion.55
  331.1 1.3 bitcast_dynamic-update-slice_fusion.2
  332.5 0.6 fusion.55
  333.1 1.3 bitcast_dynamic-update-slice_fusion.2
  334.4 19.7 %custom-call.20 = f32[2,128,128]{1,2,0:T(8,128)S(1)} custom-call(f32[2,128,128]{2,1,0:T(8,128)S(1)} %get-tuple-element.124), custom_call_target="InvertDiagBlocksLowerTriangular" | custom-call | tf_op jit(solution)/shard_map/while/body/eval_jaxpr/triangular_solve | solution.py:21
  354.1 0.4 fusion.53
  354.5 0.6 convolution_subtract_fusion.5
  355.1 0.4 fusion.54
  355.6 1.0 fusion.50
  356.6 1.0 fusion.51
  357.9 11.7 %cholesky.185 = f32[128,128]{1,0:T(8,128)S(1)} custom-call(f32[128,128]{1,0:T(8,128)S(1)} %cholesky.184), custom_call_target="Cholesky" | custom-call | tf_op jit(solution)/shard_map/while/body/eval_jaxpr/jit(cholesky)/cholesky | solution.py:20
  369.6 9.8 %custom-call.18 = f32[1,128,128]{1,2,0:T(8,128)S(1)} custom-call(f32[1,128,128]{2,1,0:T(8,128)S(1)} %get-tuple-element.116), custom_call_target="InvertDiagBlocksLowerTriangular" | custom-call | tf_op jit(solution)/shard_map/while/body/eval_jaxpr/jit(cholesky)/cholesky | solution.py:20
  379.5 0.2 constant_dynamic-update-slice_fusion.3
  379.7 0.3 convolution_subtract_fusion.4
  379.9 11.7 %cholesky.187 = f32[128,128]{1,0:T(8,128)S(1)} custom-call(f32[128,128]{1,0:T(8,128)S(1)} %convolution_subtract_fusion.4), custom_call_target="Cholesky" | custom-call | tf_op jit(solution)/shard_map/while/body/eval_jaxpr/jit(cholesky)/cholesky | solution.py:20
  391.7 0.7 compare_reduce_fusion.3
  393.8 3.9 while.14
  393.8 0.6 fusion.55
  394.4 1.3 bitcast_dynamic-update-slice_fusion.2
  395.7 0.6 fusion.55
  396.3 1.3 bitcast_dynamic-update-slice_fusion.2
  397.7 19.7 %custom-call.20 = f32[2,128,128]{1,2,0:T(8,128)S(1)} custom-call(f32[2,128,128]{2,1,0:T(8,128)S(1)} %get-tuple-element.124), custom_call_target="InvertDiagBlocksLowerTriangular" | custom-call | tf_op jit(solution)/shard_map/while/body/eval_jaxpr/triangular_solve | solution.py:21
  417.4 0.4 fusion.53
  417.8 0.6 convolution_subtract_fusion.5
  418.4 0.4 fusion.54
  418.8 4.8 %convolution_convert_fusion = bf16[4096,256]{1,0:T(8,128)(2,1)} fusion(bf16[4096,512]{1,0:T(8,128)(2,1)} %bitcast.67, f32[512,256]{0,1:T(8,128)S(1)} %get-tuple-element.22), kind=kOutput, calls=%fused_computation.28 | convolution fusion | flops 1074921472 | bytes 6815744 | tf_op jit(solution)/shard_map/dot_general | solution.py:209
  (37 shorter events, 0.8 us)
Async XLA Ops:
  6.5 4.7 %copy-start = (s32[8,8]{1,0:T(8,128)S(1)}, s32[8,8]{1,0:T(8,128)}, u32[]{:S(2)}) copy-start(s32[8,8]{1,0:T(8,128)} %param.12) | copy-start | bytes 772
  6.5 5.4 %copy-start.1 = (s32[8,8]{1,0:T(8,128)S(1)}, s32[8,8]{1,0:T(8,128)}, u32[]{:S(2)}) copy-start(s32[8,8]{1,0:T(8,128)} %param.14) | copy-start | bytes 772
  6.5 6.1 %copy-start.3 = (s32[8]{0:T(128)S(1)}, s32[8]{0:T(128)}, u32[]{:S(2)}) copy-start(s32[8]{0:T(128)} %param.13) | copy-start | bytes 100
  6.5 6.1 %copy-start.2 = (s32[8]{0:T(128)S(1)}, s32[8]{0:T(128)}, u32[]{:S(2)}) copy-start(s32[8]{0:T(128)} %param.16) | copy-start | bytes 100
  6.5 203.4 %all-gather.2.cloned.1.call-start = ((), (), s32[]{:S(2)}) async-start(), calls=%async_computation | async-start | bytes 35651584 | tf_op jit(solution)/shard_map/all_gather | solution.py:193
Sparse Core Ops, SparseCore 0:
  9.5 200.4 all-gather.1

commit v5 on v4

--- a/solution.py
+++ b/solution.py
@@ -96,71 +96,93 @@
     )(ids, counts, kinds, bath_pattern, group_rows, own_rows, energy, coupling_blocks, bath_blocks)
 
 
-def allreduce_kernel(order, cols, x_ref, o_ref, *scratch):
-    stages = len(order)
+def allreduce_kernel(fields, cols, x_ref, o_ref, *scratch):
+    stages = len(fields)
     recv_bufs = scratch[:stages]
     send_sems, recv_sems, work = scratch[stages], scratch[stages + 1], scratch[stages + 2]
     me = lax.axis_index("row") * cols + lax.axis_index("col")
 
-    def bit(s):
-        return (me // (1 << s)) % 2
-
-    def place(s):
-        other = me + (1 - 2 * bit(s)) * (1 << s)
+    def field(s, r):
+        return (me // (1 << s)) % r
+
+    def place(s, r, d):
+        other = me + ((field(s, r) + d) % r - field(s, r)) * (1 << s)
         return (other // cols, other % cols)
 
     barrier = pltpu.get_barrier_semaphore()
-    for s in order:
-        pl.semaphore_signal(barrier, inc=1, device_id=place(s), device_id_type=pl.DeviceIdType.MESH)
-    pl.semaphore_wait(barrier, stages)
+    partners = 0
+    for s, r in fields:
+        for d in range(1, r):
+            pl.semaphore_signal(barrier, inc=1, device_id=place(s, r, d), device_id_type=pl.DeviceIdType.MESH)
+            partners += 1
+    pl.semaphore_wait(barrier, partners)
 
     base = 0
     size = x_ref.shape[0]
-    for j, s in enumerate(order):
-        half = size // 2
-        b = bit(s)
-        keep = pl.multiple_of(base + b * half, 8)
-        give = pl.multiple_of(base + (1 - b) * half, 8)
+    slot = 0
+    for j, (s, r) in enumerate(fields):
+        part = size // r
+        f = field(s, r)
         src = x_ref if j == 0 else work
-        copy = pltpu.make_async_remote_copy(
-            src_ref=src.at[pl.ds(give, half)],
-            dst_ref=recv_bufs[j],
-            send_sem=send_sems.at[j],
-            recv_sem=recv_sems.at[j],
-            device_id=place(s),
-            device_id_type=pl.DeviceIdType.MESH,
-        )
-        copy.start()
-        copy.wait()
-        work[pl.ds(keep, half)] = src[pl.ds(keep, half)] + recv_bufs[j][...]
-        base, size = keep, half
+        copies = []
+        for d in range(1, r):
+            give = pl.multiple_of(base + ((f + d) % r) * part, 8)
+            copy = pltpu.make_async_remote_copy(
+                src_ref=src.at[pl.ds(give, part)],
+                dst_ref=recv_bufs[j].at[d - 1],
+                send_sem=send_sems.at[slot],
+                recv_sem=recv_sems.at[slot],
+                device_id=place(s, r, d),
+                device_id_type=pl.DeviceIdType.MESH,
+            )
+            copy.start()
+            copies.append(copy)
+            slot += 1
+        for copy in copies:
+            copy.wait()
+        keep = pl.multiple_of(base + f * part, 8)
+        total = src[pl.ds(keep, part)]
+        for d in range(1, r):
+            total = total + recv_bufs[j][d - 1]
+        work[pl.ds(keep, part)] = total
+        base, size = keep, part
     o_ref[pl.ds(base, size)] = work[pl.ds(base, size)]
     for j in reversed(range(stages)):
-        s = order[j]
+        s, r = fields[j]
         block = o_ref.at[pl.ds(base, size)]
-        copy = pltpu.make_async_remote_copy(
-            src_ref=block,
-            dst_ref=block,
-            send_sem=send_sems.at[stages + j],
-            recv_sem=recv_sems.at[stages + j],
-            device_id=place(s),
-            device_id_type=pl.DeviceIdType.MESH,
-        )
-        copy.start()
-        copy.wait()
-        base = pl.multiple_of(base - bit(s) * size, 8)
-        size = size * 2
-
-
-def kernel_sum(local, order, cols):
+        copies = []
+        for d in range(1, r):
+            copy = pltpu.make_async_remote_copy(
+                src_ref=block,
+                dst_ref=block,
+                send_sem=send_sems.at[slot],
+                recv_sem=recv_sems.at[slot],
+                device_id=place(s, r, d),
+                device_id_type=pl.DeviceIdType.MESH,
+            )
+            copy.start()
+            copies.append(copy)
+            slot += 1
+        for copy in copies:
+            copy.wait()
+        base = pl.multiple_of(base - field(s, r) * size, 8)
+        size = size * r
+
+
+def kernel_sum(local, fields, cols):
     lanes = 128
     flat = local.reshape(-1, lanes)
     rows = flat.shape[0]
-    scratch = [pltpu.VMEM((rows >> (j + 1), lanes), jnp.float32) for j in range(len(order))]
-    scratch += [pltpu.SemaphoreType.DMA((2 * len(order),)), pltpu.SemaphoreType.DMA((2 * len(order),))]
+    scratch = []
+    left = rows
+    for s, r in fields:
+        left //= r
+        scratch.append(pltpu.VMEM((r - 1, left, lanes), jnp.float32))
+    copies = 2 * sum(r - 1 for _, r in fields)
+    scratch += [pltpu.SemaphoreType.DMA((copies,)), pltpu.SemaphoreType.DMA((copies,))]
     scratch += [pltpu.VMEM(flat.shape, jnp.float32)]
     total = pl.pallas_call(
-        functools.partial(allreduce_kernel, tuple(order), cols),
+        functools.partial(allreduce_kernel, tuple(fields), cols),
         out_shape=jax.ShapeDtypeStruct(flat.shape, flat.dtype),
         in_specs=[pl.BlockSpec(memory_space=pltpu.VMEM)],
         out_specs=pl.BlockSpec(memory_space=pltpu.VMEM),
@@ -203,8 +225,11 @@
     )
     devices = lax.axis_size("row") * col_count
     stage_bits = devices.bit_length() - 1
-    order = [4, 0, 2, 5, 1, 3, 6] if stage_bits == 7 else list(range(stage_bits))
-    gram_sum = kernel_sum(local_gram, order, col_count)
+    if stage_bits == 7:
+        fields = [(4, 2), (0, 4), (2, 4), (5, 4)]
+    else:
+        fields = [(s, 2) for s in range(stage_bits)]
+    gram_sum = kernel_sum(local_gram, fields, col_count)
     rotation = orthonormal_steps(gram_sum, rank_cols).astype(jnp.bfloat16)
     return jnp.dot(stacked, rotation, preferred_element_type=jnp.float32).astype(jnp.bfloat16)
 

time: 431 us -> 413 us (0.958)
  Pallas kernels: 73.9 us -> 55.6 us
    pallas_call x1, Pallas kernels: 58.8 us -> 40.3 us  [kernel_sum(): pl.pallas_call(functools.partial(allreduce_kernel, tuple(fields), cols),...]
where the time goes in v5:
time: 413 us; the launch traced here: 412 us
  waiting for transfers between devices  197 us (48%)
  other arithmetic  108 us (26%)
  Pallas kernels  55.6 us (13%)
  matrix products  18.5 us (4%)
  local copies, waits for them, and re-layouts  16 us (4%)
  between operations  13.5 us (3%)
    all_gather x1, waiting for transfers between devices, shards(): gathered = lax.all_gather(density_factor, 'col', axis=0, tiled=True)  197 us
    another operation x12, other arithmetic, sweep(): factor = jnp.linalg.cholesky(inner)  68 us
    pallas_call x1, Pallas kernels, kernel_sum(): pl.pallas_call(functools.partial(allreduce_kernel, tuple(fields), cols),...  40.3 us
    another operation x8, other arithmetic, sweep(): lax.linalg.triangular_solve(factor, image, left_side=False, lower=True, t...  39.5 us
    pallas_call x1, Pallas kernels, stacked_blocks(): pl.pallas_call(functools.partial(step_kernel, slots), grid_spec=grid_spec...  15.3 us
  transfers between devices with their start and end apart: 1, of which 1 were waited for; matrix products, arithmetic and copies ran while one was open for 1% of the time, Pallas kernels for 0%

profile of v5, /device:TPU:1, one launch (start us, length us, event | category | flops | bytes accessed | tf_op | source)
XLA Modules:
  0.0 412.1 jit_solution(6790980541455509033)
XLA Ops:
  6.6 0.7 all-gather.2.cloned.1.call-update
  7.3 4.0 reshape.69.ons_ref
  11.3 0.7 reshape.41.ids_ref
  11.9 0.6 reshape.42.kind_ref
  12.7 0.6 broadcast_clamp_fusion.1
  13.2 196.7 %all-gather.2.cloned.1.call-done = bf16[65536,256]{1,0:T(8,128)(2,1)} async-done(((bf16[4096,256]{1,0:T(8,128)(2,1)}), bf16[65536,256]{1,0:T(8,128)(2,1)}) %all-gather.2.cloned.1.call-update) | async-done | bytes 33554448 | tf_op jit(solution)/shard_map/all_gather | solution.py:215
  210.0 15.3 %shard_map.82 = bf16[8,512,512]{2,1,0:T(8,128)(2,1)} custom-call(s32[64]{0:T(128)} %reshape.41.ids_ref, s32[8]{0:T(128)} %get-tuple-element.56.cnt_ref, s32[64]{0:T(128)} %reshape.42.kind_ref, s32[8]{0:T(128)} %get-tuple-element.55.bath_ref, bf16[128,512,256]{2,1,0:T(8,128)(2,1)} %bitcast.68, bf16[8,512,256]{2,1,0:T(8,128)(2,1)} %bitcast.69, ...), custom_call_target="tpu_custom_call" | custom-call | tf_op jit(solution)/shard_map/pallas_call | solution.py:91
  225.3 5.8 %convolution_bitcast_fusion = f32[512,512]{1,0:T(8,128)S(1)} fusion(bf16[8,512,512]{2,1,0:T(8,128)(2,1)} %shard_map.82), kind=kOutput, calls=%fused_computation.29 | convolution fusion | flops 2147483648 | bytes 5242880 | tf_op jit(solution)/shard_map/dot_general | solution.py:223
  231.1 1.0 reshape.47.x_ref
  232.1 40.3 %shard_map.83 = f32[2048,128]{1,0:T(8,128)} custom-call(f32[2048,128]{1,0:T(8,128)} %reshape.47.x_ref), custom_call_target="tpu_custom_call" | custom-call | tf_op jit(solution)/shard_map/pallas_call | solution.py:184
  272.4 1.4 reshape.48
  273.8 126.7 %while.13 = (s32[]{:T(128)}, f32[512,256]{0,1:T(8,128)S(1)}, f32[512,512]{1,0:T(8,128)S(1)}, s32[]{:T(128)}, s32[]{:T(128)}, /*index=5*/f32[]{:T(128)}, s32[]{:T(128)}) while((s32[]{:T(128)}, f32[512,256]{0,1:T(8,128)S(1)}, f32[512,512]{1,0:T(8,128)S(1)}, s32[]{:T(128)}, s32[]{:T(128)}, /*index=5*/f32[]{:T(128)}, s32[]{:T(128)}) %tuple.52), condition=%wide.region_5.6_spmd, body=%wide.region_0.5_spmd.sunk | while | flops 1561018624 | bytes 9177364 | solution.py:25
  274.0 1.0 fusion.50
  275.0 1.0 fusion.51
  276.1 0.1 copy.16
  276.3 11.7 %cholesky.185 = f32[128,128]{1,0:T(8,128)S(1)} custom-call(f32[128,128]{1,0:T(8,128)S(1)} %cholesky.184), custom_call_target="Cholesky" | custom-call | tf_op jit(solution)/shard_map/while/body/eval_jaxpr/jit(cholesky)/cholesky | solution.py:20
  288.0 9.8 %custom-call.18 = f32[1,128,128]{1,2,0:T(8,128)S(1)} custom-call(f32[1,128,128]{2,1,0:T(8,128)S(1)} %get-tuple-element.116), custom_call_target="InvertDiagBlocksLowerTriangular" | custom-call | tf_op jit(solution)/shard_map/while/body/eval_jaxpr/jit(cholesky)/cholesky | solution.py:20
  297.8 0.2 constant_dynamic-update-slice_fusion.3
  298.1 0.3 convolution_subtract_fusion.4
  298.3 11.7 %cholesky.187 = f32[128,128]{1,0:T(8,128)S(1)} custom-call(f32[128,128]{1,0:T(8,128)S(1)} %convolution_subtract_fusion.4), custom_call_target="Cholesky" | custom-call | tf_op jit(solution)/shard_map/while/body/eval_jaxpr/jit(cholesky)/cholesky | solution.py:20
  310.1 0.7 compare_reduce_fusion.3
  312.1 3.9 while.14
  312.1 0.6 fusion.55
  312.8 1.3 bitcast_dynamic-update-slice_fusion.2
  314.1 0.6 fusion.55
  314.7 1.3 bitcast_dynamic-update-slice_fusion.2
  316.1 19.7 %custom-call.20 = f32[2,128,128]{1,2,0:T(8,128)S(1)} custom-call(f32[2,128,128]{2,1,0:T(8,128)S(1)} %get-tuple-element.124), custom_call_target="InvertDiagBlocksLowerTriangular" | custom-call | tf_op jit(solution)/shard_map/while/body/eval_jaxpr/triangular_solve | solution.py:21
  335.7 0.4 fusion.53
  336.2 0.6 convolution_subtract_fusion.5
  336.8 0.4 fusion.54
  337.2 1.0 fusion.50
  338.3 1.0 fusion.51
  339.5 11.7 %cholesky.185 = f32[128,128]{1,0:T(8,128)S(1)} custom-call(f32[128,128]{1,0:T(8,128)S(1)} %cholesky.184), custom_call_target="Cholesky" | custom-call | tf_op jit(solution)/shard_map/while/body/eval_jaxpr/jit(cholesky)/cholesky | solution.py:20
  351.2 9.8 %custom-call.18 = f32[1,128,128]{1,2,0:T(8,128)S(1)} custom-call(f32[1,128,128]{2,1,0:T(8,128)S(1)} %get-tuple-element.116), custom_call_target="InvertDiagBlocksLowerTriangular" | custom-call | tf_op jit(solution)/shard_map/while/body/eval_jaxpr/jit(cholesky)/cholesky | solution.py:20
  361.1 0.2 constant_dynamic-update-slice_fusion.3
  361.3 0.3 convolution_subtract_fusion.4
  361.6 11.7 %cholesky.187 = f32[128,128]{1,0:T(8,128)S(1)} custom-call(f32[128,128]{1,0:T(8,128)S(1)} %convolution_subtract_fusion.4), custom_call_target="Cholesky" | custom-call | tf_op jit(solution)/shard_map/while/body/eval_jaxpr/jit(cholesky)/cholesky | solution.py:20
  373.3 0.7 compare_reduce_fusion.3
  375.4 3.9 while.14
  375.4 0.6 fusion.55
  376.0 1.3 bitcast_dynamic-update-slice_fusion.2
  377.4 0.6 fusion.55
  378.0 1.3 bitcast_dynamic-update-slice_fusion.2
  379.3 19.7 %custom-call.20 = f32[2,128,128]{1,2,0:T(8,128)S(1)} custom-call(f32[2,128,128]{2,1,0:T(8,128)S(1)} %get-tuple-element.124), custom_call_target="InvertDiagBlocksLowerTriangular" | custom-call | tf_op jit(solution)/shard_map/while/body/eval_jaxpr/triangular_solve | solution.py:21
  399.0 0.4 fusion.53
  399.4 0.6 convolution_subtract_fusion.5
  400.0 0.4 fusion.54
  400.5 4.8 %convolution_convert_fusion = bf16[4096,256]{1,0:T(8,128)(2,1)} fusion(bf16[4096,512]{1,0:T(8,128)(2,1)} %bitcast.67, f32[512,256]{0,1:T(8,128)S(1)} %get-tuple-element.22), kind=kOutput, calls=%fused_computation.28 | convolution fusion | flops 1074921472 | bytes 6815744 | tf_op jit(solution)/shard_map/dot_general | solution.py:234
  (37 shorter events, 0.8 us)
Async XLA Ops:
  6.5 4.7 %copy-start = (s32[8,8]{1,0:T(8,128)S(1)}, s32[8,8]{1,0:T(8,128)}, u32[]{:S(2)}) copy-start(s32[8,8]{1,0:T(8,128)} %param.12) | copy-start | bytes 772
  6.5 5.4 %copy-start.1 = (s32[8,8]{1,0:T(8,128)S(1)}, s32[8,8]{1,0:T(8,128)}, u32[]{:S(2)}) copy-start(s32[8,8]{1,0:T(8,128)} %param.14) | copy-start | bytes 772
  6.5 6.1 %copy-start.3 = (s32[8]{0:T(128)S(1)}, s32[8]{0:T(128)}, u32[]{:S(2)}) copy-start(s32[8]{0:T(128)} %param.13) | copy-start | bytes 100
  6.5 6.1 %copy-start.2 = (s32[8]{0:T(128)S(1)}, s32[8]{0:T(128)}, u32[]{:S(2)}) copy-start(s32[8]{0:T(128)} %param.16) | copy-start | bytes 100
  6.5 203.4 %all-gather.2.cloned.1.call-start = ((), (), s32[]{:S(2)}) async-start(), calls=%async_computation | async-start | bytes 35651584 | tf_op jit(solution)/shard_map/all_gather | solution.py:215
Sparse Core Ops, SparseCore 0:
  9.5 200.4 all-gather.1

commit v6 on v5

--- a/solution.py
+++ b/solution.py
@@ -226,7 +226,7 @@
     devices = lax.axis_size("row") * col_count
     stage_bits = devices.bit_length() - 1
     if stage_bits == 7:
-        fields = [(4, 2), (0, 4), (2, 4), (5, 4)]
+        fields = [(4, 2), (0, 16), (5, 4)]
     else:
         fields = [(s, 2) for s in range(stage_bits)]
     gram_sum = kernel_sum(local_gram, fields, col_count)

time: 413 us -> 409 us (level)
  no operation moved by 1% of the time
where the time goes in v6:
time: 409 us; the launch traced here: 408 us
  waiting for transfers between devices  197 us (48%)
  other arithmetic  108 us (26%)
  Pallas kernels  51.7 us (13%)
  matrix products  18.5 us (5%)
  local copies, waits for them, and re-layouts  16 us (4%)
  between operations  13.5 us (3%)
    all_gather x1, waiting for transfers between devices, shards(): gathered = lax.all_gather(density_factor, 'col', axis=0, tiled=True)  197 us
    another operation x12, other arithmetic, sweep(): factor = jnp.linalg.cholesky(inner)  68 us
    another operation x8, other arithmetic, sweep(): lax.linalg.triangular_solve(factor, image, left_side=False, lower=True, t...  39.5 us
    pallas_call x1, Pallas kernels, kernel_sum(): pl.pallas_call(functools.partial(allreduce_kernel, tuple(fields), cols),...  36.5 us
    pallas_call x1, Pallas kernels, stacked_blocks(): pl.pallas_call(functools.partial(step_kernel, slots), grid_spec=grid_spec...  15.2 us
  transfers between devices with their start and end apart: 1, of which 1 were waited for; matrix products, arithmetic and copies ran while one was open for 1% of the time, Pallas kernels for 0%

profile of v6, /device:TPU:1, one launch (start us, length us, event | category | flops | bytes accessed | tf_op | source)
XLA Modules:
  0.0 408.3 jit_solution(10091404424497275868)
XLA Ops:
  6.6 0.7 all-gather.2.cloned.1.call-update
  7.3 4.0 reshape.69.ons_ref
  11.3 0.7 reshape.41.ids_ref
  11.9 0.6 reshape.42.kind_ref
  12.7 0.6 broadcast_clamp_fusion.1
  13.2 196.7 %all-gather.2.cloned.1.call-done = bf16[65536,256]{1,0:T(8,128)(2,1)} async-done(((bf16[4096,256]{1,0:T(8,128)(2,1)}), bf16[65536,256]{1,0:T(8,128)(2,1)}) %all-gather.2.cloned.1.call-update) | async-done | bytes 33554448 | tf_op jit(solution)/shard_map/all_gather | solution.py:215
  210.0 15.2 %shard_map.82 = bf16[8,512,512]{2,1,0:T(8,128)(2,1)} custom-call(s32[64]{0:T(128)} %reshape.41.ids_ref, s32[8]{0:T(128)} %get-tuple-element.56.cnt_ref, s32[64]{0:T(128)} %reshape.42.kind_ref, s32[8]{0:T(128)} %get-tuple-element.55.bath_ref, bf16[128,512,256]{2,1,0:T(8,128)(2,1)} %bitcast.68, bf16[8,512,256]{2,1,0:T(8,128)(2,1)} %bitcast.69, ...), custom_call_target="tpu_custom_call" | custom-call | tf_op jit(solution)/shard_map/pallas_call | solution.py:91
  225.1 5.8 %convolution_bitcast_fusion = f32[512,512]{1,0:T(8,128)S(1)} fusion(bf16[8,512,512]{2,1,0:T(8,128)(2,1)} %shard_map.82), kind=kOutput, calls=%fused_computation.29 | convolution fusion | flops 2147483648 | bytes 5242880 | tf_op jit(solution)/shard_map/dot_general | solution.py:223
  231.0 1.0 reshape.47.x_ref
  232.0 36.5 %shard_map.83 = f32[2048,128]{1,0:T(8,128)} custom-call(f32[2048,128]{1,0:T(8,128)} %reshape.47.x_ref), custom_call_target="tpu_custom_call" | custom-call | tf_op jit(solution)/shard_map/pallas_call | solution.py:184
  268.5 1.4 reshape.48
  269.9 126.7 %while.13 = (s32[]{:T(128)}, f32[512,256]{0,1:T(8,128)S(1)}, f32[512,512]{1,0:T(8,128)S(1)}, s32[]{:T(128)}, s32[]{:T(128)}, /*index=5*/f32[]{:T(128)}, s32[]{:T(128)}) while((s32[]{:T(128)}, f32[512,256]{0,1:T(8,128)S(1)}, f32[512,512]{1,0:T(8,128)S(1)}, s32[]{:T(128)}, s32[]{:T(128)}, /*index=5*/f32[]{:T(128)}, s32[]{:T(128)}) %tuple.52), condition=%wide.region_5.6_spmd, body=%wide.region_0.5_spmd.sunk | while | flops 1561018624 | bytes 9177364 | solution.py:25
  270.1 1.0 fusion.50
  271.2 1.0 fusion.51
  272.2 0.1 copy.16
  272.4 11.7 %cholesky.185 = f32[128,128]{1,0:T(8,128)S(1)} custom-call(f32[128,128]{1,0:T(8,128)S(1)} %cholesky.184), custom_call_target="Cholesky" | custom-call | tf_op jit(solution)/shard_map/while/body/eval_jaxpr/jit(cholesky)/cholesky | solution.py:20
  284.1 9.8 %custom-call.18 = f32[1,128,128]{1,2,0:T(8,128)S(1)} custom-call(f32[1,128,128]{2,1,0:T(8,128)S(1)} %get-tuple-element.116), custom_call_target="InvertDiagBlocksLowerTriangular" | custom-call | tf_op jit(solution)/shard_map/while/body/eval_jaxpr/jit(cholesky)/cholesky | solution.py:20
  294.0 0.2 constant_dynamic-update-slice_fusion.3
  294.2 0.3 convolution_subtract_fusion.4
  294.5 11.7 %cholesky.187 = f32[128,128]{1,0:T(8,128)S(1)} custom-call(f32[128,128]{1,0:T(8,128)S(1)} %convolution_subtract_fusion.4), custom_call_target="Cholesky" | custom-call | tf_op jit(solution)/shard_map/while/body/eval_jaxpr/jit(cholesky)/cholesky | solution.py:20
  306.2 0.7 compare_reduce_fusion.3
  308.3 3.9 while.14
  308.3 0.6 fusion.55
  308.9 1.3 bitcast_dynamic-update-slice_fusion.2
  310.3 0.6 fusion.55
  310.9 1.3 bitcast_dynamic-update-slice_fusion.2
  312.2 19.7 %custom-call.20 = f32[2,128,128]{1,2,0:T(8,128)S(1)} custom-call(f32[2,128,128]{2,1,0:T(8,128)S(1)} %get-tuple-element.124), custom_call_target="InvertDiagBlocksLowerTriangular" | custom-call | tf_op jit(solution)/shard_map/while/body/eval_jaxpr/triangular_solve | solution.py:21
  331.9 0.4 fusion.53
  332.3 0.6 convolution_subtract_fusion.5
  332.9 0.4 fusion.54
  333.4 1.0 fusion.50
  334.4 1.0 fusion.51
  335.6 11.7 %cholesky.185 = f32[128,128]{1,0:T(8,128)S(1)} custom-call(f32[128,128]{1,0:T(8,128)S(1)} %cholesky.184), custom_call_target="Cholesky" | custom-call | tf_op jit(solution)/shard_map/while/body/eval_jaxpr/jit(cholesky)/cholesky | solution.py:20
  347.4 9.8 %custom-call.18 = f32[1,128,128]{1,2,0:T(8,128)S(1)} custom-call(f32[1,128,128]{2,1,0:T(8,128)S(1)} %get-tuple-element.116), custom_call_target="InvertDiagBlocksLowerTriangular" | custom-call | tf_op jit(solution)/shard_map/while/body/eval_jaxpr/jit(cholesky)/cholesky | solution.py:20
  357.2 0.2 constant_dynamic-update-slice_fusion.3
  357.5 0.3 convolution_subtract_fusion.4
  357.7 11.7 %cholesky.187 = f32[128,128]{1,0:T(8,128)S(1)} custom-call(f32[128,128]{1,0:T(8,128)S(1)} %convolution_subtract_fusion.4), custom_call_target="Cholesky" | custom-call | tf_op jit(solution)/shard_map/while/body/eval_jaxpr/jit(cholesky)/cholesky | solution.py:20
  369.5 0.7 compare_reduce_fusion.3
  371.5 3.9 while.14
  371.5 0.6 fusion.55
  372.2 1.3 bitcast_dynamic-update-slice_fusion.2
  373.5 0.6 fusion.55
  374.1 1.3 bitcast_dynamic-update-slice_fusion.2
  375.5 19.7 %custom-call.20 = f32[2,128,128]{1,2,0:T(8,128)S(1)} custom-call(f32[2,128,128]{2,1,0:T(8,128)S(1)} %get-tuple-element.124), custom_call_target="InvertDiagBlocksLowerTriangular" | custom-call | tf_op jit(solution)/shard_map/while/body/eval_jaxpr/triangular_solve | solution.py:21
  395.1 0.4 fusion.53
  395.6 0.6 convolution_subtract_fusion.5
  396.2 0.4 fusion.54
  396.6 4.8 %convolution_convert_fusion = bf16[4096,256]{1,0:T(8,128)(2,1)} fusion(bf16[4096,512]{1,0:T(8,128)(2,1)} %bitcast.67, f32[512,256]{0,1:T(8,128)S(1)} %get-tuple-element.22), kind=kOutput, calls=%fused_computation.28 | convolution fusion | flops 1074921472 | bytes 6815744 | tf_op jit(solution)/shard_map/dot_general | solution.py:234
  (37 shorter events, 0.8 us)
Async XLA Ops:
  6.5 4.7 %copy-start = (s32[8,8]{1,0:T(8,128)S(1)}, s32[8,8]{1,0:T(8,128)}, u32[]{:S(2)}) copy-start(s32[8,8]{1,0:T(8,128)} %param.12) | copy-start | bytes 772
  6.5 5.4 %copy-start.1 = (s32[8,8]{1,0:T(8,128)S(1)}, s32[8,8]{1,0:T(8,128)}, u32[]{:S(2)}) copy-start(s32[8,8]{1,0:T(8,128)} %param.14) | copy-start | bytes 772
  6.5 6.1 %copy-start.3 = (s32[8]{0:T(128)S(1)}, s32[8]{0:T(128)}, u32[]{:S(2)}) copy-start(s32[8]{0:T(128)} %param.13) | copy-start | bytes 100
  6.5 6.1 %copy-start.2 = (s32[8]{0:T(128)S(1)}, s32[8]{0:T(128)}, u32[]{:S(2)}) copy-start(s32[8]{0:T(128)} %param.16) | copy-start | bytes 100
  6.5 203.4 %all-gather.2.cloned.1.call-start = ((), (), s32[]{:S(2)}) async-start(), calls=%async_computation | async-start | bytes 35651584 | tf_op jit(solution)/shard_map/all_gather | solution.py:215
Sparse Core Ops, SparseCore 0:
  9.5 200.4 all-gather.1

commit v7 on v6

--- a/solution.py
+++ b/solution.py
@@ -226,7 +226,7 @@
     devices = lax.axis_size("row") * col_count
     stage_bits = devices.bit_length() - 1
     if stage_bits == 7:
-        fields = [(4, 2), (0, 16), (5, 4)]
+        fields = [(0, 16), (4, 8)]
     else:
         fields = [(s, 2) for s in range(stage_bits)]
     gram_sum = kernel_sum(local_gram, fields, col_count)

time: 409 us -> 418 us (1.022)
  Pallas kernels: 51.7 us -> 60.9 us
    pallas_call x1, Pallas kernels: 36.5 us -> 45.4 us  [kernel_sum(): pl.pallas_call(functools.partial(allreduce_kernel, tuple(fields), cols),...]
where the time goes in v7:
time: 418 us; the launch traced here: 417 us
  waiting for transfers between devices  197 us (47%)
  other arithmetic  108 us (26%)
  Pallas kernels  60.9 us (15%)
  matrix products  18.5 us (4%)
  local copies, waits for them, and re-layouts  16 us (4%)
  between operations  13.5 us (3%)
    all_gather x1, waiting for transfers between devices, shards(): gathered = lax.all_gather(density_factor, 'col', axis=0, tiled=True)  197 us
    another operation x12, other arithmetic, sweep(): factor = jnp.linalg.cholesky(inner)  68 us
    pallas_call x1, Pallas kernels, kernel_sum(): pl.pallas_call(functools.partial(allreduce_kernel, tuple(fields), cols),...  45.4 us
    another operation x8, other arithmetic, sweep(): lax.linalg.triangular_solve(factor, image, left_side=False, lower=True, t...  39.5 us
    pallas_call x1, Pallas kernels, stacked_blocks(): pl.pallas_call(functools.partial(step_kernel, slots), grid_spec=grid_spec...  15.5 us
  transfers between devices with their start and end apart: 1, of which 1 were waited for; matrix products, arithmetic and copies ran while one was open for 1% of the time, Pallas kernels for 0%

profile of v7, /device:TPU:1, one launch (start us, length us, event | category | flops | bytes accessed | tf_op | source)
XLA Modules:
  0.0 417.5 jit_solution(10936757019882776369)
XLA Ops:
  6.6 0.7 all-gather.2.cloned.1.call-update
  7.3 4.0 reshape.69.ons_ref
  11.3 0.7 reshape.41.ids_ref
  11.9 0.6 reshape.42.kind_ref
  12.7 0.6 broadcast_clamp_fusion.1
  13.2 196.7 %all-gather.2.cloned.1.call-done = bf16[65536,256]{1,0:T(8,128)(2,1)} async-done(((bf16[4096,256]{1,0:T(8,128)(2,1)}), bf16[65536,256]{1,0:T(8,128)(2,1)}) %all-gather.2.cloned.1.call-update) | async-done | bytes 33554448 | tf_op jit(solution)/shard_map/all_gather | solution.py:215
  210.0 15.5 %shard_map.82 = bf16[8,512,512]{2,1,0:T(8,128)(2,1)} custom-call(s32[64]{0:T(128)} %reshape.41.ids_ref, s32[8]{0:T(128)} %get-tuple-element.56.cnt_ref, s32[64]{0:T(128)} %reshape.42.kind_ref, s32[8]{0:T(128)} %get-tuple-element.55.bath_ref, bf16[128,512,256]{2,1,0:T(8,128)(2,1)} %bitcast.68, bf16[8,512,256]{2,1,0:T(8,128)(2,1)} %bitcast.69, ...), custom_call_target="tpu_custom_call" | custom-call | tf_op jit(solution)/shard_map/pallas_call | solution.py:91
  225.5 5.8 %convolution_bitcast_fusion = f32[512,512]{1,0:T(8,128)S(1)} fusion(bf16[8,512,512]{2,1,0:T(8,128)(2,1)} %shard_map.82), kind=kOutput, calls=%fused_computation.29 | convolution fusion | flops 2147483648 | bytes 5242880 | tf_op jit(solution)/shard_map/dot_general | solution.py:223
  231.3 1.0 reshape.47.x_ref
  232.3 45.4 %shard_map.83 = f32[2048,128]{1,0:T(8,128)} custom-call(f32[2048,128]{1,0:T(8,128)} %reshape.47.x_ref), custom_call_target="tpu_custom_call" | custom-call | tf_op jit(solution)/shard_map/pallas_call | solution.py:184
  277.7 1.4 reshape.48
  279.2 126.7 %while.13 = (s32[]{:T(128)}, f32[512,256]{0,1:T(8,128)S(1)}, f32[512,512]{1,0:T(8,128)S(1)}, s32[]{:T(128)}, s32[]{:T(128)}, /*index=5*/f32[]{:T(128)}, s32[]{:T(128)}) while((s32[]{:T(128)}, f32[512,256]{0,1:T(8,128)S(1)}, f32[512,512]{1,0:T(8,128)S(1)}, s32[]{:T(128)}, s32[]{:T(128)}, /*index=5*/f32[]{:T(128)}, s32[]{:T(128)}) %tuple.52), condition=%wide.region_5.6_spmd, body=%wide.region_0.5_spmd.sunk | while | flops 1561018624 | bytes 9177364 | solution.py:25
  279.3 1.0 fusion.50
  280.4 1.0 fusion.51
  281.4 0.1 copy.16
  281.6 11.7 %cholesky.185 = f32[128,128]{1,0:T(8,128)S(1)} custom-call(f32[128,128]{1,0:T(8,128)S(1)} %cholesky.184), custom_call_target="Cholesky" | custom-call | tf_op jit(solution)/shard_map/while/body/eval_jaxpr/jit(cholesky)/cholesky | solution.py:20
  293.3 9.8 %custom-call.18 = f32[1,128,128]{1,2,0:T(8,128)S(1)} custom-call(f32[1,128,128]{2,1,0:T(8,128)S(1)} %get-tuple-element.116), custom_call_target="InvertDiagBlocksLowerTriangular" | custom-call | tf_op jit(solution)/shard_map/while/body/eval_jaxpr/jit(cholesky)/cholesky | solution.py:20
  303.2 0.2 constant_dynamic-update-slice_fusion.3
  303.4 0.3 convolution_subtract_fusion.4
  303.7 11.7 %cholesky.187 = f32[128,128]{1,0:T(8,128)S(1)} custom-call(f32[128,128]{1,0:T(8,128)S(1)} %convolution_subtract_fusion.4), custom_call_target="Cholesky" | custom-call | tf_op jit(solution)/shard_map/while/body/eval_jaxpr/jit(cholesky)/cholesky | solution.py:20
  315.4 0.7 compare_reduce_fusion.3
  317.5 3.9 while.14
  317.5 0.6 fusion.55
  318.1 1.3 bitcast_dynamic-update-slice_fusion.2
  319.5 0.6 fusion.55
  320.1 1.3 bitcast_dynamic-update-slice_fusion.2
  321.4 19.7 %custom-call.20 = f32[2,128,128]{1,2,0:T(8,128)S(1)} custom-call(f32[2,128,128]{2,1,0:T(8,128)S(1)} %get-tuple-element.124), custom_call_target="InvertDiagBlocksLowerTriangular" | custom-call | tf_op jit(solution)/shard_map/while/body/eval_jaxpr/triangular_solve | solution.py:21
  341.1 0.4 fusion.53
  341.5 0.6 convolution_subtract_fusion.5
  342.1 0.4 fusion.54
  342.6 1.0 fusion.50
  343.6 1.0 fusion.51
  344.8 11.7 %cholesky.185 = f32[128,128]{1,0:T(8,128)S(1)} custom-call(f32[128,128]{1,0:T(8,128)S(1)} %cholesky.184), custom_call_target="Cholesky" | custom-call | tf_op jit(solution)/shard_map/while/body/eval_jaxpr/jit(cholesky)/cholesky | solution.py:20
  356.6 9.8 %custom-call.18 = f32[1,128,128]{1,2,0:T(8,128)S(1)} custom-call(f32[1,128,128]{2,1,0:T(8,128)S(1)} %get-tuple-element.116), custom_call_target="InvertDiagBlocksLowerTriangular" | custom-call | tf_op jit(solution)/shard_map/while/body/eval_jaxpr/jit(cholesky)/cholesky | solution.py:20
  366.4 0.2 constant_dynamic-update-slice_fusion.3
  366.6 0.3 convolution_subtract_fusion.4
  366.9 11.7 %cholesky.187 = f32[128,128]{1,0:T(8,128)S(1)} custom-call(f32[128,128]{1,0:T(8,128)S(1)} %convolution_subtract_fusion.4), custom_call_target="Cholesky" | custom-call | tf_op jit(solution)/shard_map/while/body/eval_jaxpr/jit(cholesky)/cholesky | solution.py:20
  378.7 0.7 compare_reduce_fusion.3
  380.7 3.9 while.14
  380.7 0.6 fusion.55
  381.4 1.3 bitcast_dynamic-update-slice_fusion.2
  382.7 0.6 fusion.55
  383.3 1.3 bitcast_dynamic-update-slice_fusion.2
  384.6 19.7 %custom-call.20 = f32[2,128,128]{1,2,0:T(8,128)S(1)} custom-call(f32[2,128,128]{2,1,0:T(8,128)S(1)} %get-tuple-element.124), custom_call_target="InvertDiagBlocksLowerTriangular" | custom-call | tf_op jit(solution)/shard_map/while/body/eval_jaxpr/triangular_solve | solution.py:21
  404.3 0.4 fusion.53
  404.8 0.6 convolution_subtract_fusion.5
  405.4 0.4 fusion.54
  405.8 4.8 %convolution_convert_fusion = bf16[4096,256]{1,0:T(8,128)(2,1)} fusion(bf16[4096,512]{1,0:T(8,128)(2,1)} %bitcast.67, f32[512,256]{0,1:T(8,128)S(1)} %get-tuple-element.22), kind=kOutput, calls=%fused_computation.28 | convolution fusion | flops 1074921472 | bytes 6815744 | tf_op jit(solution)/shard_map/dot_general | solution.py:234
  (37 shorter events, 0.8 us)
Async XLA Ops:
  6.5 4.7 %copy-start = (s32[8,8]{1,0:T(8,128)S(1)}, s32[8,8]{1,0:T(8,128)}, u32[]{:S(2)}) copy-start(s32[8,8]{1,0:T(8,128)} %param.12) | copy-start | bytes 772
  6.5 5.4 %copy-start.1 = (s32[8,8]{1,0:T(8,128)S(1)}, s32[8,8]{1,0:T(8,128)}, u32[]{:S(2)}) copy-start(s32[8,8]{1,0:T(8,128)} %param.14) | copy-start | bytes 772
  6.5 6.1 %copy-start.3 = (s32[8]{0:T(128)S(1)}, s32[8]{0:T(128)}, u32[]{:S(2)}) copy-start(s32[8]{0:T(128)} %param.13) | copy-start | bytes 100
  6.5 6.1 %copy-start.2 = (s32[8]{0:T(128)S(1)}, s32[8]{0:T(128)}, u32[]{:S(2)}) copy-start(s32[8]{0:T(128)} %param.16) | copy-start | bytes 100
  6.5 203.4 %all-gather.2.cloned.1.call-start = ((), (), s32[]{:S(2)}) async-start(), calls=%async_computation | async-start | bytes 35651584 | tf_op jit(solution)/shard_map/all_gather | solution.py:215
Sparse Core Ops, SparseCore 0:
  9.5 200.4 all-gather.1

commit v8 on v6

--- a/solution.py
+++ b/solution.py
@@ -26,7 +26,7 @@
 
 
 def step_kernel(slots, ids_ref, cnt_ref, kind_ref, bath_ref,
-                group_hbm, own_ref, ons_ref, cpl_ref, bth_ref, out_ref, buf, sems, acc):
+                group_hbm, own_ref, ons_ref, cpl_ref, bth_ref, out_ref, gram_ref, buf, sems, acc):
     b = pl.program_id(0)
     last = pl.num_programs(0) - 1
     rank_cols = own_ref.shape[2]
@@ -65,6 +65,18 @@
     out_ref[0, :, :rank_cols] = moved.astype(out_ref.dtype)
     bathed = jnp.dot(bth_ref[0], own, preferred_element_type=jnp.float32)
     out_ref[0, :, rank_cols:] = bathed.astype(out_ref.dtype)
+    stacked = out_ref[0]
+    part = lax.dot_general(
+        stacked, stacked, (((0,), (0,)), ((), ())), preferred_element_type=jnp.float32
+    )
+
+    @pl.when(b == 0)
+    def _():
+        gram_ref[...] = part
+
+    @pl.when(b > 0)
+    def _():
+        gram_ref[...] += part
 
 
 def stacked_blocks(group_rows, own_rows, energy, ids, counts, kinds, bath_pattern, coupling_blocks, bath_blocks):
@@ -81,7 +93,10 @@
             pl.BlockSpec((kinds_n, block_rows, block_rows), lambda b, *_: (0, 0, 0)),
             pl.BlockSpec((1, block_rows, block_rows), lambda b, i, c, t, bp: (bp[b], 0, 0)),
         ],
-        out_specs=pl.BlockSpec((1, block_rows, 2 * rank_cols), lambda b, *_: (b, 0, 0)),
+        out_specs=[
+            pl.BlockSpec((1, block_rows, 2 * rank_cols), lambda b, *_: (b, 0, 0)),
+            pl.BlockSpec((2 * rank_cols, 2 * rank_cols), lambda b, *_: (0, 0)),
+        ],
         scratch_shapes=[
             pltpu.VMEM((2, slots, block_rows, rank_cols), group_rows.dtype),
             pltpu.SemaphoreType.DMA((2, slots)),
@@ -91,7 +106,10 @@
     return pl.pallas_call(
         functools.partial(step_kernel, slots),
         grid_spec=grid_spec,
-        out_shape=jax.ShapeDtypeStruct((blocks, block_rows, 2 * rank_cols), jnp.bfloat16),
+        out_shape=[
+            jax.ShapeDtypeStruct((blocks, block_rows, 2 * rank_cols), jnp.bfloat16),
+            jax.ShapeDtypeStruct((2 * rank_cols, 2 * rank_cols), jnp.float32),
+        ],
         compiler_params=pltpu.CompilerParams(dimension_semantics=("arbitrary",)),
     )(ids, counts, kinds, bath_pattern, group_rows, own_rows, energy, coupling_blocks, bath_blocks)
 
@@ -216,13 +234,11 @@
     group_rows = gathered.reshape(group_blocks, block_rows, rank_cols)
     own_rows = density_factor.reshape(blocks, block_rows, rank_cols)
     energy = onsite.reshape(blocks, block_rows, 1)
-    stacked = stacked_blocks(
+    stacked, local_gram = stacked_blocks(
         group_rows, own_rows, energy, in_group.reshape(-1), counts, kinds.reshape(-1), bath_kind,
         coupling_blocks, bath_blocks,
-    ).reshape(blocks * block_rows, 2 * rank_cols)
-    local_gram = lax.dot_general(
-        stacked, stacked, (((0,), (0,)), ((), ())), preferred_element_type=jnp.float32
-    )
+    )
+    stacked = stacked.reshape(blocks * block_rows, 2 * rank_cols)
     devices = lax.axis_size("row") * col_count
     stage_bits = devices.bit_length() - 1
     if stage_bits == 7:

time: 409 us -> 412 us (level)
  Pallas kernels: 51.7 us -> 59 us
  matrix products: 18.5 us -> 12.7 us
    pallas_call x1, Pallas kernels: 15.2 us -> 24.2 us  [stacked_blocks(): pl.pallas_call(functools.partial(step_kernel, slots), grid_spec=grid_spec...]
    dot_general x1 -> x0, matrix products: 5.81 us -> none  [shards(): lax.dot_general(stacked, stacked, (((0,), (0,)), ((), ())), preferred_ele...]
where the time goes in v8:
time: 412 us
  waiting for transfers between devices  197 us (48%)
  other arithmetic  108 us (26%)
  Pallas kernels  59 us (14%)
  local copies, waits for them, and re-layouts  17.6 us (4%)
  between operations  13.5 us (3%)
  matrix products  12.7 us (3%)
    all_gather x1, waiting for transfers between devices, shards(): gathered = lax.all_gather(density_factor, 'col', axis=0, tiled=True)  197 us
    another operation x12, other arithmetic, sweep(): factor = jnp.linalg.cholesky(inner)  68 us
    another operation x8, other arithmetic, sweep(): lax.linalg.triangular_solve(factor, image, left_side=False, lower=True, t...  39.5 us
    pallas_call x1, Pallas kernels, kernel_sum(): pl.pallas_call(functools.partial(allreduce_kernel, tuple(fields), cols),...  34.8 us
    pallas_call x1, Pallas kernels, stacked_blocks(): pl.pallas_call(functools.partial(step_kernel, slots), grid_spec=grid_spec...  24.2 us
  transfers between devices with their start and end apart: 1, of which 1 were waited for; matrix products, arithmetic and copies ran while one was open for 1% of the time, Pallas kernels for 0%

profile of v8, /device:TPU:1, one launch (start us, length us, event | category | flops | bytes accessed | tf_op | source)
XLA Modules:
  0.0 411.6 jit_solution(2925307833850616624)
XLA Ops:
  6.6 0.7 all-gather.2.cloned.1.call-update
  7.3 4.0 reshape.68.ons_ref
  11.3 0.6 reshape.41.ids_ref
  11.9 0.7 reshape.42.kind_ref
  12.7 0.6 broadcast_clamp_fusion.1
  13.3 196.7 %all-gather.2.cloned.1.call-done = bf16[65536,256]{1,0:T(8,128)(2,1)} async-done(((bf16[4096,256]{1,0:T(8,128)(2,1)}), bf16[65536,256]{1,0:T(8,128)(2,1)}) %all-gather.2.cloned.1.call-update) | async-done | bytes 33554448 | tf_op jit(solution)/shard_map/all_gather | solution.py:233
  210.0 24.2 %shard_map.82 = (bf16[8,512,512]{2,1,0:T(8,128)(2,1)}, f32[512,512]{1,0:T(8,128)}) custom-call(s32[64]{0:T(128)} %reshape.41.ids_ref, s32[8]{0:T(128)} %get-tuple-element.60.cnt_ref, s32[64]{0:T(128)} %reshape.42.kind_ref, s32[8]{0:T(128)} %get-tuple-element.59.bath_ref, bf16[128,512,256]{2,1,0:T(8,128)(2,1)} %bitcast.63, bf16[8,512,256]{2,1,0:T(8,128)(2,1)} %bitcast.64, ...), custom_call_target="tpu_custom_call" | custom-call | tf_op jit(solution)/shard_map/pallas_call | solution.py:106
  234.2 2.3 reshape.47.x_ref
  236.4 34.8 %shard_map.83 = f32[2048,128]{1,0:T(8,128)} custom-call(f32[2048,128]{1,0:T(8,128)} %reshape.47.x_ref), custom_call_target="tpu_custom_call" | custom-call | tf_op jit(solution)/shard_map/pallas_call | solution.py:202
  271.3 1.4 reshape.48
  272.7 127.3 %while.13 = (s32[]{:T(128)}, f32[512,256]{0,1:T(8,128)S(1)}, f32[512,512]{1,0:T(8,128)S(1)}, s32[]{:T(128)}, s32[]{:T(128)}, /*index=5*/f32[]{:T(128)}, s32[]{:T(128)}) while((s32[]{:T(128)}, f32[512,256]{0,1:T(8,128)S(1)}, f32[512,512]{1,0:T(8,128)S(1)}, s32[]{:T(128)}, s32[]{:T(128)}, /*index=5*/f32[]{:T(128)}, s32[]{:T(128)}) %tuple.52), condition=%wide.region_5.6_spmd, body=%wide.region_0.5_spmd.sunk | while | flops 1561018624 | bytes 9177364 | solution.py:25
  272.9 1.0 fusion.48
  273.9 1.0 fusion.49
  274.9 0.1 copy.13
  275.1 11.7 %cholesky.185 = f32[128,128]{1,0:T(8,128)S(1)} custom-call(f32[128,128]{1,0:T(8,128)S(1)} %cholesky.184), custom_call_target="Cholesky" | custom-call | tf_op jit(solution)/shard_map/while/body/eval_jaxpr/jit(cholesky)/cholesky | solution.py:20
  286.9 9.8 %custom-call.18 = f32[1,128,128]{1,2,0:T(8,128)S(1)} custom-call(f32[1,128,128]{2,1,0:T(8,128)S(1)} %get-tuple-element.120), custom_call_target="InvertDiagBlocksLowerTriangular" | custom-call | tf_op jit(solution)/shard_map/while/body/eval_jaxpr/jit(cholesky)/cholesky | solution.py:20
  296.7 0.2 constant_dynamic-update-slice_fusion.3
  296.9 0.3 convolution_subtract_fusion.4
  297.2 11.7 %cholesky.187 = f32[128,128]{1,0:T(8,128)S(1)} custom-call(f32[128,128]{1,0:T(8,128)S(1)} %convolution_subtract_fusion.4), custom_call_target="Cholesky" | custom-call | tf_op jit(solution)/shard_map/while/body/eval_jaxpr/jit(cholesky)/cholesky | solution.py:20
  309.0 0.7 compare_reduce_fusion.3
  311.1 4.1 while.14
  311.1 0.6 fusion.53
  311.8 1.4 bitcast_dynamic-update-slice_fusion.2
  313.2 0.6 fusion.53
  313.8 1.4 bitcast_dynamic-update-slice_fusion.2
  315.2 19.7 %custom-call.20 = f32[2,128,128]{1,2,0:T(8,128)S(1)} custom-call(f32[2,128,128]{2,1,0:T(8,128)S(1)} %get-tuple-element.128), custom_call_target="InvertDiagBlocksLowerTriangular" | custom-call | tf_op jit(solution)/shard_map/while/body/eval_jaxpr/triangular_solve | solution.py:21
  334.9 0.4 fusion.51
  335.3 0.6 convolution_subtract_fusion.5
  335.9 0.4 fusion.52
  336.4 1.0 fusion.48
  337.5 1.0 fusion.49
  338.5 0.1 copy.13
  338.7 11.7 %cholesky.185 = f32[128,128]{1,0:T(8,128)S(1)} custom-call(f32[128,128]{1,0:T(8,128)S(1)} %cholesky.184), custom_call_target="Cholesky" | custom-call | tf_op jit(solution)/shard_map/while/body/eval_jaxpr/jit(cholesky)/cholesky | solution.py:20
  350.4 9.8 %custom-call.18 = f32[1,128,128]{1,2,0:T(8,128)S(1)} custom-call(f32[1,128,128]{2,1,0:T(8,128)S(1)} %get-tuple-element.120), custom_call_target="InvertDiagBlocksLowerTriangular" | custom-call | tf_op jit(solution)/shard_map/while/body/eval_jaxpr/jit(cholesky)/cholesky | solution.py:20
  360.3 0.2 constant_dynamic-update-slice_fusion.3
  360.5 0.3 convolution_subtract_fusion.4
  360.8 11.7 %cholesky.187 = f32[128,128]{1,0:T(8,128)S(1)} custom-call(f32[128,128]{1,0:T(8,128)S(1)} %convolution_subtract_fusion.4), custom_call_target="Cholesky" | custom-call | tf_op jit(solution)/shard_map/while/body/eval_jaxpr/jit(cholesky)/cholesky | solution.py:20
  372.5 0.7 compare_reduce_fusion.3
  374.7 4.1 while.14
  374.7 0.6 fusion.53
  375.3 1.4 bitcast_dynamic-update-slice_fusion.2
  376.7 0.6 fusion.53
  377.4 1.4 bitcast_dynamic-update-slice_fusion.2
  378.8 19.7 %custom-call.20 = f32[2,128,128]{1,2,0:T(8,128)S(1)} custom-call(f32[2,128,128]{2,1,0:T(8,128)S(1)} %get-tuple-element.128), custom_call_target="InvertDiagBlocksLowerTriangular" | custom-call | tf_op jit(solution)/shard_map/while/body/eval_jaxpr/triangular_solve | solution.py:21
  398.5 0.4 fusion.51
  398.9 0.6 convolution_subtract_fusion.5
  399.5 0.4 fusion.52
  400.0 4.8 %convolution_convert_fusion = bf16[4096,256]{1,0:T(8,128)(2,1)} fusion(bf16[4096,512]{1,0:T(8,128)(2,1)} %bitcast.65, f32[512,256]{0,1:T(8,128)S(1)} %get-tuple-element.26), kind=kOutput, calls=%fused_computation.28 | convolution fusion | flops 1074921472 | bytes 6815744 | tf_op jit(solution)/shard_map/dot_general | solution.py:250
  (36 shorter events, 0.7 us)
Async XLA Ops:
  6.5 4.7 %copy-start = (s32[8,8]{1,0:T(8,128)S(1)}, s32[8,8]{1,0:T(8,128)}, u32[]{:S(2)}) copy-start(s32[8,8]{1,0:T(8,128)} %param.12) | copy-start | bytes 772
  6.5 5.4 %copy-start.1 = (s32[8,8]{1,0:T(8,128)S(1)}, s32[8,8]{1,0:T(8,128)}, u32[]{:S(2)}) copy-start(s32[8,8]{1,0:T(8,128)} %param.14) | copy-start | bytes 772
  6.5 6.1 %copy-start.3 = (s32[8]{0:T(128)S(1)}, s32[8]{0:T(128)}, u32[]{:S(2)}) copy-start(s32[8]{0:T(128)} %param.13) | copy-start | bytes 100
  6.5 6.1 %copy-start.2 = (s32[8]{0:T(128)S(1)}, s32[8]{0:T(128)}, u32[]{:S(2)}) copy-start(s32[8]{0:T(128)} %param.16) | copy-start | bytes 100
  6.5 203.4 %all-gather.2.cloned.1.call-start = ((), (), s32[]{:S(2)}) async-start(), calls=%async_computation | async-start | bytes 35651584 | tf_op jit(solution)/shard_map/all_gather | solution.py:233
Sparse Core Ops, SparseCore 0:
  9.5 200.4 all-gather.1

commit v9 on v6

--- a/solution.py
+++ b/solution.py
@@ -25,8 +25,8 @@
     return lax.fori_loop(0, SWEEPS, sweep, jnp.eye(2 * rank_cols, rank_cols, dtype=jnp.float32))
 
 
-def step_kernel(slots, ids_ref, cnt_ref, kind_ref, bath_ref,
-                group_hbm, own_ref, ons_ref, cpl_ref, bth_ref, out_ref, buf, sems, acc):
+def step_kernel(slots, ids_ref, cnt_ref, kind_ref,
+                group_hbm, own_ref, ons_ref, cpl_ref, out_ref, buf, sems, acc):
     b = pl.program_id(0)
     last = pl.num_programs(0) - 1
     rank_cols = own_ref.shape[2]
@@ -62,26 +62,23 @@
     own = own_ref[0]
     wide = own.astype(jnp.float32)
     moved = wide - time_step * (ons_ref[0] * wide + coupled)
-    out_ref[0, :, :rank_cols] = moved.astype(out_ref.dtype)
-    bathed = jnp.dot(bth_ref[0], own, preferred_element_type=jnp.float32)
-    out_ref[0, :, rank_cols:] = bathed.astype(out_ref.dtype)
-
-
-def stacked_blocks(group_rows, own_rows, energy, ids, counts, kinds, bath_pattern, coupling_blocks, bath_blocks):
+    out_ref[0] = moved.astype(out_ref.dtype)
+
+
+def moved_blocks(group_rows, own_rows, energy, ids, counts, kinds, coupling_blocks):
     blocks, block_rows, rank_cols = own_rows.shape
     slots = ids.shape[0] // blocks
     kinds_n = coupling_blocks.shape[0]
     grid_spec = pltpu.PrefetchScalarGridSpec(
-        num_scalar_prefetch=4,
+        num_scalar_prefetch=3,
         grid=(blocks,),
         in_specs=[
             pl.BlockSpec(memory_space=pl.ANY),
             pl.BlockSpec((1, block_rows, rank_cols), lambda b, *_: (b, 0, 0)),
             pl.BlockSpec((1, block_rows, 1), lambda b, *_: (b, 0, 0)),
             pl.BlockSpec((kinds_n, block_rows, block_rows), lambda b, *_: (0, 0, 0)),
-            pl.BlockSpec((1, block_rows, block_rows), lambda b, i, c, t, bp: (bp[b], 0, 0)),
         ],
-        out_specs=pl.BlockSpec((1, block_rows, 2 * rank_cols), lambda b, *_: (b, 0, 0)),
+        out_specs=pl.BlockSpec((1, block_rows, rank_cols), lambda b, *_: (b, 0, 0)),
         scratch_shapes=[
             pltpu.VMEM((2, slots, block_rows, rank_cols), group_rows.dtype),
             pltpu.SemaphoreType.DMA((2, slots)),
@@ -91,9 +88,9 @@
     return pl.pallas_call(
         functools.partial(step_kernel, slots),
         grid_spec=grid_spec,
-        out_shape=jax.ShapeDtypeStruct((blocks, block_rows, 2 * rank_cols), jnp.bfloat16),
+        out_shape=jax.ShapeDtypeStruct((blocks, block_rows, rank_cols), jnp.bfloat16),
         compiler_params=pltpu.CompilerParams(dimension_semantics=("arbitrary",)),
-    )(ids, counts, kinds, bath_pattern, group_rows, own_rows, energy, coupling_blocks, bath_blocks)
+    )(ids, counts, kinds, group_rows, own_rows, energy, coupling_blocks)
 
 
 def allreduce_kernel(fields, cols, x_ref, o_ref, *scratch):
@@ -212,16 +209,26 @@
     counts = jnp.clip(neighbour_count, 1, slots)
     kinds = jnp.clip(coupling_type, 0, coupling_blocks.shape[0] - 1)
     bath_kind = jnp.clip(bath_pattern, 0, bath_blocks.shape[0] - 1)
+    own_rows = density_factor.reshape(blocks, block_rows, rank_cols)
+    bathed = jnp.einsum(
+        "bij,bjr->bir", bath_blocks[bath_kind], own_rows, preferred_element_type=jnp.float32
+    ).astype(jnp.bfloat16).reshape(blocks * block_rows, rank_cols)
+    contract_rows = (((0,), (0,)), ((), ()))
+    bath_gram = lax.dot_general(bathed, bathed, contract_rows, preferred_element_type=jnp.float32)
     gathered = lax.all_gather(density_factor, "col", axis=0, tiled=True)
     group_rows = gathered.reshape(group_blocks, block_rows, rank_cols)
-    own_rows = density_factor.reshape(blocks, block_rows, rank_cols)
     energy = onsite.reshape(blocks, block_rows, 1)
-    stacked = stacked_blocks(
-        group_rows, own_rows, energy, in_group.reshape(-1), counts, kinds.reshape(-1), bath_kind,
-        coupling_blocks, bath_blocks,
-    ).reshape(blocks * block_rows, 2 * rank_cols)
-    local_gram = lax.dot_general(
-        stacked, stacked, (((0,), (0,)), ((), ())), preferred_element_type=jnp.float32
+    moved = moved_blocks(
+        group_rows, own_rows, energy, in_group.reshape(-1), counts, kinds.reshape(-1), coupling_blocks,
+    ).reshape(blocks * block_rows, rank_cols)
+    moved_gram = lax.dot_general(moved, moved, contract_rows, preferred_element_type=jnp.float32)
+    cross_gram = lax.dot_general(moved, bathed, contract_rows, preferred_element_type=jnp.float32)
+    local_gram = jnp.concatenate(
+        [
+            jnp.concatenate([moved_gram, cross_gram], axis=1),
+            jnp.concatenate([cross_gram.T, bath_gram], axis=1),
+        ],
+        axis=0,
     )
     devices = lax.axis_size("row") * col_count
     stage_bits = devices.bit_length() - 1
@@ -231,7 +238,9 @@
         fields = [(s, 2) for s in range(stage_bits)]
     gram_sum = kernel_sum(local_gram, fields, col_count)
     rotation = orthonormal_steps(gram_sum, rank_cols).astype(jnp.bfloat16)
-    return jnp.dot(stacked, rotation, preferred_element_type=jnp.float32).astype(jnp.bfloat16)
+    product = jnp.dot(moved, rotation[:rank_cols], preferred_element_type=jnp.float32)
+    product += jnp.dot(bathed, rotation[rank_cols:], preferred_element_type=jnp.float32)
+    return product.astype(jnp.bfloat16)
 
 
 def solution(mesh):

time: 409 us -> 406 us (level)
  waiting for transfers between devices: 197 us -> 189 us
  local copies, waits for them, and re-layouts: 16 us -> 20.5 us
    all_gather x1, waiting for transfers between devices: 197 us -> 188 us  [shards(): gathered = lax.all_gather(density_factor, 'col', axis=0, tiled=True)]
    dot_general x2 -> x6, matrix products: 10.6 us -> 13.7 us  [the longest x1 4.12 us: shards(): jnp.einsum('bij,bjr->bir', bath_blocks[bath_kind], own_rows, preferred_el...]
  transfers between devices with their start and end apart: 1 -> 1, of which waited for: 1 -> 1; matrix products, arithmetic and copies ran while one was open for 1% -> 3% of each run, Pallas kernels for 0% -> 0%
where the time goes in v9:
time: 406 us
  waiting for transfers between devices  189 us (47%)
  other arithmetic  108 us (27%)
  Pallas kernels  49.7 us (12%)
  matrix products  21.5 us (5%)
  local copies, waits for them, and re-layouts  20.5 us (5%)
  between operations  13.6 us (3%)
    all_gather x1, waiting for transfers between devices, shards(): gathered = lax.all_gather(density_factor, 'col', axis=0, tiled=True)  188 us
    another operation x12, other arithmetic, sweep(): factor = jnp.linalg.cholesky(inner)  68 us
    another operation x8, other arithmetic, sweep(): lax.linalg.triangular_solve(factor, image, left_side=False, lower=True, t...  39.5 us
    pallas_call x1, Pallas kernels, kernel_sum(): pl.pallas_call(functools.partial(allreduce_kernel, tuple(fields), cols),...  35.5 us
    pallas_call x1, Pallas kernels, moved_blocks(): pl.pallas_call(functools.partial(step_kernel, slots), grid_spec=grid_spec...  14.2 us
    another operation x12, local copies, waits for them, and re-layouts  8.23 us
  transfers between devices with their start and end apart: 1, of which 1 were waited for; matrix products, arithmetic and copies ran while one was open for 3% of the time, Pallas kernels for 0%

profile of v9, /device:TPU:1, one launch (start us, length us, event | category | flops | bytes accessed | tf_op | source)
XLA Modules:
  0.0 405.7 jit_solution(17548903374355830319)
XLA Ops:
  6.6 0.7 all-gather.2.cloned.1.call-update
  7.4 0.6 reshape.44.ids_ref
  8.0 0.7 reshape.45.kind_ref
  8.7 3.3 reshape.84.ons_ref
  12.0 2.9 gather_fusion
  15.0 0.6 broadcast_clamp_fusion.1.cnt_ref
  15.5 4.1 %convolution_convert_fusion = bf16[8,512,256]{2,1,0:T(8,128)(2,1)S(1)} fusion(bf16[8,512,512]{2,1,0:T(8,128)(2,1)} %gather_fusion, bf16[8,512,256]{2,1,0:T(8,128)(2,1)} %bitcast.82), kind=kOutput, calls=%fused_computation.31 | convolution fusion | flops 1074790400 | bytes 8388608 | tf_op jit(solution)/shard_map/bij,bjr->bir/dot_general | solution.py:213
  19.7 1.3 copy-done.3
  21.0 0.9 convolution_bitcast_fusion
  22.0 188.0 %all-gather.2.cloned.1.call-done = bf16[65536,256]{1,0:T(8,128)(2,1)} async-done(((bf16[4096,256]{1,0:T(8,128)(2,1)}), bf16[65536,256]{1,0:T(8,128)(2,1)}) %all-gather.2.cloned.1.call-update) | async-done | bytes 33554448 | tf_op jit(solution)/shard_map/all_gather | solution.py:218
  210.0 14.2 %shard_map.82 = bf16[8,512,256]{2,1,0:T(8,128)(2,1)} custom-call(s32[64]{0:T(128)} %reshape.44.ids_ref, s32[8]{0:T(128)} %broadcast_clamp_fusion.1.cnt_ref, s32[64]{0:T(128)} %reshape.45.kind_ref, bf16[128,512,256]{2,1,0:T(8,128)(2,1)} %bitcast.80, bf16[8,512,256]{2,1,0:T(8,128)(2,1)} %bitcast.83, f32[8,512,1]{2,1,0:T(8,128)} %reshape.84.ons_ref, ...), custom_call_target="tpu_custom_call" | custom-call | tf_op jit(solution)/shard_map/pallas_call | solution.py:88
  224.2 3.1 fusion.16
  227.3 1.0 convolution_bitcast_fusion.1
  228.9 1.0 reshape.50.x_ref
  230.0 35.5 %shard_map.83 = f32[2048,128]{1,0:T(8,128)} custom-call(f32[2048,128]{1,0:T(8,128)} %reshape.50.x_ref), custom_call_target="tpu_custom_call" | custom-call | tf_op jit(solution)/shard_map/pallas_call | solution.py:181
  265.5 1.4 reshape.51
  266.9 127.3 %while.13 = (s32[]{:T(128)}, f32[512,256]{0,1:T(8,128)S(1)}, f32[512,512]{1,0:T(8,128)S(1)}, s32[]{:T(128)}, s32[]{:T(128)}, /*index=5*/f32[]{:T(128)}, s32[]{:T(128)}) while((s32[]{:T(128)}, f32[512,256]{0,1:T(8,128)S(1)}, f32[512,512]{1,0:T(8,128)S(1)}, s32[]{:T(128)}, s32[]{:T(128)}, /*index=5*/f32[]{:T(128)}, s32[]{:T(128)}) %tuple.51), condition=%wide.region_5.6_spmd, body=%wide.region_0.5_spmd.sunk | while | flops 1561018624 | bytes 9177372 | solution.py:25
  267.1 1.0 fusion.61
  268.1 1.0 fusion.62
  269.3 11.7 %cholesky.185 = f32[128,128]{1,0:T(8,128)S(1)} custom-call(f32[128,128]{1,0:T(8,128)S(1)} %cholesky.184), custom_call_target="Cholesky" | custom-call | tf_op jit(solution)/shard_map/while/body/eval_jaxpr/jit(cholesky)/cholesky | solution.py:20
  281.1 9.8 %custom-call.20 = f32[1,128,128]{1,2,0:T(8,128)S(1)} custom-call(f32[1,128,128]{2,1,0:T(8,128)S(1)} %get-tuple-element.114), custom_call_target="InvertDiagBlocksLowerTriangular" | custom-call | tf_op jit(solution)/shard_map/while/body/eval_jaxpr/jit(cholesky)/cholesky | solution.py:20
  291.4 11.7 %cholesky.187 = f32[128,128]{1,0:T(8,128)S(1)} custom-call(f32[128,128]{1,0:T(8,128)S(1)} %convolution_subtract_fusion.4), custom_call_target="Cholesky" | custom-call | tf_op jit(solution)/shard_map/while/body/eval_jaxpr/jit(cholesky)/cholesky | solution.py:20
  303.2 0.7 compare_reduce_fusion.3
  305.3 4.1 %while.14 = (s32[]{:T(128)}, f32[256,256]{1,0:T(8,128)S(1)}, s32[2,2]{1,0:T(2,128)S(1)}, f32[2,128,128]{2,1,0:T(8,128)S(1)}, s32[]{:T(128)}) while((s32[]{:T(128)}, f32[256,256]{1,0:T(8,128)S(1)}, s32[2,2]{1,0:T(2,128)S(1)}, f32[2,128,128]{2,1,0:T(8,128)S(1)}, s32[]{:T(128)}) %tuple.48), condition=%wide.while_cond, body=%wide.while_body.sunk | while | flops 2 | bytes 131189 | solution.py:21
  305.3 0.7 fusion.66
  306.0 1.4 bitcast_dynamic-update-slice_fusion.2
  307.4 0.7 fusion.66
  308.1 1.4 bitcast_dynamic-update-slice_fusion.2
  309.5 19.7 %custom-call.22 = f32[2,128,128]{1,2,0:T(8,128)S(1)} custom-call(f32[2,128,128]{2,1,0:T(8,128)S(1)} %get-tuple-element.122), custom_call_target="InvertDiagBlocksLowerTriangular" | custom-call | tf_op jit(solution)/shard_map/while/body/eval_jaxpr/triangular_solve | solution.py:21
  329.1 0.4 fusion.64
  329.6 0.6 convolution_subtract_fusion.5
  330.6 1.0 fusion.61
  331.7 1.0 fusion.62
  332.9 11.7 %cholesky.185 = f32[128,128]{1,0:T(8,128)S(1)} custom-call(f32[128,128]{1,0:T(8,128)S(1)} %cholesky.184), custom_call_target="Cholesky" | custom-call | tf_op jit(solution)/shard_map/while/body/eval_jaxpr/jit(cholesky)/cholesky | solution.py:20
  344.7 9.8 %custom-call.20 = f32[1,128,128]{1,2,0:T(8,128)S(1)} custom-call(f32[1,128,128]{2,1,0:T(8,128)S(1)} %get-tuple-element.114), custom_call_target="InvertDiagBlocksLowerTriangular" | custom-call | tf_op jit(solution)/shard_map/while/body/eval_jaxpr/jit(cholesky)/cholesky | solution.py:20
  355.0 11.7 %cholesky.187 = f32[128,128]{1,0:T(8,128)S(1)} custom-call(f32[128,128]{1,0:T(8,128)S(1)} %convolution_subtract_fusion.4), custom_call_target="Cholesky" | custom-call | tf_op jit(solution)/shard_map/while/body/eval_jaxpr/jit(cholesky)/cholesky | solution.py:20
  366.7 0.7 compare_reduce_fusion.3
  368.9 4.1 %while.14 = (s32[]{:T(128)}, f32[256,256]{1,0:T(8,128)S(1)}, s32[2,2]{1,0:T(2,128)S(1)}, f32[2,128,128]{2,1,0:T(8,128)S(1)}, s32[]{:T(128)}) while((s32[]{:T(128)}, f32[256,256]{1,0:T(8,128)S(1)}, s32[2,2]{1,0:T(2,128)S(1)}, f32[2,128,128]{2,1,0:T(8,128)S(1)}, s32[]{:T(128)}) %tuple.48), condition=%wide.while_cond, body=%wide.while_body.sunk | while | flops 2 | bytes 131189 | solution.py:21
  368.9 0.7 fusion.66
  369.5 1.4 bitcast_dynamic-update-slice_fusion.2
  371.0 0.7 fusion.66
  371.6 1.4 bitcast_dynamic-update-slice_fusion.2
  373.0 19.7 %custom-call.22 = f32[2,128,128]{1,2,0:T(8,128)S(1)} custom-call(f32[2,128,128]{2,1,0:T(8,128)S(1)} %get-tuple-element.122), custom_call_target="InvertDiagBlocksLowerTriangular" | custom-call | tf_op jit(solution)/shard_map/while/body/eval_jaxpr/triangular_solve | solution.py:21
  392.7 0.4 fusion.64
  393.1 0.6 convolution_subtract_fusion.5
  393.7 0.4 fusion.65
  394.2 2.5 fusion.11
  396.8 2.1 fusion.8
  (60 shorter events, 3.1 us)
Async XLA Ops:
  6.5 5.5 %copy-start = (bf16[4,512,512]{2,1,0:T(8,128)(2,1)S(1)}, bf16[4,512,512]{2,1,0:T(8,128)(2,1)}, u32[]{:S(2)}) copy-start(bf16[4,512,512]{2,1,0:T(8,128)(2,1)} %param.17) | copy-start | bytes 6291460
  6.5 0.8 copy-start.6
  6.5 1.5 copy-start.7
  6.5 2.2 copy-start.5
  6.5 5.4 %copy-start.8 = (s32[8]{0:T(128)S(1)}, s32[8]{0:T(128)}, u32[]{:S(2)}) copy-start(s32[8]{0:T(128)} %param.16) | copy-start | bytes 100
  6.5 203.4 %all-gather.2.cloned.1.call-start = ((), (), s32[]{:S(2)}) async-start(), calls=%async_computation | async-start | bytes 35651584 | tf_op jit(solution)/shard_map/all_gather | solution.py:218
  12.0 3.0 copy-start.9
  19.7 1.4 copy-start.3
  224.2 3.1 copy-start.2
  394.2 2.5 copy-start.4
  396.7 2.1 copy-start.1
Sparse Core Ops, SparseCore 0:
  9.5 200.4 all-gather.1

commit v10 on v9

--- a/solution.py
+++ b/solution.py
@@ -54,11 +54,9 @@
         def _():
             pltpu.make_async_copy(group_hbm.at[0], buf.at[slot, k], sems.at[slot, k]).wait()
             t = kind_ref[b * slots + k]
-            acc[t] += buf[slot, k].astype(jnp.float32)
-
-    coupled = jnp.dot(cpl_ref[0], acc[0].astype(jnp.bfloat16), preferred_element_type=jnp.float32)
-    for t in range(1, cpl_ref.shape[0]):
-        coupled += jnp.dot(cpl_ref[t], acc[t].astype(jnp.bfloat16), preferred_element_type=jnp.float32)
+            acc[...] += jnp.dot(cpl_ref[t], buf[slot, k], preferred_element_type=jnp.float32)
+
+    coupled = acc[...]
     own = own_ref[0]
     wide = own.astype(jnp.float32)
     moved = wide - time_step * (ons_ref[0] * wide + coupled)
@@ -82,7 +80,7 @@
         scratch_shapes=[
             pltpu.VMEM((2, slots, block_rows, rank_cols), group_rows.dtype),
             pltpu.SemaphoreType.DMA((2, slots)),
-            pltpu.VMEM((kinds_n, block_rows, rank_cols), jnp.float32),
+            pltpu.VMEM((block_rows, rank_cols), jnp.float32),
         ],
     )
     return pl.pallas_call(

time: 406 us -> 413 us (1.017)
  Pallas kernels: 49.7 us -> 56.8 us
    pallas_call x1, Pallas kernels: 14.2 us -> 20.3 us  [moved_blocks(): pl.pallas_call(functools.partial(step_kernel, slots), grid_spec=grid_spec...]
where the time goes in v10:
time: 413 us
  waiting for transfers between devices  189 us (46%)
  other arithmetic  108 us (26%)
  Pallas kernels  56.8 us (14%)
  matrix products  21.5 us (5%)
  local copies, waits for them, and re-layouts  20.5 us (5%)
  between operations  13.6 us (3%)
    all_gather x1, waiting for transfers between devices, shards(): gathered = lax.all_gather(density_factor, 'col', axis=0, tiled=True)  188 us
    another operation x12, other arithmetic, sweep(): factor = jnp.linalg.cholesky(inner)  68 us
    another operation x8, other arithmetic, sweep(): lax.linalg.triangular_solve(factor, image, left_side=False, lower=True, t...  39.5 us
    pallas_call x1, Pallas kernels, kernel_sum(): pl.pallas_call(functools.partial(allreduce_kernel, tuple(fields), cols),...  36.4 us
    pallas_call x1, Pallas kernels, moved_blocks(): pl.pallas_call(functools.partial(step_kernel, slots), grid_spec=grid_spec...  20.3 us
  transfers between devices with their start and end apart: 1, of which 1 were waited for; matrix products, arithmetic and copies ran while one was open for 3% of the time, Pallas kernels for 0%

profile of v10, /device:TPU:1, one launch (start us, length us, event | category | flops | bytes accessed | tf_op | source)
XLA Modules:
  0.0 412.7 jit_solution(34565728867884366)
XLA Ops:
  6.6 0.7 all-gather.2.cloned.1.call-update
  7.4 0.6 reshape.44.ids_ref
  8.0 0.7 reshape.45.kind_ref
  8.7 3.3 reshape.84.ons_ref
  12.0 2.9 gather_fusion
  15.0 0.6 broadcast_clamp_fusion.1.cnt_ref
  15.5 4.1 convolution_convert_fusion
  19.7 1.3 copy-done.3
  21.0 0.9 convolution_bitcast_fusion
  22.0 188.0 %all-gather.2.cloned.1.call-done = bf16[65536,256]{1,0:T(8,128)(2,1)} async-done(((bf16[4096,256]{1,0:T(8,128)(2,1)}), bf16[65536,256]{1,0:T(8,128)(2,1)}) %all-gather.2.cloned.1.call-update) | async-done | bytes 33554448 | tf_op jit(solution)/shard_map/all_gather | solution.py:216
  210.0 20.3 %shard_map.82 = bf16[8,512,256]{2,1,0:T(8,128)(2,1)} custom-call(s32[64]{0:T(128)} %reshape.44.ids_ref, s32[8]{0:T(128)} %broadcast_clamp_fusion.1.cnt_ref, s32[64]{0:T(128)} %reshape.45.kind_ref, bf16[128,512,256]{2,1,0:T(8,128)(2,1)} %bitcast.80, bf16[8,512,256]{2,1,0:T(8,128)(2,1)} %bitcast.83, f32[8,512,1]{2,1,0:T(8,128)} %reshape.84.ons_ref, ...), custom_call_target="tpu_custom_call" | custom-call | tf_op jit(solution)/shard_map/pallas_call | solution.py:86
  230.3 3.1 fusion.16
  233.5 1.0 convolution_bitcast_fusion.1
  235.1 1.0 reshape.50.x_ref
  236.1 36.4 %shard_map.83 = f32[2048,128]{1,0:T(8,128)} custom-call(f32[2048,128]{1,0:T(8,128)} %reshape.50.x_ref), custom_call_target="tpu_custom_call" | custom-call | tf_op jit(solution)/shard_map/pallas_call | solution.py:179
  272.6 1.4 reshape.51
  274.0 127.3 %while.13 = (s32[]{:T(128)}, f32[512,256]{0,1:T(8,128)S(1)}, f32[512,512]{1,0:T(8,128)S(1)}, s32[]{:T(128)}, s32[]{:T(128)}, /*index=5*/f32[]{:T(128)}, s32[]{:T(128)}) while((s32[]{:T(128)}, f32[512,256]{0,1:T(8,128)S(1)}, f32[512,512]{1,0:T(8,128)S(1)}, s32[]{:T(128)}, s32[]{:T(128)}, /*index=5*/f32[]{:T(128)}, s32[]{:T(128)}) %tuple.51), condition=%wide.region_5.6_spmd, body=%wide.region_0.5_spmd.sunk | while | flops 1561018624 | bytes 9177372 | solution.py:25
  274.2 1.0 fusion.61
  275.2 1.0 fusion.62
  276.4 11.7 %cholesky.185 = f32[128,128]{1,0:T(8,128)S(1)} custom-call(f32[128,128]{1,0:T(8,128)S(1)} %cholesky.184), custom_call_target="Cholesky" | custom-call | tf_op jit(solution)/shard_map/while/body/eval_jaxpr/jit(cholesky)/cholesky | solution.py:20
  288.2 9.8 %custom-call.20 = f32[1,128,128]{1,2,0:T(8,128)S(1)} custom-call(f32[1,128,128]{2,1,0:T(8,128)S(1)} %get-tuple-element.114), custom_call_target="InvertDiagBlocksLowerTriangular" | custom-call | tf_op jit(solution)/shard_map/while/body/eval_jaxpr/jit(cholesky)/cholesky | solution.py:20
  298.5 11.7 %cholesky.187 = f32[128,128]{1,0:T(8,128)S(1)} custom-call(f32[128,128]{1,0:T(8,128)S(1)} %convolution_subtract_fusion.4), custom_call_target="Cholesky" | custom-call | tf_op jit(solution)/shard_map/while/body/eval_jaxpr/jit(cholesky)/cholesky | solution.py:20
  310.2 0.7 compare_reduce_fusion.3
  312.4 4.1 %while.14 = (s32[]{:T(128)}, f32[256,256]{1,0:T(8,128)S(1)}, s32[2,2]{1,0:T(2,128)S(1)}, f32[2,128,128]{2,1,0:T(8,128)S(1)}, s32[]{:T(128)}) while((s32[]{:T(128)}, f32[256,256]{1,0:T(8,128)S(1)}, s32[2,2]{1,0:T(2,128)S(1)}, f32[2,128,128]{2,1,0:T(8,128)S(1)}, s32[]{:T(128)}) %tuple.48), condition=%wide.while_cond, body=%wide.while_body.sunk | while | flops 2 | bytes 131189 | solution.py:21
  312.4 0.7 fusion.66
  313.0 1.4 bitcast_dynamic-update-slice_fusion.2
  314.5 0.7 fusion.66
  315.1 1.4 bitcast_dynamic-update-slice_fusion.2
  316.5 19.7 %custom-call.22 = f32[2,128,128]{1,2,0:T(8,128)S(1)} custom-call(f32[2,128,128]{2,1,0:T(8,128)S(1)} %get-tuple-element.122), custom_call_target="InvertDiagBlocksLowerTriangular" | custom-call | tf_op jit(solution)/shard_map/while/body/eval_jaxpr/triangular_solve | solution.py:21
  336.2 0.4 fusion.64
  336.6 0.6 convolution_subtract_fusion.5
  337.2 0.4 fusion.65
  337.7 1.0 fusion.61
  338.7 1.0 fusion.62
  340.0 11.7 %cholesky.185 = f32[128,128]{1,0:T(8,128)S(1)} custom-call(f32[128,128]{1,0:T(8,128)S(1)} %cholesky.184), custom_call_target="Cholesky" | custom-call | tf_op jit(solution)/shard_map/while/body/eval_jaxpr/jit(cholesky)/cholesky | solution.py:20
  351.7 9.8 %custom-call.20 = f32[1,128,128]{1,2,0:T(8,128)S(1)} custom-call(f32[1,128,128]{2,1,0:T(8,128)S(1)} %get-tuple-element.114), custom_call_target="InvertDiagBlocksLowerTriangular" | custom-call | tf_op jit(solution)/shard_map/while/body/eval_jaxpr/jit(cholesky)/cholesky | solution.py:20
  362.0 11.7 %cholesky.187 = f32[128,128]{1,0:T(8,128)S(1)} custom-call(f32[128,128]{1,0:T(8,128)S(1)} %convolution_subtract_fusion.4), custom_call_target="Cholesky" | custom-call | tf_op jit(solution)/shard_map/while/body/eval_jaxpr/jit(cholesky)/cholesky | solution.py:20
  373.8 0.7 compare_reduce_fusion.3
  375.9 4.1 %while.14 = (s32[]{:T(128)}, f32[256,256]{1,0:T(8,128)S(1)}, s32[2,2]{1,0:T(2,128)S(1)}, f32[2,128,128]{2,1,0:T(8,128)S(1)}, s32[]{:T(128)}) while((s32[]{:T(128)}, f32[256,256]{1,0:T(8,128)S(1)}, s32[2,2]{1,0:T(2,128)S(1)}, f32[2,128,128]{2,1,0:T(8,128)S(1)}, s32[]{:T(128)}) %tuple.48), condition=%wide.while_cond, body=%wide.while_body.sunk | while | flops 2 | bytes 131189 | solution.py:21
  375.9 0.7 fusion.66
  376.6 1.4 bitcast_dynamic-update-slice_fusion.2
  378.0 0.7 fusion.66
  378.7 1.4 bitcast_dynamic-update-slice_fusion.2
  380.1 19.7 %custom-call.22 = f32[2,128,128]{1,2,0:T(8,128)S(1)} custom-call(f32[2,128,128]{2,1,0:T(8,128)S(1)} %get-tuple-element.122), custom_call_target="InvertDiagBlocksLowerTriangular" | custom-call | tf_op jit(solution)/shard_map/while/body/eval_jaxpr/triangular_solve | solution.py:21
  399.8 0.4 fusion.64
  400.2 0.6 convolution_subtract_fusion.5
  401.3 2.5 fusion.11
  403.8 2.1 fusion.8
  (60 shorter events, 3.1 us)
Async XLA Ops:
  6.5 5.5 %copy-start = (bf16[4,512,512]{2,1,0:T(8,128)(2,1)S(1)}, bf16[4,512,512]{2,1,0:T(8,128)(2,1)}, u32[]{:S(2)}) copy-start(bf16[4,512,512]{2,1,0:T(8,128)(2,1)} %param.17) | copy-start | bytes 6291460
  6.5 0.8 copy-start.6
  6.5 1.5 copy-start.7
  6.5 2.2 copy-start.5
  6.5 5.4 %copy-start.8 = (s32[8]{0:T(128)S(1)}, s32[8]{0:T(128)}, u32[]{:S(2)}) copy-start(s32[8]{0:T(128)} %param.16) | copy-start | bytes 100
  6.5 203.4 %all-gather.2.cloned.1.call-start = ((), (), s32[]{:S(2)}) async-start(), calls=%async_computation | async-start | bytes 35651584 | tf_op jit(solution)/shard_map/all_gather | solution.py:216
  12.0 3.0 copy-start.9
  19.7 1.4 copy-start.3
  230.3 3.1 copy-start.2
  401.3 2.5 copy-start.4
  403.8 2.1 copy-start.1
Sparse Core Ops, SparseCore 0:
  9.5 200.4 all-gather.1

commit v11 on v10

--- a/solution.py
+++ b/solution.py
@@ -25,8 +25,8 @@
     return lax.fori_loop(0, SWEEPS, sweep, jnp.eye(2 * rank_cols, rank_cols, dtype=jnp.float32))
 
 
-def step_kernel(slots, ids_ref, cnt_ref, kind_ref,
-                group_hbm, own_ref, ons_ref, cpl_ref, out_ref, buf, sems, acc):
+def step_kernel(slots, ids_ref, cnt_ref, kind_ref, first_ref, used_ref, lead_ref,
+                group_hbm, own_ref, ons_ref, cpl_ref, out_ref, buf, sems, acc, cacc):
     b = pl.program_id(0)
     last = pl.num_programs(0) - 1
     rank_cols = own_ref.shape[2]
@@ -48,27 +48,47 @@
         fetch(b + 1, (b + 1) % 2)
 
     slot = b % 2
-    acc[...] = jnp.zeros_like(acc)
     for k in range(slots):
         @pl.when(k < cnt_ref[b])
         def _():
             pltpu.make_async_copy(group_hbm.at[0], buf.at[slot, k], sems.at[slot, k]).wait()
             t = kind_ref[b * slots + k]
-            acc[...] += jnp.dot(cpl_ref[t], buf[slot, k], preferred_element_type=jnp.float32)
-
-    coupled = acc[...]
+            first = first_ref[b * slots + k]
+
+            @pl.when(first == 1)
+            def _():
+                acc[t] = buf[slot, k].astype(jnp.float32)
+
+            @pl.when(first == 0)
+            def _():
+                acc[t] += buf[slot, k].astype(jnp.float32)
+
+    kinds_n = cpl_ref.shape[0]
+    for t in range(kinds_n):
+        used = used_ref[b * kinds_n + t]
+        lead = lead_ref[b * kinds_n + t]
+
+        @pl.when((used == 1) & (lead == 1))
+        def _():
+            cacc[...] = jnp.dot(cpl_ref[t], acc[t].astype(jnp.bfloat16), preferred_element_type=jnp.float32)
+
+        @pl.when((used == 1) & (lead == 0))
+        def _():
+            cacc[...] += jnp.dot(cpl_ref[t], acc[t].astype(jnp.bfloat16), preferred_element_type=jnp.float32)
+
+    coupled = cacc[...]
     own = own_ref[0]
     wide = own.astype(jnp.float32)
     moved = wide - time_step * (ons_ref[0] * wide + coupled)
     out_ref[0] = moved.astype(out_ref.dtype)
 
 
-def moved_blocks(group_rows, own_rows, energy, ids, counts, kinds, coupling_blocks):
+def moved_blocks(group_rows, own_rows, energy, ids, counts, kinds, first, used, lead, coupling_blocks):
     blocks, block_rows, rank_cols = own_rows.shape
     slots = ids.shape[0] // blocks
     kinds_n = coupling_blocks.shape[0]
     grid_spec = pltpu.PrefetchScalarGridSpec(
-        num_scalar_prefetch=3,
+        num_scalar_prefetch=6,
         grid=(blocks,),
         in_specs=[
             pl.BlockSpec(memory_space=pl.ANY),
@@ -80,6 +100,7 @@
         scratch_shapes=[
             pltpu.VMEM((2, slots, block_rows, rank_cols), group_rows.dtype),
             pltpu.SemaphoreType.DMA((2, slots)),
+            pltpu.VMEM((kinds_n, block_rows, rank_cols), jnp.float32),
             pltpu.VMEM((block_rows, rank_cols), jnp.float32),
         ],
     )
@@ -88,7 +109,7 @@
         grid_spec=grid_spec,
         out_shape=jax.ShapeDtypeStruct((blocks, block_rows, rank_cols), jnp.bfloat16),
         compiler_params=pltpu.CompilerParams(dimension_semantics=("arbitrary",)),
-    )(ids, counts, kinds, group_rows, own_rows, energy, coupling_blocks)
+    )(ids, counts, kinds, first, used, lead, group_rows, own_rows, energy, coupling_blocks)
 
 
 def allreduce_kernel(fields, cols, x_ref, o_ref, *scratch):
@@ -216,8 +237,19 @@
     gathered = lax.all_gather(density_factor, "col", axis=0, tiled=True)
     group_rows = gathered.reshape(group_blocks, block_rows, rank_cols)
     energy = onsite.reshape(blocks, block_rows, 1)
+    kinds_n = coupling_blocks.shape[0]
+    live = jnp.arange(slots, dtype=jnp.int32)[None, :] < counts[:, None]
+    same = (kinds[:, :, None] == kinds[:, None, :]) & live[:, None, :]
+    earlier = jnp.arange(slots)[None, :, None] > jnp.arange(slots)[None, None, :]
+    first = (live & ~jnp.any(same & earlier, axis=2)).astype(jnp.int32)
+    used = jnp.any(
+        (kinds[:, :, None] == jnp.arange(kinds_n, dtype=jnp.int32)[None, None, :]) & live[:, :, None], axis=1
+    )
+    lower = jnp.arange(kinds_n)[:, None] > jnp.arange(kinds_n)[None, :]
+    lead = (used & ~jnp.any(used[:, None, :] & lower[None], axis=2)).astype(jnp.int32)
     moved = moved_blocks(
-        group_rows, own_rows, energy, in_group.reshape(-1), counts, kinds.reshape(-1), coupling_blocks,
+        group_rows, own_rows, energy, in_group.reshape(-1), counts, kinds.reshape(-1),
+        first.reshape(-1), used.astype(jnp.int32).reshape(-1), lead.reshape(-1), coupling_blocks,
     ).reshape(blocks * block_rows, rank_cols)
     moved_gram = lax.dot_general(moved, moved, contract_rows, preferred_element_type=jnp.float32)
     cross_gram = lax.dot_general(moved, bathed, contract_rows, preferred_element_type=jnp.float32)

time: 413 us -> 409 us (level)
  Pallas kernels: 56.8 us -> 52.5 us
    pallas_call x1, Pallas kernels: 20.3 us -> 15.1 us  [moved_blocks(): pl.pallas_call(functools.partial(step_kernel, slots), grid_spec=grid_spec...]
  transfers between devices with their start and end apart: 1 -> 1, of which waited for: 1 -> 1; matrix products, arithmetic and copies ran while one was open for 3% -> 4% of each run, Pallas kernels for 0% -> 0%
where the time goes in v11:
time: 409 us; the launch traced here: 408 us
  waiting for transfers between devices  187 us (46%)
  other arithmetic  109 us (27%)
  Pallas kernels  52.5 us (13%)
  local copies, waits for them, and re-layouts  22.3 us (5%)
  matrix products  21.5 us (5%)
  between operations  13.6 us (3%)
    all_gather x1, waiting for transfers between devices, shards(): gathered = lax.all_gather(density_factor, 'col', axis=0, tiled=True)  186 us
    another operation x12, other arithmetic, sweep(): factor = jnp.linalg.cholesky(inner)  68 us
    another operation x8, other arithmetic, sweep(): lax.linalg.triangular_solve(factor, image, left_side=False, lower=True, t...  39.5 us
    pallas_call x1, Pallas kernels, kernel_sum(): pl.pallas_call(functools.partial(allreduce_kernel, tuple(fields), cols),...  37.4 us
    pallas_call x1, Pallas kernels, moved_blocks(): pl.pallas_call(functools.partial(step_kernel, slots), grid_spec=grid_spec...  15.1 us
  transfers between devices with their start and end apart: 1, of which 1 were waited for; matrix products, arithmetic and copies ran while one was open for 4% of the time, Pallas kernels for 0%

profile of v11, /device:TPU:1, one launch (start us, length us, event | category | flops | bytes accessed | tf_op | source)
XLA Modules:
  0.0 408.1 jit_solution(1243352416397756260)
XLA Ops:
  6.6 0.7 all-gather.2.cloned.1.call-update
  7.4 0.6 reshape.130.kind_ref
  8.5 0.7 reshape.158.used_ref
  9.2 0.7 reshape.159.lead_ref
  10.2 0.7 reshape.157.first_ref
  10.9 3.3 reshape.172.ons_ref
  14.2 0.6 reshape.129.ids_ref
  14.8 2.9 gather_fusion
  17.7 4.1 %convolution_convert_fusion = bf16[8,512,256]{2,1,0:T(8,128)(2,1)S(1)} fusion(bf16[8,512,512]{2,1,0:T(8,128)(2,1)} %gather_fusion, bf16[8,512,256]{2,1,0:T(8,128)(2,1)} %bitcast.82), kind=kOutput, calls=%fused_computation.31 | convolution fusion | flops 1074790400 | bytes 8388608 | tf_op jit(solution)/shard_map/bij,bjr->bir/dot_general | solution.py:232
  21.9 1.3 copy-done.3
  23.2 0.9 convolution_bitcast_fusion
  24.1 185.9 %all-gather.2.cloned.1.call-done = bf16[65536,256]{1,0:T(8,128)(2,1)} async-done(((bf16[4096,256]{1,0:T(8,128)(2,1)}), bf16[65536,256]{1,0:T(8,128)(2,1)}) %all-gather.2.cloned.1.call-update) | async-done | bytes 33554448 | tf_op jit(solution)/shard_map/all_gather | solution.py:237
  210.0 15.1 %shard_map.82 = bf16[8,512,256]{2,1,0:T(8,128)(2,1)} custom-call(s32[64]{0:T(128)} %reshape.129.ids_ref, s32[8]{0:T(128)} %copy-done.6, s32[64]{0:T(128)} %reshape.130.kind_ref, s32[64]{0:T(128)} %reshape.157.first_ref, s32[32]{0:T(128)} %reshape.158.used_ref, s32[32]{0:T(128)} %reshape.159.lead_ref, bf16[128,512,256]{2,1,0:T(8,128)(2,1)} %bitcast.80, ...), custom_call_target="tpu_custom_call" | custom-call | tf_op jit(solution)/shard_map/pallas_call | solution.py:107
  225.1 3.1 fusion.18
  228.3 1.0 convolution_bitcast_fusion.1
  229.9 1.0 reshape.135.x_ref
  230.9 37.4 %shard_map.83 = f32[2048,128]{1,0:T(8,128)} custom-call(f32[2048,128]{1,0:T(8,128)} %reshape.135.x_ref), custom_call_target="tpu_custom_call" | custom-call | tf_op jit(solution)/shard_map/pallas_call | solution.py:200
  268.3 1.4 reshape.136
  269.7 127.0 %while.13 = (s32[]{:T(128)}, f32[512,256]{0,1:T(8,128)S(1)}, f32[512,512]{1,0:T(8,128)S(1)}, s32[]{:T(128)}, s32[]{:T(128)}, /*index=5*/f32[]{:T(128)}, s32[]{:T(128)}) while((s32[]{:T(128)}, f32[512,256]{0,1:T(8,128)S(1)}, f32[512,512]{1,0:T(8,128)S(1)}, s32[]{:T(128)}, s32[]{:T(128)}, /*index=5*/f32[]{:T(128)}, s32[]{:T(128)}) %tuple.53), condition=%wide.region_8.9_spmd, body=%wide.region_3.8_spmd.sunk | while | flops 1561018624 | bytes 9177364 | solution.py:25
  269.9 1.0 fusion.63
  270.9 1.0 fusion.64
  272.2 11.7 %cholesky.185 = f32[128,128]{1,0:T(8,128)S(1)} custom-call(f32[128,128]{1,0:T(8,128)S(1)} %cholesky.184), custom_call_target="Cholesky" | custom-call | tf_op jit(solution)/shard_map/while/body/eval_jaxpr/jit(cholesky)/cholesky | solution.py:20
  283.9 9.8 %custom-call.20 = f32[1,128,128]{1,2,0:T(8,128)S(1)} custom-call(f32[1,128,128]{2,1,0:T(8,128)S(1)} %get-tuple-element.118), custom_call_target="InvertDiagBlocksLowerTriangular" | custom-call | tf_op jit(solution)/shard_map/while/body/eval_jaxpr/jit(cholesky)/cholesky | solution.py:20
  294.2 11.7 %cholesky.187 = f32[128,128]{1,0:T(8,128)S(1)} custom-call(f32[128,128]{1,0:T(8,128)S(1)} %convolution_subtract_fusion.4), custom_call_target="Cholesky" | custom-call | tf_op jit(solution)/shard_map/while/body/eval_jaxpr/jit(cholesky)/cholesky | solution.py:20
  306.0 0.7 compare_reduce_fusion.3
  308.1 4.0 while.14
  308.1 0.6 fusion.68
  308.8 1.3 bitcast_dynamic-update-slice_fusion.2
  310.1 0.6 fusion.68
  310.8 1.3 bitcast_dynamic-update-slice_fusion.2
  312.1 19.7 %custom-call.22 = f32[2,128,128]{1,2,0:T(8,128)S(1)} custom-call(f32[2,128,128]{2,1,0:T(8,128)S(1)} %get-tuple-element.126), custom_call_target="InvertDiagBlocksLowerTriangular" | custom-call | tf_op jit(solution)/shard_map/while/body/eval_jaxpr/triangular_solve | solution.py:21
  331.8 0.4 fusion.66
  332.2 0.6 convolution_subtract_fusion.5
  333.3 1.0 fusion.63
  334.3 1.0 fusion.64
  335.6 11.7 %cholesky.185 = f32[128,128]{1,0:T(8,128)S(1)} custom-call(f32[128,128]{1,0:T(8,128)S(1)} %cholesky.184), custom_call_target="Cholesky" | custom-call | tf_op jit(solution)/shard_map/while/body/eval_jaxpr/jit(cholesky)/cholesky | solution.py:20
  347.3 9.8 %custom-call.20 = f32[1,128,128]{1,2,0:T(8,128)S(1)} custom-call(f32[1,128,128]{2,1,0:T(8,128)S(1)} %get-tuple-element.118), custom_call_target="InvertDiagBlocksLowerTriangular" | custom-call | tf_op jit(solution)/shard_map/while/body/eval_jaxpr/jit(cholesky)/cholesky | solution.py:20
  357.6 11.7 %cholesky.187 = f32[128,128]{1,0:T(8,128)S(1)} custom-call(f32[128,128]{1,0:T(8,128)S(1)} %convolution_subtract_fusion.4), custom_call_target="Cholesky" | custom-call | tf_op jit(solution)/shard_map/while/body/eval_jaxpr/jit(cholesky)/cholesky | solution.py:20
  369.4 0.7 compare_reduce_fusion.3
  371.5 4.0 while.14
  371.5 0.6 fusion.68
  372.2 1.3 bitcast_dynamic-update-slice_fusion.2
  373.5 0.6 fusion.68
  374.2 1.3 bitcast_dynamic-update-slice_fusion.2
  375.5 19.7 %custom-call.22 = f32[2,128,128]{1,2,0:T(8,128)S(1)} custom-call(f32[2,128,128]{2,1,0:T(8,128)S(1)} %get-tuple-element.126), custom_call_target="InvertDiagBlocksLowerTriangular" | custom-call | tf_op jit(solution)/shard_map/while/body/eval_jaxpr/triangular_solve | solution.py:21
  395.6 0.6 convolution_subtract_fusion.5
  396.7 2.5 fusion.11
  399.2 2.1 fusion.8
  (74 shorter events, 4.7 us)
Async XLA Ops:
  6.5 8.3 %copy-start = (bf16[4,512,512]{2,1,0:T(8,128)(2,1)S(1)}, bf16[4,512,512]{2,1,0:T(8,128)(2,1)}, u32[]{:S(2)}) copy-start(bf16[4,512,512]{2,1,0:T(8,128)(2,1)} %param.17) | copy-start | bytes 6291460
  6.5 0.8 copy-start.7
  6.5 1.5 copy-start.9
  6.5 4.4 %copy-start.5 = (f32[4096]{0:T(1024)S(1)}, f32[4096]{0:T(1024)}, u32[]{:S(2)}) copy-start(f32[4096]{0:T(1024)} %param.11) | copy-start | bytes 49156
  6.5 7.6 %copy-start.8 = (s32[8,8]{1,0:T(8,128)S(1)}, s32[8,8]{1,0:T(8,128)}, u32[]{:S(2)}) copy-start(s32[8,8]{1,0:T(8,128)} %param.12) | copy-start | bytes 772
  6.5 8.3 %copy-start.10 = (s32[8]{0:T(128)S(1)}, s32[8]{0:T(128)}, u32[]{:S(2)}) copy-start(s32[8]{0:T(128)} %param.16) | copy-start | bytes 100
  6.6 203.4 %all-gather.2.cloned.1.call-start = ((), (), s32[]{:S(2)}) async-start(), calls=%async_computation | async-start | bytes 35651584 | tf_op jit(solution)/shard_map/all_gather | solution.py:237
  8.0 9.7 %copy-start.6 = (s32[8]{0:T(128)}, s32[8]{0:T(128)S(1)}, u32[]{:S(2)}) copy-start(s32[8]{0:T(128)S(1)} %broadcast_clamp_fusion.1.cnt_ref) | copy-start | bytes 100
  21.9 1.3 copy-start.3
  225.1 3.1 copy-start.2
  396.7 2.5 copy-start.4
  399.2 2.1 copy-start.1
Sparse Core Ops, SparseCore 0:
  9.5 200.4 all-gather.1

commit v12 on v9

--- a/solution.py
+++ b/solution.py
@@ -166,7 +166,7 @@
         size = size * r
 
 
-def kernel_sum(local, fields, cols):
+def kernel_sum(local, fields, cols, channel):
     lanes = 128
     flat = local.reshape(-1, lanes)
     rows = flat.shape[0]
@@ -184,7 +184,7 @@
         in_specs=[pl.BlockSpec(memory_space=pltpu.VMEM)],
         out_specs=pl.BlockSpec(memory_space=pltpu.VMEM),
         scratch_shapes=scratch,
-        compiler_params=pltpu.CompilerParams(collective_id=0, has_side_effects=True),
+        compiler_params=pltpu.CompilerParams(collective_id=channel, has_side_effects=True),
     )(flat)
     return total.reshape(local.shape)
 
@@ -215,6 +215,16 @@
     ).astype(jnp.bfloat16).reshape(blocks * block_rows, rank_cols)
     contract_rows = (((0,), (0,)), ((), ()))
     bath_gram = lax.dot_general(bathed, bathed, contract_rows, preferred_element_type=jnp.float32)
+    devices = lax.axis_size("row") * col_count
+    stage_bits = devices.bit_length() - 1
+    if stage_bits == 7:
+        fields = [(4, 2), (0, 16), (5, 4)]
+    else:
+        fields = [(s, 2) for s in range(stage_bits)]
+    bath_flat = bath_gram.reshape(-1, 128)
+    bath_flat = jnp.concatenate([bath_flat, jnp.zeros_like(bath_flat)], axis=0)
+    bath_sum = kernel_sum(bath_flat, fields, col_count, 1)[: bath_flat.shape[0] // 2]
+    bath_sum = bath_sum.reshape(bath_gram.shape)
     gathered = lax.all_gather(density_factor, "col", axis=0, tiled=True)
     group_rows = gathered.reshape(group_blocks, block_rows, rank_cols)
     energy = onsite.reshape(blocks, block_rows, 1)
@@ -223,20 +233,15 @@
     ).reshape(blocks * block_rows, rank_cols)
     moved_gram = lax.dot_general(moved, moved, contract_rows, preferred_element_type=jnp.float32)
     cross_gram = lax.dot_general(moved, bathed, contract_rows, preferred_element_type=jnp.float32)
-    local_gram = jnp.concatenate(
+    upper = kernel_sum(jnp.concatenate([moved_gram, cross_gram], axis=0), fields, col_count, 0)
+    moved_sum, cross_sum = upper[:rank_cols], upper[rank_cols:]
+    gram_sum = jnp.concatenate(
         [
-            jnp.concatenate([moved_gram, cross_gram], axis=1),
-            jnp.concatenate([cross_gram.T, bath_gram], axis=1),
+            jnp.concatenate([moved_sum, cross_sum], axis=1),
+            jnp.concatenate([cross_sum.T, bath_sum], axis=1),
         ],
         axis=0,
     )
-    devices = lax.axis_size("row") * col_count
-    stage_bits = devices.bit_length() - 1
-    if stage_bits == 7:
-        fields = [(4, 2), (0, 16), (5, 4)]
-    else:
-        fields = [(s, 2) for s in range(stage_bits)]
-    gram_sum = kernel_sum(local_gram, fields, col_count)
     rotation = orthonormal_steps(gram_sum, rank_cols).astype(jnp.bfloat16)
     product = jnp.dot(moved, rotation[:rank_cols], preferred_element_type=jnp.float32)
     product += jnp.dot(bathed, rotation[rank_cols:], preferred_element_type=jnp.float32)

time: 406 us -> 405 us (level)
  waiting for transfers between devices: 189 us -> 155 us
  Pallas kernels: 49.7 us -> 82 us
    all_gather x1, waiting for transfers between devices: 188 us -> 154 us  [shards(): gathered = lax.all_gather(density_factor, 'col', axis=0, tiled=True)]
    pallas_call x1 -> x2, Pallas kernels: 35.5 us -> 68.1 us  [kernel_sum(): pl.pallas_call(functools.partial(allreduce_kernel, tuple(fields), cols),...]
  transfers between devices with their start and end apart: 1 -> 1, of which waited for: 1 -> 1; matrix products, arithmetic and copies ran while one was open for 3% -> 4% of each run, Pallas kernels for 0% -> 9%
where the time goes in v12:
time: 405 us; the launch traced here: 404 us
  waiting for transfers between devices  155 us (38%)
  other arithmetic  108 us (27%)
  Pallas kernels  82 us (20%)
  matrix products  21.1 us (5%)
  local copies, waits for them, and re-layouts  20.7 us (5%)
  between operations  13.6 us (3%)
    all_gather x1, waiting for transfers between devices, shards(): gathered = lax.all_gather(density_factor, 'col', axis=0, tiled=True)  154 us
    pallas_call x2, Pallas kernels, kernel_sum(): pl.pallas_call(functools.partial(allreduce_kernel, tuple(fields), cols),...  68.1 us
    another operation x12, other arithmetic, sweep(): factor = jnp.linalg.cholesky(inner)  68 us
    another operation x8, other arithmetic, sweep(): lax.linalg.triangular_solve(factor, image, left_side=False, lower=True, t...  39.5 us
    pallas_call x1, Pallas kernels, moved_blocks(): pl.pallas_call(functools.partial(step_kernel, slots), grid_spec=grid_spec...  13.9 us
  transfers between devices with their start and end apart: 1, of which 1 were waited for; matrix products, arithmetic and copies ran while one was open for 4% of the time, Pallas kernels for 9%

profile of v12, /device:TPU:1, one launch (start us, length us, event | category | flops | bytes accessed | tf_op | source)
XLA Modules:
  0.0 404.0 jit_solution(14508461901114280011)
XLA Ops:
  6.6 0.7 all-gather.2.cloned.1.call-update
  7.4 0.7 reshape.50.ids_ref
  8.1 0.7 reshape.51.kind_ref
  8.7 3.3 reshape.91.ons_ref
  12.0 2.9 gather_fusion
  14.9 4.1 %convolution_convert_fusion = bf16[8,512,256]{2,1,0:T(8,128)(2,1)S(1)} fusion(bf16[8,512,512]{2,1,0:T(8,128)(2,1)} %gather_fusion, bf16[8,512,256]{2,1,0:T(8,128)(2,1)} %bitcast.82), kind=kOutput, calls=%fused_computation.31 | convolution fusion | flops 1074790400 | bytes 8388608 | tf_op jit(solution)/shard_map/bij,bjr->bir/dot_general | solution.py:213
  19.0 0.7 convolution_bitcast_fusion
  19.8 0.6 copy-done.3
  20.4 0.8 concatenate.19.x_ref
  21.2 38.3 %shard_map.84 = f32[1024,128]{1,0:T(8,128)} custom-call(f32[1024,128]{1,0:T(8,128)} %concatenate.19.x_ref), custom_call_target="tpu_custom_call" | custom-call | tf_op jit(solution)/shard_map/pallas_call | solution.py:181
  59.5 1.0 slice.67
  60.7 0.6 broadcast_clamp_fusion.1.cnt_ref
  61.2 154.4 %all-gather.2.cloned.1.call-done = bf16[65536,256]{1,0:T(8,128)(2,1)} async-done(((bf16[4096,256]{1,0:T(8,128)(2,1)}), bf16[65536,256]{1,0:T(8,128)(2,1)}) %all-gather.2.cloned.1.call-update) | async-done | bytes 33554448 | tf_op jit(solution)/shard_map/all_gather | solution.py:228
  215.6 13.9 %shard_map.82 = bf16[8,512,256]{2,1,0:T(8,128)(2,1)} custom-call(s32[64]{0:T(128)} %reshape.50.ids_ref, s32[8]{0:T(128)} %broadcast_clamp_fusion.1.cnt_ref, s32[64]{0:T(128)} %reshape.51.kind_ref, bf16[128,512,256]{2,1,0:T(8,128)(2,1)} %bitcast.80, bf16[8,512,256]{2,1,0:T(8,128)(2,1)} %bitcast.83, f32[8,512,1]{2,1,0:T(8,128)} %reshape.91.ons_ref, ...), custom_call_target="tpu_custom_call" | custom-call | tf_op jit(solution)/shard_map/pallas_call | solution.py:88
  229.5 3.1 convolution_bitcast_fusion.1
  232.6 0.7 convolution_bitcast_fusion.2
  233.4 0.8 reshape.56.x_ref
  234.3 29.8 %shard_map.83 = f32[1024,128]{1,0:T(8,128)} custom-call(f32[1024,128]{1,0:T(8,128)} %reshape.56.x_ref), custom_call_target="tpu_custom_call" | custom-call | tf_op jit(solution)/shard_map/pallas_call | solution.py:181
  264.1 1.1 fusion.14
  265.6 126.9 %while.13 = (s32[]{:T(128)}, f32[512,256]{0,1:T(8,128)S(1)}, f32[512,512]{1,0:T(8,128)S(1)}, s32[]{:T(128)}, s32[]{:T(128)}, /*index=5*/f32[]{:T(128)}, s32[]{:T(128)}) while((s32[]{:T(128)}, f32[512,256]{0,1:T(8,128)S(1)}, f32[512,512]{1,0:T(8,128)S(1)}, s32[]{:T(128)}, s32[]{:T(128)}, /*index=5*/f32[]{:T(128)}, s32[]{:T(128)}) %tuple.52), condition=%wide.region_5.6_spmd, body=%wide.region_0.5_spmd.sunk | while | flops 1561018624 | bytes 9177372 | solution.py:25
  265.8 1.0 fusion.61
  266.8 1.0 fusion.62
  268.1 11.7 %cholesky.185 = f32[128,128]{1,0:T(8,128)S(1)} custom-call(f32[128,128]{1,0:T(8,128)S(1)} %cholesky.184), custom_call_target="Cholesky" | custom-call | tf_op jit(solution)/shard_map/while/body/eval_jaxpr/jit(cholesky)/cholesky | solution.py:20
  279.8 9.8 %custom-call.20 = f32[1,128,128]{1,2,0:T(8,128)S(1)} custom-call(f32[1,128,128]{2,1,0:T(8,128)S(1)} %get-tuple-element.116), custom_call_target="InvertDiagBlocksLowerTriangular" | custom-call | tf_op jit(solution)/shard_map/while/body/eval_jaxpr/jit(cholesky)/cholesky | solution.py:20
  290.1 11.7 %cholesky.187 = f32[128,128]{1,0:T(8,128)S(1)} custom-call(f32[128,128]{1,0:T(8,128)S(1)} %convolution_subtract_fusion.4), custom_call_target="Cholesky" | custom-call | tf_op jit(solution)/shard_map/while/body/eval_jaxpr/jit(cholesky)/cholesky | solution.py:20
  301.9 0.7 compare_reduce_fusion.3
  304.0 4.0 while.14
  304.0 0.6 fusion.66
  304.6 1.3 bitcast_dynamic-update-slice_fusion.2
  306.0 0.6 fusion.66
  306.6 1.3 bitcast_dynamic-update-slice_fusion.2
  308.0 19.7 %custom-call.22 = f32[2,128,128]{1,2,0:T(8,128)S(1)} custom-call(f32[2,128,128]{2,1,0:T(8,128)S(1)} %get-tuple-element.124), custom_call_target="InvertDiagBlocksLowerTriangular" | custom-call | tf_op jit(solution)/shard_map/while/body/eval_jaxpr/triangular_solve | solution.py:21
  328.1 0.6 convolution_subtract_fusion.5
  329.2 1.0 fusion.61
  330.2 1.0 fusion.62
  331.4 11.7 %cholesky.185 = f32[128,128]{1,0:T(8,128)S(1)} custom-call(f32[128,128]{1,0:T(8,128)S(1)} %cholesky.184), custom_call_target="Cholesky" | custom-call | tf_op jit(solution)/shard_map/while/body/eval_jaxpr/jit(cholesky)/cholesky | solution.py:20
  343.2 9.8 %custom-call.20 = f32[1,128,128]{1,2,0:T(8,128)S(1)} custom-call(f32[1,128,128]{2,1,0:T(8,128)S(1)} %get-tuple-element.116), custom_call_target="InvertDiagBlocksLowerTriangular" | custom-call | tf_op jit(solution)/shard_map/while/body/eval_jaxpr/jit(cholesky)/cholesky | solution.py:20
  353.5 11.7 %cholesky.187 = f32[128,128]{1,0:T(8,128)S(1)} custom-call(f32[128,128]{1,0:T(8,128)S(1)} %convolution_subtract_fusion.4), custom_call_target="Cholesky" | custom-call | tf_op jit(solution)/shard_map/while/body/eval_jaxpr/jit(cholesky)/cholesky | solution.py:20
  365.3 0.7 compare_reduce_fusion.3
  367.3 4.0 while.14
  367.3 0.6 fusion.66
  368.0 1.3 bitcast_dynamic-update-slice_fusion.2
  369.4 0.6 fusion.66
  370.0 1.3 bitcast_dynamic-update-slice_fusion.2
  371.4 19.7 %custom-call.22 = f32[2,128,128]{1,2,0:T(8,128)S(1)} custom-call(f32[2,128,128]{2,1,0:T(8,128)S(1)} %get-tuple-element.124), custom_call_target="InvertDiagBlocksLowerTriangular" | custom-call | tf_op jit(solution)/shard_map/while/body/eval_jaxpr/triangular_solve | solution.py:21
  391.5 0.6 convolution_subtract_fusion.5
  392.6 2.5 fusion.11
  395.1 2.1 fusion.8
  (67 shorter events, 4.3 us)
Async XLA Ops:
  6.5 5.5 %copy-start = (bf16[4,512,512]{2,1,0:T(8,128)(2,1)S(1)}, bf16[4,512,512]{2,1,0:T(8,128)(2,1)}, u32[]{:S(2)}) copy-start(bf16[4,512,512]{2,1,0:T(8,128)(2,1)} %param.17) | copy-start | bytes 6291460
  6.5 0.8 copy-start.6
  6.5 1.5 copy-start.7
  6.5 2.2 copy-start.5
  6.5 5.4 %copy-start.8 = (s32[8]{0:T(128)S(1)}, s32[8]{0:T(128)}, u32[]{:S(2)}) copy-start(s32[8]{0:T(128)} %param.16) | copy-start | bytes 100
  6.5 209.0 %all-gather.2.cloned.1.call-start = ((), (), s32[]{:S(2)}) async-start(), calls=%async_computation | async-start | bytes 35651584 | tf_op jit(solution)/shard_map/all_gather | solution.py:228
  19.0 1.3 copy-start.3
  20.4 40.3 %copy-start.9 = (s32[8]{0:T(128)S(1)}, s32[8]{0:T(128)}, u32[]{:S(2)}) copy-start(s32[8]{0:T(128)} %param.13) | copy-start | bytes 100
  229.5 3.1 copy-start.2
  392.6 2.5 copy-start.4
  395.1 2.1 copy-start.1
Sparse Core Ops, SparseCore 0:
  9.5 206.0 all-gather.1

commit v13 on v12

--- a/solution.py
+++ b/solution.py
@@ -233,7 +233,8 @@
     ).reshape(blocks * block_rows, rank_cols)
     moved_gram = lax.dot_general(moved, moved, contract_rows, preferred_element_type=jnp.float32)
     cross_gram = lax.dot_general(moved, bathed, contract_rows, preferred_element_type=jnp.float32)
-    upper = kernel_sum(jnp.concatenate([moved_gram, cross_gram], axis=0), fields, col_count, 0)
+    late_fields = [(4, 2), (5, 4), (0, 16)] if stage_bits == 7 else fields
+    upper = kernel_sum(jnp.concatenate([moved_gram, cross_gram], axis=0), late_fields, col_count, 0)
     moved_sum, cross_sum = upper[:rank_cols], upper[rank_cols:]
     gram_sum = jnp.concatenate(
         [

time: 405 us -> 405 us (level)
  no operation moved by 1% of the time
where the time goes in v13:
time: 405 us; the launch traced here: 404 us
  waiting for transfers between devices  155 us (38%)
  other arithmetic  108 us (27%)
  Pallas kernels  82.4 us (20%)
  matrix products  21.1 us (5%)
  local copies, waits for them, and re-layouts  20.7 us (5%)
  between operations  13.6 us (3%)
    all_gather x1, waiting for transfers between devices, shards(): gathered = lax.all_gather(density_factor, 'col', axis=0, tiled=True)  154 us
    pallas_call x2, Pallas kernels, kernel_sum(): pl.pallas_call(functools.partial(allreduce_kernel, tuple(fields), cols),...  68.2 us
    another operation x12, other arithmetic, sweep(): factor = jnp.linalg.cholesky(inner)  68 us
    another operation x8, other arithmetic, sweep(): lax.linalg.triangular_solve(factor, image, left_side=False, lower=True, t...  39.5 us
    pallas_call x1, Pallas kernels, moved_blocks(): pl.pallas_call(functools.partial(step_kernel, slots), grid_spec=grid_spec...  14.2 us
  transfers between devices with their start and end apart: 1, of which 1 were waited for; matrix products, arithmetic and copies ran while one was open for 4% of the time, Pallas kernels for 9%

profile of v13, /device:TPU:1, one launch (start us, length us, event | category | flops | bytes accessed | tf_op | source)
XLA Modules:
  0.0 404.3 jit_solution(2637187502776237663)
XLA Ops:
  6.6 0.7 all-gather.2.cloned.1.call-update
  7.4 0.7 reshape.50.ids_ref
  8.1 0.7 reshape.51.kind_ref
  8.7 3.3 reshape.91.ons_ref
  12.0 2.9 gather_fusion
  14.9 4.1 %convolution_convert_fusion = bf16[8,512,256]{2,1,0:T(8,128)(2,1)S(1)} fusion(bf16[8,512,512]{2,1,0:T(8,128)(2,1)} %gather_fusion, bf16[8,512,256]{2,1,0:T(8,128)(2,1)} %bitcast.82), kind=kOutput, calls=%fused_computation.31 | convolution fusion | flops 1074790400 | bytes 8388608 | tf_op jit(solution)/shard_map/bij,bjr->bir/dot_general | solution.py:213
  19.0 0.7 convolution_bitcast_fusion
  19.8 0.6 copy-done.3
  20.4 0.8 concatenate.19.x_ref
  21.2 38.3 %shard_map.84 = f32[1024,128]{1,0:T(8,128)} custom-call(f32[1024,128]{1,0:T(8,128)} %concatenate.19.x_ref), custom_call_target="tpu_custom_call" | custom-call | tf_op jit(solution)/shard_map/pallas_call | solution.py:181
  59.5 1.0 slice.67
  60.7 0.6 broadcast_clamp_fusion.1.cnt_ref
  61.2 154.4 %all-gather.2.cloned.1.call-done = bf16[65536,256]{1,0:T(8,128)(2,1)} async-done(((bf16[4096,256]{1,0:T(8,128)(2,1)}), bf16[65536,256]{1,0:T(8,128)(2,1)}) %all-gather.2.cloned.1.call-update) | async-done | bytes 33554448 | tf_op jit(solution)/shard_map/all_gather | solution.py:228
  215.6 14.2 %shard_map.82 = bf16[8,512,256]{2,1,0:T(8,128)(2,1)} custom-call(s32[64]{0:T(128)} %reshape.50.ids_ref, s32[8]{0:T(128)} %broadcast_clamp_fusion.1.cnt_ref, s32[64]{0:T(128)} %reshape.51.kind_ref, bf16[128,512,256]{2,1,0:T(8,128)(2,1)} %bitcast.80, bf16[8,512,256]{2,1,0:T(8,128)(2,1)} %bitcast.83, f32[8,512,1]{2,1,0:T(8,128)} %reshape.91.ons_ref, ...), custom_call_target="tpu_custom_call" | custom-call | tf_op jit(solution)/shard_map/pallas_call | solution.py:88
  229.8 3.1 convolution_bitcast_fusion.1
  232.9 0.7 convolution_bitcast_fusion.2
  233.7 0.8 reshape.56.x_ref
  234.6 29.9 %shard_map.83 = f32[1024,128]{1,0:T(8,128)} custom-call(f32[1024,128]{1,0:T(8,128)} %reshape.56.x_ref), custom_call_target="tpu_custom_call" | custom-call | tf_op jit(solution)/shard_map/pallas_call | solution.py:181
  264.4 1.1 fusion.14
  266.0 126.9 %while.13 = (s32[]{:T(128)}, f32[512,256]{0,1:T(8,128)S(1)}, f32[512,512]{1,0:T(8,128)S(1)}, s32[]{:T(128)}, s32[]{:T(128)}, /*index=5*/f32[]{:T(128)}, s32[]{:T(128)}) while((s32[]{:T(128)}, f32[512,256]{0,1:T(8,128)S(1)}, f32[512,512]{1,0:T(8,128)S(1)}, s32[]{:T(128)}, s32[]{:T(128)}, /*index=5*/f32[]{:T(128)}, s32[]{:T(128)}) %tuple.52), condition=%wide.region_5.6_spmd, body=%wide.region_0.5_spmd.sunk | while | flops 1561018624 | bytes 9177372 | solution.py:25
  266.2 1.0 fusion.61
  267.2 1.0 fusion.62
  268.4 11.7 %cholesky.185 = f32[128,128]{1,0:T(8,128)S(1)} custom-call(f32[128,128]{1,0:T(8,128)S(1)} %cholesky.184), custom_call_target="Cholesky" | custom-call | tf_op jit(solution)/shard_map/while/body/eval_jaxpr/jit(cholesky)/cholesky | solution.py:20
  280.2 9.8 %custom-call.20 = f32[1,128,128]{1,2,0:T(8,128)S(1)} custom-call(f32[1,128,128]{2,1,0:T(8,128)S(1)} %get-tuple-element.116), custom_call_target="InvertDiagBlocksLowerTriangular" | custom-call | tf_op jit(solution)/shard_map/while/body/eval_jaxpr/jit(cholesky)/cholesky | solution.py:20
  290.5 11.7 %cholesky.187 = f32[128,128]{1,0:T(8,128)S(1)} custom-call(f32[128,128]{1,0:T(8,128)S(1)} %convolution_subtract_fusion.4), custom_call_target="Cholesky" | custom-call | tf_op jit(solution)/shard_map/while/body/eval_jaxpr/jit(cholesky)/cholesky | solution.py:20
  302.2 0.7 compare_reduce_fusion.3
  304.3 4.0 while.14
  304.3 0.6 fusion.66
  304.9 1.3 bitcast_dynamic-update-slice_fusion.2
  306.3 0.6 fusion.66
  307.0 1.3 bitcast_dynamic-update-slice_fusion.2
  308.3 19.7 %custom-call.22 = f32[2,128,128]{1,2,0:T(8,128)S(1)} custom-call(f32[2,128,128]{2,1,0:T(8,128)S(1)} %get-tuple-element.124), custom_call_target="InvertDiagBlocksLowerTriangular" | custom-call | tf_op jit(solution)/shard_map/while/body/eval_jaxpr/triangular_solve | solution.py:21
  328.4 0.6 convolution_subtract_fusion.5
  329.5 1.0 fusion.61
  330.5 1.0 fusion.62
  331.8 11.7 %cholesky.185 = f32[128,128]{1,0:T(8,128)S(1)} custom-call(f32[128,128]{1,0:T(8,128)S(1)} %cholesky.184), custom_call_target="Cholesky" | custom-call | tf_op jit(solution)/shard_map/while/body/eval_jaxpr/jit(cholesky)/cholesky | solution.py:20
  343.5 9.8 %custom-call.20 = f32[1,128,128]{1,2,0:T(8,128)S(1)} custom-call(f32[1,128,128]{2,1,0:T(8,128)S(1)} %get-tuple-element.116), custom_call_target="InvertDiagBlocksLowerTriangular" | custom-call | tf_op jit(solution)/shard_map/while/body/eval_jaxpr/jit(cholesky)/cholesky | solution.py:20
  353.8 11.7 %cholesky.187 = f32[128,128]{1,0:T(8,128)S(1)} custom-call(f32[128,128]{1,0:T(8,128)S(1)} %convolution_subtract_fusion.4), custom_call_target="Cholesky" | custom-call | tf_op jit(solution)/shard_map/while/body/eval_jaxpr/jit(cholesky)/cholesky | solution.py:20
  365.6 0.7 compare_reduce_fusion.3
  367.7 4.0 while.14
  367.7 0.6 fusion.66
  368.3 1.3 bitcast_dynamic-update-slice_fusion.2
  369.7 0.6 fusion.66
  370.3 1.3 bitcast_dynamic-update-slice_fusion.2
  371.7 19.7 %custom-call.22 = f32[2,128,128]{1,2,0:T(8,128)S(1)} custom-call(f32[2,128,128]{2,1,0:T(8,128)S(1)} %get-tuple-element.124), custom_call_target="InvertDiagBlocksLowerTriangular" | custom-call | tf_op jit(solution)/shard_map/while/body/eval_jaxpr/triangular_solve | solution.py:21
  391.8 0.6 convolution_subtract_fusion.5
  392.9 2.5 fusion.11
  395.4 2.1 fusion.8
  (67 shorter events, 4.2 us)
Async XLA Ops:
  6.5 5.5 %copy-start = (bf16[4,512,512]{2,1,0:T(8,128)(2,1)S(1)}, bf16[4,512,512]{2,1,0:T(8,128)(2,1)}, u32[]{:S(2)}) copy-start(bf16[4,512,512]{2,1,0:T(8,128)(2,1)} %param.17) | copy-start | bytes 6291460
  6.5 0.8 copy-start.6
  6.5 1.5 copy-start.7
  6.5 2.2 copy-start.5
  6.5 5.4 %copy-start.8 = (s32[8]{0:T(128)S(1)}, s32[8]{0:T(128)}, u32[]{:S(2)}) copy-start(s32[8]{0:T(128)} %param.16) | copy-start | bytes 100
  6.5 209.0 %all-gather.2.cloned.1.call-start = ((), (), s32[]{:S(2)}) async-start(), calls=%async_computation | async-start | bytes 35651584 | tf_op jit(solution)/shard_map/all_gather | solution.py:228
  19.0 1.3 copy-start.3
  20.4 40.3 %copy-start.9 = (s32[8]{0:T(128)S(1)}, s32[8]{0:T(128)}, u32[]{:S(2)}) copy-start(s32[8]{0:T(128)} %param.13) | copy-start | bytes 100
  229.8 3.1 copy-start.2
  392.9 2.5 copy-start.4
  395.4 2.1 copy-start.1
Sparse Core Ops, SparseCore 0:
  9.5 206.0 all-gather.1

commit v14 on v12

--- a/solution.py
+++ b/solution.py
@@ -223,7 +223,8 @@
         fields = [(s, 2) for s in range(stage_bits)]
     bath_flat = bath_gram.reshape(-1, 128)
     bath_flat = jnp.concatenate([bath_flat, jnp.zeros_like(bath_flat)], axis=0)
-    bath_sum = kernel_sum(bath_flat, fields, col_count, 1)[: bath_flat.shape[0] // 2]
+    early_fields = [(4, 2), (5, 4), (0, 16)] if stage_bits == 7 else fields
+    bath_sum = kernel_sum(bath_flat, early_fields, col_count, 1)[: bath_flat.shape[0] // 2]
     bath_sum = bath_sum.reshape(bath_gram.shape)
     gathered = lax.all_gather(density_factor, "col", axis=0, tiled=True)
     group_rows = gathered.reshape(group_blocks, block_rows, rank_cols)

time: 405 us -> 400 us (0.988)
  no operation moved by 1% of the time
where the time goes in v14:
time: 400 us
  waiting for transfers between devices  154 us (38%)
  other arithmetic  108 us (27%)
  Pallas kernels  78.7 us (20%)
  matrix products  21.1 us (5%)
  local copies, waits for them, and re-layouts  20.7 us (5%)
  between operations  13.6 us (3%)
    all_gather x1, waiting for transfers between devices, shards(): gathered = lax.all_gather(density_factor, 'col', axis=0, tiled=True)  153 us
    another operation x12, other arithmetic, sweep(): factor = jnp.linalg.cholesky(inner)  68 us
    pallas_call x2, Pallas kernels, kernel_sum(): pl.pallas_call(functools.partial(allreduce_kernel, tuple(fields), cols),...  65.3 us
    another operation x8, other arithmetic, sweep(): lax.linalg.triangular_solve(factor, image, left_side=False, lower=True, t...  39.5 us
    pallas_call x1, Pallas kernels, moved_blocks(): pl.pallas_call(functools.partial(step_kernel, slots), grid_spec=grid_spec...  13.4 us
  transfers between devices with their start and end apart: 1, of which 1 were waited for; matrix products, arithmetic and copies ran while one was open for 4% of the time, Pallas kernels for 9%

profile of v14, /device:TPU:1, one launch (start us, length us, event | category | flops | bytes accessed | tf_op | source)
XLA Modules:
  0.0 399.7 jit_solution(7983105304642692419)
XLA Ops:
  6.6 0.7 all-gather.2.cloned.1.call-update
  7.4 0.7 reshape.50.ids_ref
  8.1 0.7 reshape.51.kind_ref
  8.7 3.3 reshape.91.ons_ref
  12.0 2.9 gather_fusion
  14.9 4.1 %convolution_convert_fusion = bf16[8,512,256]{2,1,0:T(8,128)(2,1)S(1)} fusion(bf16[8,512,512]{2,1,0:T(8,128)(2,1)} %gather_fusion, bf16[8,512,256]{2,1,0:T(8,128)(2,1)} %bitcast.82), kind=kOutput, calls=%fused_computation.31 | convolution fusion | flops 1074790400 | bytes 8388608 | tf_op jit(solution)/shard_map/bij,bjr->bir/dot_general | solution.py:213
  19.0 0.7 convolution_bitcast_fusion
  19.8 0.6 copy-done.3
  20.4 0.8 concatenate.19.x_ref
  21.2 35.1 %shard_map.84 = f32[1024,128]{1,0:T(8,128)} custom-call(f32[1024,128]{1,0:T(8,128)} %concatenate.19.x_ref), custom_call_target="tpu_custom_call" | custom-call | tf_op jit(solution)/shard_map/pallas_call | solution.py:181
  56.3 1.0 slice.67
  57.4 0.6 broadcast_clamp_fusion.1.cnt_ref
  58.0 153.4 %all-gather.2.cloned.1.call-done = bf16[65536,256]{1,0:T(8,128)(2,1)} async-done(((bf16[4096,256]{1,0:T(8,128)(2,1)}), bf16[65536,256]{1,0:T(8,128)(2,1)}) %all-gather.2.cloned.1.call-update) | async-done | bytes 33554448 | tf_op jit(solution)/shard_map/all_gather | solution.py:229
  211.4 13.4 %shard_map.82 = bf16[8,512,256]{2,1,0:T(8,128)(2,1)} custom-call(s32[64]{0:T(128)} %reshape.50.ids_ref, s32[8]{0:T(128)} %broadcast_clamp_fusion.1.cnt_ref, s32[64]{0:T(128)} %reshape.51.kind_ref, bf16[128,512,256]{2,1,0:T(8,128)(2,1)} %bitcast.80, bf16[8,512,256]{2,1,0:T(8,128)(2,1)} %bitcast.83, f32[8,512,1]{2,1,0:T(8,128)} %reshape.91.ons_ref, ...), custom_call_target="tpu_custom_call" | custom-call | tf_op jit(solution)/shard_map/pallas_call | solution.py:88
  224.8 3.1 convolution_bitcast_fusion.1
  227.9 0.7 convolution_bitcast_fusion.2
  228.7 0.8 reshape.56.x_ref
  229.6 30.2 %shard_map.83 = f32[1024,128]{1,0:T(8,128)} custom-call(f32[1024,128]{1,0:T(8,128)} %reshape.56.x_ref), custom_call_target="tpu_custom_call" | custom-call | tf_op jit(solution)/shard_map/pallas_call | solution.py:181
  259.8 1.1 fusion.14
  261.3 126.9 %while.13 = (s32[]{:T(128)}, f32[512,256]{0,1:T(8,128)S(1)}, f32[512,512]{1,0:T(8,128)S(1)}, s32[]{:T(128)}, s32[]{:T(128)}, /*index=5*/f32[]{:T(128)}, s32[]{:T(128)}) while((s32[]{:T(128)}, f32[512,256]{0,1:T(8,128)S(1)}, f32[512,512]{1,0:T(8,128)S(1)}, s32[]{:T(128)}, s32[]{:T(128)}, /*index=5*/f32[]{:T(128)}, s32[]{:T(128)}) %tuple.52), condition=%wide.region_5.6_spmd, body=%wide.region_0.5_spmd.sunk | while | flops 1561018624 | bytes 9177372 | solution.py:25
  261.5 1.0 fusion.61
  262.5 1.0 fusion.62
  263.8 11.7 %cholesky.185 = f32[128,128]{1,0:T(8,128)S(1)} custom-call(f32[128,128]{1,0:T(8,128)S(1)} %cholesky.184), custom_call_target="Cholesky" | custom-call | tf_op jit(solution)/shard_map/while/body/eval_jaxpr/jit(cholesky)/cholesky | solution.py:20
  275.5 9.8 %custom-call.20 = f32[1,128,128]{1,2,0:T(8,128)S(1)} custom-call(f32[1,128,128]{2,1,0:T(8,128)S(1)} %get-tuple-element.116), custom_call_target="InvertDiagBlocksLowerTriangular" | custom-call | tf_op jit(solution)/shard_map/while/body/eval_jaxpr/jit(cholesky)/cholesky | solution.py:20
  285.8 11.7 %cholesky.187 = f32[128,128]{1,0:T(8,128)S(1)} custom-call(f32[128,128]{1,0:T(8,128)S(1)} %convolution_subtract_fusion.4), custom_call_target="Cholesky" | custom-call | tf_op jit(solution)/shard_map/while/body/eval_jaxpr/jit(cholesky)/cholesky | solution.py:20
  297.6 0.7 compare_reduce_fusion.3
  299.7 4.0 %while.14 = (s32[]{:T(128)}, f32[256,256]{1,0:T(8,128)S(1)}, s32[2,2]{1,0:T(2,128)S(1)}, f32[2,128,128]{2,1,0:T(8,128)S(1)}, s32[]{:T(128)}) while((s32[]{:T(128)}, f32[256,256]{1,0:T(8,128)S(1)}, s32[2,2]{1,0:T(2,128)S(1)}, f32[2,128,128]{2,1,0:T(8,128)S(1)}, s32[]{:T(128)}) %tuple.49), condition=%wide.while_cond, body=%wide.while_body.sunk | while | flops 2 | bytes 131189 | solution.py:21
  299.7 0.6 fusion.66
  300.3 1.3 bitcast_dynamic-update-slice_fusion.2
  301.7 0.6 fusion.66
  302.3 1.3 bitcast_dynamic-update-slice_fusion.2
  303.7 19.7 %custom-call.22 = f32[2,128,128]{1,2,0:T(8,128)S(1)} custom-call(f32[2,128,128]{2,1,0:T(8,128)S(1)} %get-tuple-element.124), custom_call_target="InvertDiagBlocksLowerTriangular" | custom-call | tf_op jit(solution)/shard_map/while/body/eval_jaxpr/triangular_solve | solution.py:21
  323.8 0.6 convolution_subtract_fusion.5
  324.9 1.0 fusion.61
  325.9 1.0 fusion.62
  327.1 11.7 %cholesky.185 = f32[128,128]{1,0:T(8,128)S(1)} custom-call(f32[128,128]{1,0:T(8,128)S(1)} %cholesky.184), custom_call_target="Cholesky" | custom-call | tf_op jit(solution)/shard_map/while/body/eval_jaxpr/jit(cholesky)/cholesky | solution.py:20
  338.9 9.8 %custom-call.20 = f32[1,128,128]{1,2,0:T(8,128)S(1)} custom-call(f32[1,128,128]{2,1,0:T(8,128)S(1)} %get-tuple-element.116), custom_call_target="InvertDiagBlocksLowerTriangular" | custom-call | tf_op jit(solution)/shard_map/while/body/eval_jaxpr/jit(cholesky)/cholesky | solution.py:20
  349.2 11.7 %cholesky.187 = f32[128,128]{1,0:T(8,128)S(1)} custom-call(f32[128,128]{1,0:T(8,128)S(1)} %convolution_subtract_fusion.4), custom_call_target="Cholesky" | custom-call | tf_op jit(solution)/shard_map/while/body/eval_jaxpr/jit(cholesky)/cholesky | solution.py:20
  360.9 0.7 compare_reduce_fusion.3
  363.0 4.0 %while.14 = (s32[]{:T(128)}, f32[256,256]{1,0:T(8,128)S(1)}, s32[2,2]{1,0:T(2,128)S(1)}, f32[2,128,128]{2,1,0:T(8,128)S(1)}, s32[]{:T(128)}) while((s32[]{:T(128)}, f32[256,256]{1,0:T(8,128)S(1)}, s32[2,2]{1,0:T(2,128)S(1)}, f32[2,128,128]{2,1,0:T(8,128)S(1)}, s32[]{:T(128)}) %tuple.49), condition=%wide.while_cond, body=%wide.while_body.sunk | while | flops 2 | bytes 131189 | solution.py:21
  363.0 0.6 fusion.66
  363.7 1.3 bitcast_dynamic-update-slice_fusion.2
  365.0 0.6 fusion.66
  365.7 1.3 bitcast_dynamic-update-slice_fusion.2
  367.0 19.7 %custom-call.22 = f32[2,128,128]{1,2,0:T(8,128)S(1)} custom-call(f32[2,128,128]{2,1,0:T(8,128)S(1)} %get-tuple-element.124), custom_call_target="InvertDiagBlocksLowerTriangular" | custom-call | tf_op jit(solution)/shard_map/while/body/eval_jaxpr/triangular_solve | solution.py:21
  387.2 0.6 convolution_subtract_fusion.5
  388.3 2.5 fusion.11
  390.8 2.1 fusion.8
  (67 shorter events, 4.2 us)
Async XLA Ops:
  6.5 5.5 %copy-start = (bf16[4,512,512]{2,1,0:T(8,128)(2,1)S(1)}, bf16[4,512,512]{2,1,0:T(8,128)(2,1)}, u32[]{:S(2)}) copy-start(bf16[4,512,512]{2,1,0:T(8,128)(2,1)} %param.17) | copy-start | bytes 6291460
  6.5 0.8 copy-start.6
  6.5 1.5 copy-start.7
  6.5 2.2 copy-start.5
  6.5 5.4 %copy-start.8 = (s32[8]{0:T(128)S(1)}, s32[8]{0:T(128)}, u32[]{:S(2)}) copy-start(s32[8]{0:T(128)} %param.16) | copy-start | bytes 100
  6.5 204.8 %all-gather.2.cloned.1.call-start = ((), (), s32[]{:S(2)}) async-start(), calls=%async_computation | async-start | bytes 35651584 | tf_op jit(solution)/shard_map/all_gather | solution.py:229
  19.0 1.3 copy-start.3
  20.4 37.0 %copy-start.9 = (s32[8]{0:T(128)S(1)}, s32[8]{0:T(128)}, u32[]{:S(2)}) copy-start(s32[8]{0:T(128)} %param.13) | copy-start | bytes 100
  224.8 3.1 copy-start.2
  388.3 2.5 copy-start.4
  390.8 2.1 copy-start.1
Sparse Core Ops, SparseCore 0:
  9.5 201.8 all-gather.1

commit v15 on v14

--- a/solution.py
+++ b/solution.py
@@ -234,7 +234,8 @@
     ).reshape(blocks * block_rows, rank_cols)
     moved_gram = lax.dot_general(moved, moved, contract_rows, preferred_element_type=jnp.float32)
     cross_gram = lax.dot_general(moved, bathed, contract_rows, preferred_element_type=jnp.float32)
-    upper = kernel_sum(jnp.concatenate([moved_gram, cross_gram], axis=0), fields, col_count, 0)
+    late_fields = [(4, 8), (0, 16)] if stage_bits == 7 else fields
+    upper = kernel_sum(jnp.concatenate([moved_gram, cross_gram], axis=0), late_fields, col_count, 0)
     moved_sum, cross_sum = upper[:rank_cols], upper[rank_cols:]
     gram_sum = jnp.concatenate(
         [

time: 400 us -> 402 us (level)
  no operation moved by 1% of the time
where the time goes in v15:
time: 402 us; the launch traced here: 401 us
  waiting for transfers between devices  154 us (38%)
  other arithmetic  108 us (27%)
  Pallas kernels  80.3 us (20%)
  matrix products  21.1 us (5%)
  local copies, waits for them, and re-layouts  20.7 us (5%)
  between operations  13.6 us (3%)
    all_gather x1, waiting for transfers between devices, shards(): gathered = lax.all_gather(density_factor, 'col', axis=0, tiled=True)  153 us
    another operation x12, other arithmetic, sweep(): factor = jnp.linalg.cholesky(inner)  68 us
    pallas_call x2, Pallas kernels, kernel_sum(): pl.pallas_call(functools.partial(allreduce_kernel, tuple(fields), cols),...  66.1 us
    another operation x8, other arithmetic, sweep(): lax.linalg.triangular_solve(factor, image, left_side=False, lower=True, t...  39.5 us
    pallas_call x1, Pallas kernels, moved_blocks(): pl.pallas_call(functools.partial(step_kernel, slots), grid_spec=grid_spec...  14.1 us
  transfers between devices with their start and end apart: 1, of which 1 were waited for; matrix products, arithmetic and copies ran while one was open for 4% of the time, Pallas kernels for 9%

profile of v15, /device:TPU:1, one launch (start us, length us, event | category | flops | bytes accessed | tf_op | source)
XLA Modules:
  0.0 401.3 jit_solution(15109313657126865633)
XLA Ops:
  6.6 0.7 all-gather.2.cloned.1.call-update
  7.4 0.7 reshape.50.ids_ref
  8.1 0.7 reshape.51.kind_ref
  8.7 3.3 reshape.91.ons_ref
  12.0 2.9 gather_fusion
  14.9 4.1 %convolution_convert_fusion = bf16[8,512,256]{2,1,0:T(8,128)(2,1)S(1)} fusion(bf16[8,512,512]{2,1,0:T(8,128)(2,1)} %gather_fusion, bf16[8,512,256]{2,1,0:T(8,128)(2,1)} %bitcast.82), kind=kOutput, calls=%fused_computation.31 | convolution fusion | flops 1074790400 | bytes 8388608 | tf_op jit(solution)/shard_map/bij,bjr->bir/dot_general | solution.py:213
  19.0 0.7 convolution_bitcast_fusion
  19.8 0.6 copy-done.3
  20.4 0.8 concatenate.19.x_ref
  21.2 35.1 %shard_map.84 = f32[1024,128]{1,0:T(8,128)} custom-call(f32[1024,128]{1,0:T(8,128)} %concatenate.19.x_ref), custom_call_target="tpu_custom_call" | custom-call | tf_op jit(solution)/shard_map/pallas_call | solution.py:181
  56.3 1.0 slice.67
  57.4 0.6 broadcast_clamp_fusion.1.cnt_ref
  58.0 153.4 %all-gather.2.cloned.1.call-done = bf16[65536,256]{1,0:T(8,128)(2,1)} async-done(((bf16[4096,256]{1,0:T(8,128)(2,1)}), bf16[65536,256]{1,0:T(8,128)(2,1)}) %all-gather.2.cloned.1.call-update) | async-done | bytes 33554448 | tf_op jit(solution)/shard_map/all_gather | solution.py:229
  211.4 14.1 %shard_map.82 = bf16[8,512,256]{2,1,0:T(8,128)(2,1)} custom-call(s32[64]{0:T(128)} %reshape.50.ids_ref, s32[8]{0:T(128)} %broadcast_clamp_fusion.1.cnt_ref, s32[64]{0:T(128)} %reshape.51.kind_ref, bf16[128,512,256]{2,1,0:T(8,128)(2,1)} %bitcast.80, bf16[8,512,256]{2,1,0:T(8,128)(2,1)} %bitcast.83, f32[8,512,1]{2,1,0:T(8,128)} %reshape.91.ons_ref, ...), custom_call_target="tpu_custom_call" | custom-call | tf_op jit(solution)/shard_map/pallas_call | solution.py:88
  225.5 3.1 convolution_bitcast_fusion.1
  228.7 0.7 convolution_bitcast_fusion.2
  229.5 0.8 reshape.56.x_ref
  230.3 31.1 %shard_map.83 = f32[1024,128]{1,0:T(8,128)} custom-call(f32[1024,128]{1,0:T(8,128)} %reshape.56.x_ref), custom_call_target="tpu_custom_call" | custom-call | tf_op jit(solution)/shard_map/pallas_call | solution.py:181
  261.4 1.1 fusion.14
  262.9 126.9 %while.13 = (s32[]{:T(128)}, f32[512,256]{0,1:T(8,128)S(1)}, f32[512,512]{1,0:T(8,128)S(1)}, s32[]{:T(128)}, s32[]{:T(128)}, /*index=5*/f32[]{:T(128)}, s32[]{:T(128)}) while((s32[]{:T(128)}, f32[512,256]{0,1:T(8,128)S(1)}, f32[512,512]{1,0:T(8,128)S(1)}, s32[]{:T(128)}, s32[]{:T(128)}, /*index=5*/f32[]{:T(128)}, s32[]{:T(128)}) %tuple.52), condition=%wide.region_5.6_spmd, body=%wide.region_0.5_spmd.sunk | while | flops 1561018624 | bytes 9177372 | solution.py:25
  263.1 1.0 fusion.61
  264.1 1.0 fusion.62
  265.4 11.7 %cholesky.185 = f32[128,128]{1,0:T(8,128)S(1)} custom-call(f32[128,128]{1,0:T(8,128)S(1)} %cholesky.184), custom_call_target="Cholesky" | custom-call | tf_op jit(solution)/shard_map/while/body/eval_jaxpr/jit(cholesky)/cholesky | solution.py:20
  277.1 9.8 %custom-call.20 = f32[1,128,128]{1,2,0:T(8,128)S(1)} custom-call(f32[1,128,128]{2,1,0:T(8,128)S(1)} %get-tuple-element.116), custom_call_target="InvertDiagBlocksLowerTriangular" | custom-call | tf_op jit(solution)/shard_map/while/body/eval_jaxpr/jit(cholesky)/cholesky | solution.py:20
  287.4 11.7 %cholesky.187 = f32[128,128]{1,0:T(8,128)S(1)} custom-call(f32[128,128]{1,0:T(8,128)S(1)} %convolution_subtract_fusion.4), custom_call_target="Cholesky" | custom-call | tf_op jit(solution)/shard_map/while/body/eval_jaxpr/jit(cholesky)/cholesky | solution.py:20
  299.2 0.7 compare_reduce_fusion.3
  301.3 4.0 %while.14 = (s32[]{:T(128)}, f32[256,256]{1,0:T(8,128)S(1)}, s32[2,2]{1,0:T(2,128)S(1)}, f32[2,128,128]{2,1,0:T(8,128)S(1)}, s32[]{:T(128)}) while((s32[]{:T(128)}, f32[256,256]{1,0:T(8,128)S(1)}, s32[2,2]{1,0:T(2,128)S(1)}, f32[2,128,128]{2,1,0:T(8,128)S(1)}, s32[]{:T(128)}) %tuple.49), condition=%wide.while_cond, body=%wide.while_body.sunk | while | flops 2 | bytes 131189 | solution.py:21
  301.3 0.6 fusion.66
  301.9 1.3 bitcast_dynamic-update-slice_fusion.2
  303.3 0.6 fusion.66
  303.9 1.3 bitcast_dynamic-update-slice_fusion.2
  305.3 19.7 %custom-call.22 = f32[2,128,128]{1,2,0:T(8,128)S(1)} custom-call(f32[2,128,128]{2,1,0:T(8,128)S(1)} %get-tuple-element.124), custom_call_target="InvertDiagBlocksLowerTriangular" | custom-call | tf_op jit(solution)/shard_map/while/body/eval_jaxpr/triangular_solve | solution.py:21
  325.4 0.6 convolution_subtract_fusion.5
  326.5 1.0 fusion.61
  327.5 1.0 fusion.62
  328.7 11.7 %cholesky.185 = f32[128,128]{1,0:T(8,128)S(1)} custom-call(f32[128,128]{1,0:T(8,128)S(1)} %cholesky.184), custom_call_target="Cholesky" | custom-call | tf_op jit(solution)/shard_map/while/body/eval_jaxpr/jit(cholesky)/cholesky | solution.py:20
  340.5 9.8 %custom-call.20 = f32[1,128,128]{1,2,0:T(8,128)S(1)} custom-call(f32[1,128,128]{2,1,0:T(8,128)S(1)} %get-tuple-element.116), custom_call_target="InvertDiagBlocksLowerTriangular" | custom-call | tf_op jit(solution)/shard_map/while/body/eval_jaxpr/jit(cholesky)/cholesky | solution.py:20
  350.8 11.7 %cholesky.187 = f32[128,128]{1,0:T(8,128)S(1)} custom-call(f32[128,128]{1,0:T(8,128)S(1)} %convolution_subtract_fusion.4), custom_call_target="Cholesky" | custom-call | tf_op jit(solution)/shard_map/while/body/eval_jaxpr/jit(cholesky)/cholesky | solution.py:20
  362.5 0.7 compare_reduce_fusion.3
  364.6 4.0 %while.14 = (s32[]{:T(128)}, f32[256,256]{1,0:T(8,128)S(1)}, s32[2,2]{1,0:T(2,128)S(1)}, f32[2,128,128]{2,1,0:T(8,128)S(1)}, s32[]{:T(128)}) while((s32[]{:T(128)}, f32[256,256]{1,0:T(8,128)S(1)}, s32[2,2]{1,0:T(2,128)S(1)}, f32[2,128,128]{2,1,0:T(8,128)S(1)}, s32[]{:T(128)}) %tuple.49), condition=%wide.while_cond, body=%wide.while_body.sunk | while | flops 2 | bytes 131189 | solution.py:21
  364.6 0.6 fusion.66
  365.3 1.3 bitcast_dynamic-update-slice_fusion.2
  366.6 0.6 fusion.66
  367.3 1.3 bitcast_dynamic-update-slice_fusion.2
  368.6 19.7 %custom-call.22 = f32[2,128,128]{1,2,0:T(8,128)S(1)} custom-call(f32[2,128,128]{2,1,0:T(8,128)S(1)} %get-tuple-element.124), custom_call_target="InvertDiagBlocksLowerTriangular" | custom-call | tf_op jit(solution)/shard_map/while/body/eval_jaxpr/triangular_solve | solution.py:21
  388.7 0.6 convolution_subtract_fusion.5
  389.9 2.5 fusion.11
  392.4 2.1 fusion.8
  (67 shorter events, 4.2 us)
Async XLA Ops:
  6.5 5.5 %copy-start = (bf16[4,512,512]{2,1,0:T(8,128)(2,1)S(1)}, bf16[4,512,512]{2,1,0:T(8,128)(2,1)}, u32[]{:S(2)}) copy-start(bf16[4,512,512]{2,1,0:T(8,128)(2,1)} %param.17) | copy-start | bytes 6291460
  6.5 0.8 copy-start.6
  6.5 1.5 copy-start.7
  6.5 2.2 copy-start.5
  6.5 5.4 %copy-start.8 = (s32[8]{0:T(128)S(1)}, s32[8]{0:T(128)}, u32[]{:S(2)}) copy-start(s32[8]{0:T(128)} %param.16) | copy-start | bytes 100
  6.5 204.8 %all-gather.2.cloned.1.call-start = ((), (), s32[]{:S(2)}) async-start(), calls=%async_computation | async-start | bytes 35651584 | tf_op jit(solution)/shard_map/all_gather | solution.py:229
  19.0 1.3 copy-start.3
  20.4 37.0 %copy-start.9 = (s32[8]{0:T(128)S(1)}, s32[8]{0:T(128)}, u32[]{:S(2)}) copy-start(s32[8]{0:T(128)} %param.13) | copy-start | bytes 100
  225.5 3.1 copy-start.2
  389.9 2.5 copy-start.4
  392.4 2.1 copy-start.1
Sparse Core Ops, SparseCore 0:
  9.5 201.8 all-gather.1

commit v16 on v14

--- a/solution.py
+++ b/solution.py
@@ -26,7 +26,7 @@
 
 
 def step_kernel(slots, ids_ref, cnt_ref, kind_ref,
-                group_hbm, own_ref, ons_ref, cpl_ref, out_ref, buf, sems, acc):
+                group_hbm, own_ref, ons_ref, cpl_hbm, out_ref, buf, sems, acc, cpl_ref, cpl_sem):
     b = pl.program_id(0)
     last = pl.num_programs(0) - 1
     rank_cols = own_ref.shape[2]
@@ -42,6 +42,7 @@
     @pl.when(b == 0)
     def _():
         fetch(0, 0)
+        pltpu.make_async_copy(cpl_hbm, cpl_ref, cpl_sem).start()
 
     @pl.when(b < last)
     def _():
@@ -55,6 +56,10 @@
             pltpu.make_async_copy(group_hbm.at[0], buf.at[slot, k], sems.at[slot, k]).wait()
             t = kind_ref[b * slots + k]
             acc[t] += buf[slot, k].astype(jnp.float32)
+
+    @pl.when(b == 0)
+    def _():
+        pltpu.make_async_copy(cpl_hbm, cpl_ref, cpl_sem).wait()
 
     coupled = jnp.dot(cpl_ref[0], acc[0].astype(jnp.bfloat16), preferred_element_type=jnp.float32)
     for t in range(1, cpl_ref.shape[0]):
@@ -76,13 +81,15 @@
             pl.BlockSpec(memory_space=pl.ANY),
             pl.BlockSpec((1, block_rows, rank_cols), lambda b, *_: (b, 0, 0)),
             pl.BlockSpec((1, block_rows, 1), lambda b, *_: (b, 0, 0)),
-            pl.BlockSpec((kinds_n, block_rows, block_rows), lambda b, *_: (0, 0, 0)),
+            pl.BlockSpec(memory_space=pl.ANY),
         ],
         out_specs=pl.BlockSpec((1, block_rows, rank_cols), lambda b, *_: (b, 0, 0)),
         scratch_shapes=[
             pltpu.VMEM((2, slots, block_rows, rank_cols), group_rows.dtype),
             pltpu.SemaphoreType.DMA((2, slots)),
             pltpu.VMEM((kinds_n, block_rows, rank_cols), jnp.float32),
+            pltpu.VMEM(coupling_blocks.shape, coupling_blocks.dtype),
+            pltpu.SemaphoreType.DMA(()),
         ],
     )
     return pl.pallas_call(

time: 400 us -> 400 us (level)
  no operation moved by 1% of the time
where the time goes in v16:
time: 400 us
  waiting for transfers between devices  154 us (38%)
  other arithmetic  108 us (27%)
  Pallas kernels  78.7 us (20%)
  matrix products  21.1 us (5%)
  local copies, waits for them, and re-layouts  20.7 us (5%)
  between operations  13.6 us (3%)
    all_gather x1, waiting for transfers between devices, shards(): gathered = lax.all_gather(density_factor, 'col', axis=0, tiled=True)  153 us
    another operation x12, other arithmetic, sweep(): factor = jnp.linalg.cholesky(inner)  68 us
    pallas_call x2, Pallas kernels, kernel_sum(): pl.pallas_call(functools.partial(allreduce_kernel, tuple(fields), cols),...  65.7 us
    another operation x8, other arithmetic, sweep(): lax.linalg.triangular_solve(factor, image, left_side=False, lower=True, t...  39.5 us
    pallas_call x1, Pallas kernels, moved_blocks(): pl.pallas_call(functools.partial(step_kernel, slots), grid_spec=grid_spec...  13 us
  transfers between devices with their start and end apart: 1, of which 1 were waited for; matrix products, arithmetic and copies ran while one was open for 4% of the time, Pallas kernels for 9%

profile of v16, /device:TPU:1, one launch (start us, length us, event | category | flops | bytes accessed | tf_op | source)
XLA Modules:
  0.0 399.7 jit_solution(16529451740325052708)
XLA Ops:
  6.6 0.7 all-gather.2.cloned.1.call-update
  7.4 0.7 reshape.50.ids_ref
  8.1 0.7 reshape.51.kind_ref
  8.7 3.3 reshape.91.ons_ref
  12.0 2.9 gather_fusion
  14.9 4.1 %convolution_convert_fusion = bf16[8,512,256]{2,1,0:T(8,128)(2,1)S(1)} fusion(bf16[8,512,512]{2,1,0:T(8,128)(2,1)} %gather_fusion, bf16[8,512,256]{2,1,0:T(8,128)(2,1)} %bitcast.82), kind=kOutput, calls=%fused_computation.31 | convolution fusion | flops 1074790400 | bytes 8388608 | tf_op jit(solution)/shard_map/bij,bjr->bir/dot_general | solution.py:220
  19.0 0.7 convolution_bitcast_fusion
  19.8 0.6 copy-done.3
  20.4 0.8 concatenate.19.x_ref
  21.2 35.1 %shard_map.84 = f32[1024,128]{1,0:T(8,128)} custom-call(f32[1024,128]{1,0:T(8,128)} %concatenate.19.x_ref), custom_call_target="tpu_custom_call" | custom-call | tf_op jit(solution)/shard_map/pallas_call | solution.py:188
  56.3 1.0 slice.67
  57.4 0.6 broadcast_clamp_fusion.1.cnt_ref
  58.0 153.4 %all-gather.2.cloned.1.call-done = bf16[65536,256]{1,0:T(8,128)(2,1)} async-done(((bf16[4096,256]{1,0:T(8,128)(2,1)}), bf16[65536,256]{1,0:T(8,128)(2,1)}) %all-gather.2.cloned.1.call-update) | async-done | bytes 33554448 | tf_op jit(solution)/shard_map/all_gather | solution.py:236
  211.4 13.0 %shard_map.82 = bf16[8,512,256]{2,1,0:T(8,128)(2,1)} custom-call(s32[64]{0:T(128)} %reshape.50.ids_ref, s32[8]{0:T(128)} %broadcast_clamp_fusion.1.cnt_ref, s32[64]{0:T(128)} %reshape.51.kind_ref, bf16[128,512,256]{2,1,0:T(8,128)(2,1)} %bitcast.80, bf16[8,512,256]{2,1,0:T(8,128)(2,1)} %bitcast.83, f32[8,512,1]{2,1,0:T(8,128)} %reshape.91.ons_ref, ...), custom_call_target="tpu_custom_call" | custom-call | tf_op jit(solution)/shard_map/pallas_call | solution.py:95
  224.4 3.1 convolution_bitcast_fusion.1
  227.5 0.7 convolution_bitcast_fusion.2
  228.3 0.8 reshape.56.x_ref
  229.2 30.7 %shard_map.83 = f32[1024,128]{1,0:T(8,128)} custom-call(f32[1024,128]{1,0:T(8,128)} %reshape.56.x_ref), custom_call_target="tpu_custom_call" | custom-call | tf_op jit(solution)/shard_map/pallas_call | solution.py:188
  259.8 1.1 fusion.14
  261.3 126.9 %while.13 = (s32[]{:T(128)}, f32[512,256]{0,1:T(8,128)S(1)}, f32[512,512]{1,0:T(8,128)S(1)}, s32[]{:T(128)}, s32[]{:T(128)}, /*index=5*/f32[]{:T(128)}, s32[]{:T(128)}) while((s32[]{:T(128)}, f32[512,256]{0,1:T(8,128)S(1)}, f32[512,512]{1,0:T(8,128)S(1)}, s32[]{:T(128)}, s32[]{:T(128)}, /*index=5*/f32[]{:T(128)}, s32[]{:T(128)}) %tuple.52), condition=%wide.region_5.6_spmd, body=%wide.region_0.5_spmd.sunk | while | flops 1561018624 | bytes 9177372 | solution.py:25
  261.5 1.0 fusion.61
  262.6 1.0 fusion.62
  263.8 11.7 %cholesky.185 = f32[128,128]{1,0:T(8,128)S(1)} custom-call(f32[128,128]{1,0:T(8,128)S(1)} %cholesky.184), custom_call_target="Cholesky" | custom-call | tf_op jit(solution)/shard_map/while/body/eval_jaxpr/jit(cholesky)/cholesky | solution.py:20
  275.6 9.8 %custom-call.20 = f32[1,128,128]{1,2,0:T(8,128)S(1)} custom-call(f32[1,128,128]{2,1,0:T(8,128)S(1)} %get-tuple-element.116), custom_call_target="InvertDiagBlocksLowerTriangular" | custom-call | tf_op jit(solution)/shard_map/while/body/eval_jaxpr/jit(cholesky)/cholesky | solution.py:20
  285.8 11.7 %cholesky.187 = f32[128,128]{1,0:T(8,128)S(1)} custom-call(f32[128,128]{1,0:T(8,128)S(1)} %convolution_subtract_fusion.4), custom_call_target="Cholesky" | custom-call | tf_op jit(solution)/shard_map/while/body/eval_jaxpr/jit(cholesky)/cholesky | solution.py:20
  297.6 0.7 compare_reduce_fusion.3
  299.7 4.0 %while.14 = (s32[]{:T(128)}, f32[256,256]{1,0:T(8,128)S(1)}, s32[2,2]{1,0:T(2,128)S(1)}, f32[2,128,128]{2,1,0:T(8,128)S(1)}, s32[]{:T(128)}) while((s32[]{:T(128)}, f32[256,256]{1,0:T(8,128)S(1)}, s32[2,2]{1,0:T(2,128)S(1)}, f32[2,128,128]{2,1,0:T(8,128)S(1)}, s32[]{:T(128)}) %tuple.49), condition=%wide.while_cond, body=%wide.while_body.sunk | while | flops 2 | bytes 131189 | solution.py:21
  299.7 0.6 fusion.66
  300.3 1.3 bitcast_dynamic-update-slice_fusion.2
  301.7 0.6 fusion.66
  302.3 1.3 bitcast_dynamic-update-slice_fusion.2
  303.7 19.7 %custom-call.22 = f32[2,128,128]{1,2,0:T(8,128)S(1)} custom-call(f32[2,128,128]{2,1,0:T(8,128)S(1)} %get-tuple-element.124), custom_call_target="InvertDiagBlocksLowerTriangular" | custom-call | tf_op jit(solution)/shard_map/while/body/eval_jaxpr/triangular_solve | solution.py:21
  323.8 0.6 convolution_subtract_fusion.5
  324.9 1.0 fusion.61
  325.9 1.0 fusion.62
  327.1 11.7 %cholesky.185 = f32[128,128]{1,0:T(8,128)S(1)} custom-call(f32[128,128]{1,0:T(8,128)S(1)} %cholesky.184), custom_call_target="Cholesky" | custom-call | tf_op jit(solution)/shard_map/while/body/eval_jaxpr/jit(cholesky)/cholesky | solution.py:20
  338.9 9.8 %custom-call.20 = f32[1,128,128]{1,2,0:T(8,128)S(1)} custom-call(f32[1,128,128]{2,1,0:T(8,128)S(1)} %get-tuple-element.116), custom_call_target="InvertDiagBlocksLowerTriangular" | custom-call | tf_op jit(solution)/shard_map/while/body/eval_jaxpr/jit(cholesky)/cholesky | solution.py:20
  349.2 11.7 %cholesky.187 = f32[128,128]{1,0:T(8,128)S(1)} custom-call(f32[128,128]{1,0:T(8,128)S(1)} %convolution_subtract_fusion.4), custom_call_target="Cholesky" | custom-call | tf_op jit(solution)/shard_map/while/body/eval_jaxpr/jit(cholesky)/cholesky | solution.py:20
  361.0 0.7 compare_reduce_fusion.3
  363.0 4.0 %while.14 = (s32[]{:T(128)}, f32[256,256]{1,0:T(8,128)S(1)}, s32[2,2]{1,0:T(2,128)S(1)}, f32[2,128,128]{2,1,0:T(8,128)S(1)}, s32[]{:T(128)}) while((s32[]{:T(128)}, f32[256,256]{1,0:T(8,128)S(1)}, s32[2,2]{1,0:T(2,128)S(1)}, f32[2,128,128]{2,1,0:T(8,128)S(1)}, s32[]{:T(128)}) %tuple.49), condition=%wide.while_cond, body=%wide.while_body.sunk | while | flops 2 | bytes 131189 | solution.py:21
  363.0 0.6 fusion.66
  363.7 1.3 bitcast_dynamic-update-slice_fusion.2
  365.1 0.6 fusion.66
  365.7 1.3 bitcast_dynamic-update-slice_fusion.2
  367.1 19.7 %custom-call.22 = f32[2,128,128]{1,2,0:T(8,128)S(1)} custom-call(f32[2,128,128]{2,1,0:T(8,128)S(1)} %get-tuple-element.124), custom_call_target="InvertDiagBlocksLowerTriangular" | custom-call | tf_op jit(solution)/shard_map/while/body/eval_jaxpr/triangular_solve | solution.py:21
  387.2 0.6 convolution_subtract_fusion.5
  388.3 2.5 fusion.11
  390.8 2.1 fusion.8
  (67 shorter events, 4.2 us)
Async XLA Ops:
  6.5 5.5 %copy-start = (bf16[4,512,512]{2,1,0:T(8,128)(2,1)S(1)}, bf16[4,512,512]{2,1,0:T(8,128)(2,1)}, u32[]{:S(2)}) copy-start(bf16[4,512,512]{2,1,0:T(8,128)(2,1)} %param.17) | copy-start | bytes 6291460
  6.5 0.8 copy-start.6
  6.5 1.5 copy-start.7
  6.5 2.2 copy-start.5
  6.5 5.4 %copy-start.8 = (s32[8]{0:T(128)S(1)}, s32[8]{0:T(128)}, u32[]{:S(2)}) copy-start(s32[8]{0:T(128)} %param.16) | copy-start | bytes 100
  6.5 204.8 %all-gather.2.cloned.1.call-start = ((), (), s32[]{:S(2)}) async-start(), calls=%async_computation | async-start | bytes 35651584 | tf_op jit(solution)/shard_map/all_gather | solution.py:236
  19.0 1.3 copy-start.3
  20.4 37.0 %copy-start.9 = (s32[8]{0:T(128)S(1)}, s32[8]{0:T(128)}, u32[]{:S(2)}) copy-start(s32[8]{0:T(128)} %param.13) | copy-start | bytes 100
  224.4 3.1 copy-start.2
  388.3 2.5 copy-start.4
  390.8 2.1 copy-start.1
Sparse Core Ops, SparseCore 0:
  9.5 201.8 all-gather.1

commit v17 on v16

--- a/solution.py
+++ b/solution.py
@@ -26,7 +26,7 @@
 
 
 def step_kernel(slots, ids_ref, cnt_ref, kind_ref,
-                group_hbm, own_ref, ons_ref, cpl_hbm, out_ref, buf, sems, acc, cpl_ref, cpl_sem):
+                group_hbm, own_ref, ons_ref, cpl_hbm, bth_ref, out_ref, buf, sems, acc, cpl_ref, cpl_sem):
     b = pl.program_id(0)
     last = pl.num_programs(0) - 1
     rank_cols = own_ref.shape[2]
@@ -67,10 +67,11 @@
     own = own_ref[0]
     wide = own.astype(jnp.float32)
     moved = wide - time_step * (ons_ref[0] * wide + coupled)
-    out_ref[0] = moved.astype(out_ref.dtype)
-
-
-def moved_blocks(group_rows, own_rows, energy, ids, counts, kinds, coupling_blocks):
+    out_ref[0, :, :rank_cols] = moved.astype(out_ref.dtype)
+    out_ref[0, :, rank_cols:] = bth_ref[0]
+
+
+def moved_blocks(group_rows, own_rows, energy, ids, counts, kinds, coupling_blocks, bathed):
     blocks, block_rows, rank_cols = own_rows.shape
     slots = ids.shape[0] // blocks
     kinds_n = coupling_blocks.shape[0]
@@ -82,8 +83,9 @@
             pl.BlockSpec((1, block_rows, rank_cols), lambda b, *_: (b, 0, 0)),
             pl.BlockSpec((1, block_rows, 1), lambda b, *_: (b, 0, 0)),
             pl.BlockSpec(memory_space=pl.ANY),
+            pl.BlockSpec((1, block_rows, rank_cols), lambda b, *_: (b, 0, 0)),
         ],
-        out_specs=pl.BlockSpec((1, block_rows, rank_cols), lambda b, *_: (b, 0, 0)),
+        out_specs=pl.BlockSpec((1, block_rows, 2 * rank_cols), lambda b, *_: (b, 0, 0)),
         scratch_shapes=[
             pltpu.VMEM((2, slots, block_rows, rank_cols), group_rows.dtype),
             pltpu.SemaphoreType.DMA((2, slots)),
@@ -95,9 +97,9 @@
     return pl.pallas_call(
         functools.partial(step_kernel, slots),
         grid_spec=grid_spec,
-        out_shape=jax.ShapeDtypeStruct((blocks, block_rows, rank_cols), jnp.bfloat16),
+        out_shape=jax.ShapeDtypeStruct((blocks, block_rows, 2 * rank_cols), jnp.bfloat16),
         compiler_params=pltpu.CompilerParams(dimension_semantics=("arbitrary",)),
-    )(ids, counts, kinds, group_rows, own_rows, energy, coupling_blocks)
+    )(ids, counts, kinds, group_rows, own_rows, energy, coupling_blocks, bathed)
 
 
 def allreduce_kernel(fields, cols, x_ref, o_ref, *scratch):
@@ -236,13 +238,13 @@
     gathered = lax.all_gather(density_factor, "col", axis=0, tiled=True)
     group_rows = gathered.reshape(group_blocks, block_rows, rank_cols)
     energy = onsite.reshape(blocks, block_rows, 1)
-    moved = moved_blocks(
+    stacked = moved_blocks(
         group_rows, own_rows, energy, in_group.reshape(-1), counts, kinds.reshape(-1), coupling_blocks,
-    ).reshape(blocks * block_rows, rank_cols)
-    moved_gram = lax.dot_general(moved, moved, contract_rows, preferred_element_type=jnp.float32)
-    cross_gram = lax.dot_general(moved, bathed, contract_rows, preferred_element_type=jnp.float32)
-    upper = kernel_sum(jnp.concatenate([moved_gram, cross_gram], axis=0), fields, col_count, 0)
-    moved_sum, cross_sum = upper[:rank_cols], upper[rank_cols:]
+        bathed.reshape(blocks, block_rows, rank_cols),
+    ).reshape(blocks * block_rows, 2 * rank_cols)
+    top = lax.dot_general(stacked[:, :rank_cols], stacked, contract_rows, preferred_element_type=jnp.float32)
+    upper = kernel_sum(top, fields, col_count, 0)
+    moved_sum, cross_sum = upper[:, :rank_cols], upper[:, rank_cols:]
     gram_sum = jnp.concatenate(
         [
             jnp.concatenate([moved_sum, cross_sum], axis=1),
@@ -251,9 +253,7 @@
         axis=0,
     )
     rotation = orthonormal_steps(gram_sum, rank_cols).astype(jnp.bfloat16)
-    product = jnp.dot(moved, rotation[:rank_cols], preferred_element_type=jnp.float32)
-    product += jnp.dot(bathed, rotation[rank_cols:], preferred_element_type=jnp.float32)
-    return product.astype(jnp.bfloat16)
+    return jnp.dot(stacked, rotation, preferred_element_type=jnp.float32).astype(jnp.bfloat16)
 
 
 def solution(mesh):

time: 400 us -> 406 us (1.015)
    dot_general x4 -> x2, matrix products: 8.4 us -> 8.88 us  [the longest x1 4.79 us: shards(): jnp.dot(stacked, rotation, preferred_element_type=jnp.float32)]
where the time goes in v17:
time: 406 us; the launch traced here: 405 us
  waiting for transfers between devices  153 us (38%)
  other arithmetic  110 us (27%)
  Pallas kernels  79 us (19%)
  matrix products  24 us (6%)
  local copies, waits for them, and re-layouts  22.9 us (6%)
  between operations  13.5 us (3%)
    all_gather x1, waiting for transfers between devices, shards(): gathered = lax.all_gather(density_factor, 'col', axis=0, tiled=True)  152 us
    another operation x12, other arithmetic, sweep(): factor = jnp.linalg.cholesky(inner)  68 us
    pallas_call x2, Pallas kernels, kernel_sum(): pl.pallas_call(functools.partial(allreduce_kernel, tuple(fields), cols),...  64.1 us
    another operation x8, other arithmetic, sweep(): lax.linalg.triangular_solve(factor, image, left_side=False, lower=True, t...  39.5 us
    pallas_call x1, Pallas kernels, moved_blocks(): pl.pallas_call(functools.partial(step_kernel, slots), grid_spec=grid_spec...  14.9 us
    another operation x12, local copies, waits for them, and re-layouts  8.14 us
  transfers between devices with their start and end apart: 1, of which 1 were waited for; matrix products, arithmetic and copies ran while one was open for 4% of the time, Pallas kernels for 9%

profile of v17, /device:TPU:1, one launch (start us, length us, event | category | flops | bytes accessed | tf_op | source)
XLA Modules:
  0.0 405.5 jit_solution(8129082852984953130)
XLA Ops:
  6.6 0.7 all-gather.2.cloned.1.call-update
  7.4 3.3 reshape.87.ons_ref
  10.7 0.6 reshape.48.ids_ref
  11.3 0.7 reshape.49.kind_ref
  12.0 2.9 gather_fusion
  14.9 4.1 %convolution_convert_fusion.1.bth_ref = bf16[8,512,256]{2,1,0:T(8,128)(2,1)S(1)} fusion(bf16[8,512,512]{2,1,0:T(8,128)(2,1)} %gather_fusion, bf16[8,512,256]{2,1,0:T(8,128)(2,1)} %bitcast.74), kind=kOutput, calls=%fused_computation.32 | convolution fusion | flops 1074790400 | bytes 8388608 | tf_op jit(solution)/shard_map/bij,bjr->bir/dot_general | solution.py:222
  19.0 1.3 copy-done.1
  20.3 0.7 convolution_bitcast_fusion
  21.1 0.8 concatenate.12.x_ref
  22.0 35.1 %shard_map.84 = f32[1024,128]{1,0:T(8,128)} custom-call(f32[1024,128]{1,0:T(8,128)} %concatenate.12.x_ref), custom_call_target="tpu_custom_call" | custom-call | tf_op jit(solution)/shard_map/pallas_call | solution.py:190
  57.0 1.0 slice.55
  58.0 0.8 reshape.57
  59.4 152.0 %all-gather.2.cloned.1.call-done = bf16[65536,256]{1,0:T(8,128)(2,1)} async-done(((bf16[4096,256]{1,0:T(8,128)(2,1)}), bf16[65536,256]{1,0:T(8,128)(2,1)}) %all-gather.2.cloned.1.call-update) | async-done | bytes 33554448 | tf_op jit(solution)/shard_map/all_gather | solution.py:238
  211.4 14.9 %shard_map.82 = bf16[8,512,512]{2,1,0:T(8,128)(2,1)} custom-call(s32[64]{0:T(128)} %reshape.48.ids_ref, s32[8]{0:T(128)} %broadcast_clamp_fusion.1.cnt_ref, s32[64]{0:T(128)} %reshape.49.kind_ref, bf16[128,512,256]{2,1,0:T(8,128)(2,1)} %bitcast.71, bf16[8,512,256]{2,1,0:T(8,128)(2,1)} %bitcast.75, f32[8,512,1]{2,1,0:T(8,128)} %reshape.87.ons_ref, ...), custom_call_target="tpu_custom_call" | custom-call | tf_op jit(solution)/shard_map/pallas_call | solution.py:97
  226.3 4.1 %fusion.8 = f32[256,512]{1,0:T(8,128)S(1)} fusion(bf16[4096,512]{1,0:T(8,128)(2,1)} %bitcast.72), kind=kOutput, calls=%fused_computation.30 | convolution fusion | flops 1073741824 | bytes 6815744 | tf_op jit(solution)/shard_map/dot_general | solution.py:245
  230.4 0.8 reshape.54.x_ref
  231.2 29.0 %shard_map.83 = f32[1024,128]{1,0:T(8,128)} custom-call(f32[1024,128]{1,0:T(8,128)} %reshape.54.x_ref), custom_call_target="tpu_custom_call" | custom-call | tf_op jit(solution)/shard_map/pallas_call | solution.py:190
  260.3 1.1 reshape.55
  261.5 0.8 copy.17
  262.3 2.1 maximum_maximum_fusion
  264.4 129.5 %while.13 = (s32[]{:T(128)}, f32[512,256]{0,1:T(8,128)S(1)}, f32[512,512]{1,0:T(8,128)}, s32[]{:T(128)}, s32[]{:T(128)}, /*index=5*/f32[]{:T(128)}, s32[]{:T(128)}) while((s32[]{:T(128)}, f32[512,256]{0,1:T(8,128)S(1)}, f32[512,512]{1,0:T(8,128)}, s32[]{:T(128)}, s32[]{:T(128)}, /*index=5*/f32[]{:T(128)}, s32[]{:T(128)}) %tuple.51), condition=%wide.region_5.6_spmd, body=%wide.region_0.5_spmd.sunk | while | flops 1561018624 | bytes 9177364 | solution.py:25
  264.4 2.2 fusion.55
  266.6 1.0 fusion.56
  267.9 11.7 %cholesky.185 = f32[128,128]{1,0:T(8,128)S(1)} custom-call(f32[128,128]{1,0:T(8,128)S(1)} %cholesky.184), custom_call_target="Cholesky" | custom-call | tf_op jit(solution)/shard_map/while/body/eval_jaxpr/jit(cholesky)/cholesky | solution.py:20
  279.6 9.8 %custom-call.20 = f32[1,128,128]{1,2,0:T(8,128)S(1)} custom-call(f32[1,128,128]{2,1,0:T(8,128)S(1)} %get-tuple-element.114), custom_call_target="InvertDiagBlocksLowerTriangular" | custom-call | tf_op jit(solution)/shard_map/while/body/eval_jaxpr/jit(cholesky)/cholesky | solution.py:20
  289.9 11.7 %cholesky.187 = f32[128,128]{1,0:T(8,128)S(1)} custom-call(f32[128,128]{1,0:T(8,128)S(1)} %convolution_subtract_fusion.4), custom_call_target="Cholesky" | custom-call | tf_op jit(solution)/shard_map/while/body/eval_jaxpr/jit(cholesky)/cholesky | solution.py:20
  301.7 0.7 compare_reduce_fusion.3
  303.8 4.1 %while.14 = (s32[]{:T(128)}, f32[256,256]{1,0:T(8,128)S(1)}, s32[2,2]{1,0:T(2,128)S(1)}, f32[2,128,128]{2,1,0:T(8,128)S(1)}, s32[]{:T(128)}) while((s32[]{:T(128)}, f32[256,256]{1,0:T(8,128)S(1)}, s32[2,2]{1,0:T(2,128)S(1)}, f32[2,128,128]{2,1,0:T(8,128)S(1)}, s32[]{:T(128)}) %tuple.48), condition=%wide.while_cond, body=%wide.while_body.sunk | while | flops 2 | bytes 131181 | solution.py:21
  303.8 0.6 fusion.60
  304.5 1.4 bitcast_dynamic-update-slice_fusion.2
  305.9 0.6 fusion.60
  306.5 1.4 bitcast_dynamic-update-slice_fusion.2
  307.9 19.7 %custom-call.22 = f32[2,128,128]{1,2,0:T(8,128)S(1)} custom-call(f32[2,128,128]{2,1,0:T(8,128)S(1)} %get-tuple-element.122), custom_call_target="InvertDiagBlocksLowerTriangular" | custom-call | tf_op jit(solution)/shard_map/while/body/eval_jaxpr/triangular_solve | solution.py:21
  328.0 0.6 convolution_subtract_fusion.5
  329.1 2.2 fusion.55
  331.4 1.0 fusion.56
  332.6 11.7 %cholesky.185 = f32[128,128]{1,0:T(8,128)S(1)} custom-call(f32[128,128]{1,0:T(8,128)S(1)} %cholesky.184), custom_call_target="Cholesky" | custom-call | tf_op jit(solution)/shard_map/while/body/eval_jaxpr/jit(cholesky)/cholesky | solution.py:20
  344.3 9.8 %custom-call.20 = f32[1,128,128]{1,2,0:T(8,128)S(1)} custom-call(f32[1,128,128]{2,1,0:T(8,128)S(1)} %get-tuple-element.114), custom_call_target="InvertDiagBlocksLowerTriangular" | custom-call | tf_op jit(solution)/shard_map/while/body/eval_jaxpr/jit(cholesky)/cholesky | solution.py:20
  354.7 11.7 %cholesky.187 = f32[128,128]{1,0:T(8,128)S(1)} custom-call(f32[128,128]{1,0:T(8,128)S(1)} %convolution_subtract_fusion.4), custom_call_target="Cholesky" | custom-call | tf_op jit(solution)/shard_map/while/body/eval_jaxpr/jit(cholesky)/cholesky | solution.py:20
  366.4 0.7 compare_reduce_fusion.3
  368.6 4.1 %while.14 = (s32[]{:T(128)}, f32[256,256]{1,0:T(8,128)S(1)}, s32[2,2]{1,0:T(2,128)S(1)}, f32[2,128,128]{2,1,0:T(8,128)S(1)}, s32[]{:T(128)}) while((s32[]{:T(128)}, f32[256,256]{1,0:T(8,128)S(1)}, s32[2,2]{1,0:T(2,128)S(1)}, f32[2,128,128]{2,1,0:T(8,128)S(1)}, s32[]{:T(128)}) %tuple.48), condition=%wide.while_cond, body=%wide.while_body.sunk | while | flops 2 | bytes 131181 | solution.py:21
  368.6 0.6 fusion.60
  369.2 1.4 bitcast_dynamic-update-slice_fusion.2
  370.6 0.6 fusion.60
  371.3 1.4 bitcast_dynamic-update-slice_fusion.2
  372.7 19.7 %custom-call.22 = f32[2,128,128]{1,2,0:T(8,128)S(1)} custom-call(f32[2,128,128]{2,1,0:T(8,128)S(1)} %get-tuple-element.122), custom_call_target="InvertDiagBlocksLowerTriangular" | custom-call | tf_op jit(solution)/shard_map/while/body/eval_jaxpr/triangular_solve | solution.py:21
  392.8 0.6 convolution_subtract_fusion.5
  393.8 4.8 %convolution_convert_fusion = bf16[4096,256]{1,0:T(8,128)(2,1)} fusion(bf16[4096,512]{1,0:T(8,128)(2,1)} %bitcast.73, f32[512,256]{0,1:T(8,128)S(1)} %get-tuple-element.22), kind=kOutput, calls=%fused_computation.29 | convolution fusion | flops 1074921472 | bytes 6815744 | tf_op jit(solution)/shard_map/dot_general | solution.py:256
  (56 shorter events, 4.3 us)
Async XLA Ops:
  6.5 5.5 %copy-start = (bf16[4,512,512]{2,1,0:T(8,128)(2,1)S(1)}, bf16[4,512,512]{2,1,0:T(8,128)(2,1)}, u32[]{:S(2)}) copy-start(bf16[4,512,512]{2,1,0:T(8,128)(2,1)} %param.17) | copy-start | bytes 6291460
  6.5 0.9 copy-start.2
  6.5 4.1 %copy-start.3 = (s32[8,8]{1,0:T(8,128)S(1)}, s32[8,8]{1,0:T(8,128)}, u32[]{:S(2)}) copy-start(s32[8,8]{1,0:T(8,128)} %param.12) | copy-start | bytes 772
  6.5 4.8 %copy-start.4 = (s32[8,8]{1,0:T(8,128)S(1)}, s32[8,8]{1,0:T(8,128)}, u32[]{:S(2)}) copy-start(s32[8,8]{1,0:T(8,128)} %param.14) | copy-start | bytes 772
  6.5 5.5 %copy-start.5 = (s32[8]{0:T(128)S(1)}, s32[8]{0:T(128)}, u32[]{:S(2)}) copy-start(s32[8]{0:T(128)} %param.16) | copy-start | bytes 100
  6.5 204.8 %all-gather.2.cloned.1.call-start = ((), (), s32[]{:S(2)}) async-start(), calls=%async_computation | async-start | bytes 35651584 | tf_op jit(solution)/shard_map/all_gather | solution.py:238
  19.0 1.3 copy-start.1
  21.1 37.8 %copy-start.6 = (s32[8]{0:T(128)S(1)}, s32[8]{0:T(128)}, u32[]{:S(2)}) copy-start(s32[8]{0:T(128)} %param.13) | copy-start | bytes 100
Sparse Core Ops, SparseCore 0:
  9.5 201.8 all-gather.1
